TPU v7x, 32 devices: a whole 2x2x4 slice. The times are simulated.
32 devices in a mesh: groups: 2 (over y), space: 4 (over z), tm: 2 (over x), rep: 2 (over core).
Axes of the slice: x: 2, y: 2, z: 4, core: 2. Of those that a mesh axis runs over, the one named last changes fastest.
Arguments:
- features: bfloat16 [1024, 16384], P(None, ('groups', 'space', 'tm', 'rep')), parts along dimension 1, may hold values from -6 to 6
- grad_out: bfloat16 [1024, 16384], P(None, ('groups', 'space', 'tm', 'rep')), parts along dimension 1, may hold values from -6 to 6
- query_weight: bfloat16 [1024, 1024], P('space'), may hold values from -0.1875 to 0.1875
- key_weight: bfloat16 [1024, 1024], P('space'), may hold values from -0.1875 to 0.1875
- value_weight: bfloat16 [1024, 1024], P('space'), may hold values from -0.1875 to 0.1875
- out_weight: bfloat16 [1024, 1024], P('space'), may hold values from -0.1875 to 0.1875
- query_scale: float32 [1024], replicated, may hold values from 0.1 to 1.9
- key_scale: float32 [1024], replicated, may hold values from 0.1 to 1.9
- value_scale: float32 [1024], replicated, may hold values from 0.1 to 1.9
- out_scale: float32 [1024], replicated, may hold values from 0.1 to 1.9
- active_blocks: int32 [32, 6], P(('groups', 'space', 'tm', 'rep')), parts along dimension 0, may hold values from 0 to 7, as said below
- active_count: int32 [32], P(('groups', 'space', 'tm', 'rep')), parts along dimension 0, may hold values from 1 to 6, as said below
Outputs:
- attention_out: bfloat16 [1024, 16384], P(None, ('groups', 'space', 'tm', 'rep')), parts along dimension 1
- input_grad: bfloat16 [1024, 16384], P(None, ('groups', 'space', 'tm', 'rep')), parts along dimension 1
There are 2 independent parts, one for each index of `groups`. A program takes and returns all parts, laid end to end along the dimension named above; an argument that names none is the same for every part. Nothing has to cross between parts.
Inputs may be any that keep to these rules, and one draw needn't show every extreme that they name: `active_blocks`: each device's row holds 6 different block numbers of its 8 blocks. `active_count`: some device has all 6 listed blocks active in every draw.
All inputs are finite; a program needn't handle non-finite values.
Results may differ from a plain program's by a relative error of at most 0.0069.
Values may be sent and summed in bfloat16 or wider, within the bound.
No kernel may reach another device: no remote copies, remote signals or barrier semaphores. Data moves between devices by JAX's collectives and lax.ppermute only.
A program may use at most 64 MiB of HBM per device.

v0:
```python
import math

import jax
import jax.numpy as jnp
from jax import lax
from jax.sharding import PartitionSpec as P

HEADS = 16
HEAD_DIM = 64
BLOCK = 64


highest = lax.Precision.HIGHEST
contract_first = (((0,), (0,)), ((), ()))


def compact_local(values, blocks, live_count):
    feature_rows = values.shape[0]
    block_grid = values.reshape(feature_rows, -1, BLOCK)
    picked = jnp.take(block_grid, blocks, axis=1)
    live_mask = (jnp.arange(blocks.shape[0], dtype=jnp.int32) < live_count).astype(values.dtype)
    return (picked * live_mask[None, :, None]).reshape(feature_rows, blocks.shape[0] * BLOCK)


def expand_local(values, blocks, total_blocks):
    feature_rows = values.shape[0]
    shaped = values.reshape(feature_rows, blocks.shape[0], BLOCK)
    target = jnp.zeros((feature_rows, total_blocks, BLOCK), values.dtype)
    return target.at[:, blocks, :].set(shaped).reshape(feature_rows, total_blocks * BLOCK)


def per_device(
    features,
    grad_out,
    query_weight,
    key_weight,
    value_weight,
    out_weight,
    query_scale,
    key_scale,
    value_scale,
    out_scale,
    active_blocks,
    active_count,
):
    blocks = active_blocks[0]
    live_count = active_count[0]
    total_blocks = features.shape[1] // BLOCK
    slot_rows = blocks.shape[0] * BLOCK
    model_width = features.shape[0]
    attn_scale = 1.0 / math.sqrt(HEAD_DIM * slot_rows * lax.axis_size(("space", "tm", "rep")))
    scaled_grad = (grad_out.astype(jnp.float32) * out_scale[:, None]).astype(jnp.bfloat16)
    x_rows = compact_local(features, blocks, live_count)
    g_rows = compact_local(scaled_grad, blocks, live_count)
    pieces = (
        lax.all_gather(query_weight, "space", axis=0, tiled=True),
        lax.all_gather(key_weight, "space", axis=0, tiled=True),
        lax.all_gather(value_weight, "space", axis=0, tiled=True),
    )
    part_rows = x_rows
    q_raw, k_raw, v_raw = tuple(
        (
            lax.dot_general(piece_w, part_rows, contract_first, preferred_element_type=jnp.float32)
            for piece_w in pieces
        )
    )
    back_raw = jnp.dot(
        lax.all_gather(out_weight, "space", axis=0, tiled=True),
        g_rows,
        preferred_element_type=jnp.float32,
    )
    query = (q_raw * query_scale[:, None]).astype(jnp.bfloat16)
    key = (k_raw * key_scale[:, None]).astype(jnp.bfloat16)
    value = (v_raw * value_scale[:, None]).astype(jnp.bfloat16)
    back = back_raw.astype(jnp.bfloat16)
    q_heads = query.reshape(HEADS, HEAD_DIM, slot_rows)
    k_heads = key.reshape(HEADS, HEAD_DIM, slot_rows)
    v_heads = value.reshape(HEADS, HEAD_DIM, slot_rows)
    b_heads = back.reshape(HEADS, HEAD_DIM, slot_rows)
    state_local = jnp.einsum("hit,hjt->hij", k_heads, v_heads, preferred_element_type=jnp.float32)
    grad_local = attn_scale * jnp.einsum(
        "hit,hjt->hij", q_heads, b_heads, preferred_element_type=jnp.float32
    )
    state, state_grad = lax.psum((state_local, grad_local), ("space", "tm", "rep"))
    attended = attn_scale * jnp.einsum(
        "hij,hit->hjt", state, q_heads.astype(jnp.float32), precision=highest
    )
    attended = attended.astype(jnp.bfloat16).reshape(model_width, slot_rows)
    query_back = attn_scale * jnp.einsum(
        "hij,hjt->hit", state, b_heads.astype(jnp.float32), precision=highest
    )
    query_back = (query_back.reshape(model_width, slot_rows) * query_scale[:, None]).astype(
        jnp.bfloat16
    )
    key_back = jnp.einsum(
        "hij,hjt->hit", state_grad, v_heads.astype(jnp.float32), precision=highest
    )
    key_back = (key_back.reshape(model_width, slot_rows) * key_scale[:, None]).astype(jnp.bfloat16)
    value_back = jnp.einsum(
        "hij,hit->hjt", state_grad, k_heads.astype(jnp.float32), precision=highest
    )
    value_back = (value_back.reshape(model_width, slot_rows) * value_scale[:, None]).astype(
        jnp.bfloat16
    )
    part_rows = attended
    y_raw = lax.dot_general(
        lax.all_gather(out_weight, "space", axis=0, tiled=True),
        part_rows,
        contract_first,
        preferred_element_type=jnp.float32,
    )
    pieces = (
        lax.all_gather(query_weight, "space", axis=0, tiled=True),
        lax.all_gather(key_weight, "space", axis=0, tiled=True),
        lax.all_gather(value_weight, "space", axis=0, tiled=True),
    )
    new_rows = jnp.dot(pieces[0], query_back, preferred_element_type=jnp.float32)
    new_rows = new_rows + jnp.dot(pieces[1], key_back, preferred_element_type=jnp.float32)
    new_rows = new_rows + jnp.dot(pieces[2], value_back, preferred_element_type=jnp.float32)
    out_rows = (y_raw * out_scale[:, None]).astype(jnp.bfloat16)
    in_rows = new_rows.astype(jnp.bfloat16)
    return (
        expand_local(out_rows, blocks, total_blocks),
        expand_local(in_rows, blocks, total_blocks),
    )


def solution(mesh):
    placed = (
        P(None, ("groups", "space", "tm", "rep")),
        P(None, ("groups", "space", "tm", "rep")),
        P("space", None),
        P("space", None),
        P("space", None),
        P("space", None),
        P(),
        P(),
        P(),
        P(),
        P(("groups", "space", "tm", "rep"), None),
        P(("groups", "space", "tm", "rep")),
    )
    return jax.shard_map(
        per_device,
        mesh=mesh,
        in_specs=placed,
        out_specs=(
            P(None, ("groups", "space", "tm", "rep")),
            P(None, ("groups", "space", "tm", "rep")),
        ),
        check_vma=False,
    )
```

profile of v0, /device:TPU:0, one launch (start us, length us, event | category | flops | bytes accessed | tf_op | source)
XLA Modules:
  0.0 321.1 jit_solution(2551632546827474694)
XLA Ops:
  7.2 0.7 all-gather.11.cloned.1.call-update
  7.9 0.0 all-gather.9.cloned.1.call-start
  8.0 0.7 all-gather.9.cloned.1.call-update
  8.7 0.7 all-gather.5.cloned.1.call-update
  9.4 0.5 all-gather.7.cloned.1.call-update
  10.0 0.0 all-reduce.3.cloned.1.call-start
  10.7 0.5 copy.26
  11.2 1.3 copy.31
  12.6 0.6 gather_fusion
  13.2 0.1 copy-done.8
  13.3 1.5 multiply_convert_fusion
  14.7 0.6 gather_fusion.1
  15.4 0.2 bitcast_multiply_fusion.3
  15.6 42.7 %all-gather.11.cloned.1.call-done = bf16[1024,1024]{1,0:T(8,128)(2,1)} async-done(((bf16[256,1024]{1,0:T(8,128)(2,1)}), bf16[1024,1024]{1,0:T(8,128)(2,1)}) %all-gather.11.cloned.1.call-update) | async-done | bytes 2097168 | tf_op jit(solution)/shard_map/all_gather | solution.py:107
  58.2 2.6 fusion.6
  60.9 0.4 copy.32
  61.2 43.3 %all-gather.9.cloned.1.call-done = bf16[1024,1024]{1,0:T(8,128)(2,1)} async-done(((bf16[256,1024]{1,0:T(8,128)(2,1)}), bf16[1024,1024]{1,0:T(8,128)(2,1)}) %all-gather.9.cloned.1.call-update) | async-done | bytes 2097168 | tf_op jit(solution)/shard_map/all_gather | solution.py:56
  104.5 2.6 fusion.5
  107.1 0.4 copy.29
  107.5 43.3 %all-gather.5.cloned.1.call-done = bf16[1024,1024]{1,0:T(8,128)(2,1)} async-done(((bf16[256,1024]{1,0:T(8,128)(2,1)}), bf16[1024,1024]{1,0:T(8,128)(2,1)}) %all-gather.5.cloned.1.call-update) | async-done | bytes 2097168 | tf_op jit(solution)/shard_map/all_gather | solution.py:57
  150.8 2.8 fusion.3
  153.6 0.4 copy.27
  154.0 42.9 %all-gather.7.cloned.1.call-done = bf16[1024,1024]{1,0:T(8,128)(2,1)} async-done(((bf16[256,1024]{1,0:T(8,128)(2,1)}), bf16[1024,1024]{1,0:T(8,128)(2,1)}) %all-gather.7.cloned.1.call-update) | async-done | bytes 2097168 | tf_op jit(solution)/shard_map/all_gather | solution.py:58
  196.9 3.7 %fusion.4 = bf16[1024,384]{0,1:T(8,128)(2,1)} fusion(bf16[1024,384]{0,1:T(8,128)(2,1)} %bitcast.102, bf16[1024,1024]{1,0:T(8,128)(2,1)} %all-gather.7.cloned.1.call-done, f32[1024]{0:T(1024)S(1)} %copy-done.10), kind=kOutput, calls=%fused_computation.20 | convolution fusion | flops 806092800 | bytes 3674112 | tf_op jit(solution)/shard_map/dot_general | solution.py:63
  200.6 1.5 copy.28
  202.1 1.2 convolution_multiply_fusion.1
  203.3 1.2 fusion.8
  204.5 92.1 %all-reduce.3.cloned.1.call-done = (f32[16,64,64]{2,1,0:T(8,128)}, f32[16,64,64]{2,1,0:T(8,128)}) async-done(((f32[16,64,64]{2,1,0:T(8,128)}, f32[16,64,64]{2,1,0:T(8,128)}), (f32[16,64,64]{2,1,0:T(8,128)}, f32[16,64,64]{2,1,0:T(8,128)})) %all-reduce.3.cloned.1.call-update) | async-done | bytes 524304 | tf_op jit(solution)/shard_map/psum | solution.py:84
  296.7 2.0 multiply_convert_fusion.2
  298.7 0.8 convolution_multiply_fusion
  299.5 0.2 copy-done.2
  299.7 0.8 fusion.12
  300.5 0.8 fusion.10
  301.3 0.2 fusion.2
  301.5 0.2 fusion
  301.8 1.1 fusion.1
  302.8 0.8 copy-done
  303.6 1.0 multiply_convert_fusion.1
  304.6 0.1 broadcast.51.clone
  304.7 0.8 scatter_fusion
  305.6 1.3 copy.34
  306.9 2.8 fusion.9
  309.7 1.0 fusion.11
  310.7 0.5 copy-done.1
  311.3 1.1 add_convert_fusion
  312.4 0.1 broadcast.51.clone.1
  312.5 0.8 scatter_fusion.1
  313.3 1.3 copy.35
  (32 shorter events, 0.2 us)
Async XLA Ops:
  7.2 3.5 %copy-start.4 = (bf16[1024,512]{1,0:T(8,128)(2,1)S(1)}, bf16[1024,512]{1,0:T(8,128)(2,1)}, u32[]{:S(2)}) copy-start(bf16[1024,512]{1,0:T(8,128)(2,1)} %param.14) | copy-start | bytes 3145732
  7.2 51.1 %all-gather.11.cloned.1.call-start = ((), (), s32[]{:S(2)}) async-start(), calls=%async_computation.3 | async-start | bytes 2621440 | tf_op jit(solution)/shard_map/all_gather | solution.py:107
  7.9 96.6 %all-gather.9.cloned.1.call-start = ((), (), s32[]{:S(2)}) async-start(), calls=%async_computation.2 | async-start | bytes 2621440 | tf_op jit(solution)/shard_map/all_gather | solution.py:56
  8.7 2.6 copy-start.5
  8.7 142.1 %all-gather.5.cloned.1.call-start = ((), (), s32[]{:S(2)}) async-start(), calls=%async_computation | async-start | bytes 2621440 | tf_op jit(solution)/shard_map/all_gather | solution.py:57
  9.4 187.5 %all-gather.7.cloned.1.call-start = ((), (), s32[]{:S(2)}) async-start(), calls=%async_computation.1 | async-start | bytes 2621440 | tf_op jit(solution)/shard_map/all_gather | solution.py:58
  10.0 286.7 %all-reduce.3.cloned.1.call-start = ((), (), s32[]{:S(2)}) async-start(), calls=%async_computation.4 | async-start | bytes 2097152 | tf_op jit(solution)/shard_map/psum | solution.py:84
  10.7 1.9 copy-start.12
  12.6 0.7 copy-start.8
  15.6 88.9 %copy-start.6 = (bf16[1024,6,64]{0,2,1:T(8,128)(2,1)}, bf16[1024,6,64]{0,2,1:T(8,128)(2,1)S(1)}, u32[]{:S(2)}) copy-start(bf16[1024,6,64]{0,2,1:T(8,128)(2,1)S(1)} %get-tuple-element.10) | copy-start | bytes 2359300
  60.9 43.7 %copy-start.9 = (f32[1024]{0:T(1024)S(1)}, f32[1024]{0:T(1024)}, u32[]{:S(2)}) copy-start(f32[1024]{0:T(1024)} %param.20) | copy-start | bytes 12292
  107.1 43.7 %copy-start.11 = (f32[1024]{0:T(1024)S(1)}, f32[1024]{0:T(1024)}, u32[]{:S(2)}) copy-start(f32[1024]{0:T(1024)} %param.21) | copy-start | bytes 12292
  153.6 43.3 %copy-start.10 = (f32[1024]{0:T(1024)S(1)}, f32[1024]{0:T(1024)}, u32[]{:S(2)}) copy-start(f32[1024]{0:T(1024)} %param.22) | copy-start | bytes 12292
  296.7 2.0 copy-start.3
  298.7 1.0 copy-start.2
  301.7 1.9 copy-start
  306.9 2.8 copy-start.7
  306.9 2.8 copy-start.13
  309.7 1.6 copy-start.1
Sparse Core Ops, SparseCore 0:
  9.6 48.6 all-gather.10
  59.8 44.6 all-gather.8
  106.1 44.6 all-gather.4
  152.2 44.6 all-gather.6
  204.6 91.9 all-reduce.2
where the time goes:
time: 322 us; the launch traced here: 321 us
  waiting for transfers between devices  267 us (83%)
  matrix products  24.3 us (8%)
  between operations  14.8 us (5%)
  local copies, waits for them, and re-layouts  11.8 us (4%)
    psum x1, waiting for transfers between devices, per_device(): lax.psum((state_local, grad_local), ('space', 'tm', 'rep'))  92.1 us
    all_gather x1, waiting for transfers between devices, per_device(): lax.all_gather(key_weight, 'space', axis=0, tiled=True)  43.3 us
    all_gather x1, waiting for transfers between devices, per_device(): lax.all_gather(query_weight, 'space', axis=0, tiled=True)  43.3 us
    all_gather x1, waiting for transfers between devices, per_device(): lax.all_gather(value_weight, 'space', axis=0, tiled=True)  42.9 us
    all_gather x1, waiting for transfers between devices, per_device(): lax.all_gather(out_weight, 'space', axis=0, tiled=True)  42.7 us
    dot_general x3, matrix products, per_device(): lax.dot_general(piece_w, part_rows, contract_first, preferred_element_typ...  9.1 us
  transfers between devices with their start and end apart: 5, of which 5 were waited for; matrix products, arithmetic and copies ran while one was open for 4% of the time, Pallas kernels for 0%

commit v1 on v0

--- a/solution.py
+++ b/solution.py
@@ -1,13 +1,305 @@
+import functools
 import math
 
 import jax
 import jax.numpy as jnp
 from jax import lax
+from jax.experimental import pallas as pl
+from jax.experimental.pallas import tpu as pltpu
 from jax.sharding import PartitionSpec as P
 
 HEADS = 16
 HEAD_DIM = 64
 BLOCK = 64
+BF16 = jnp.bfloat16
+F32 = jnp.float32
+REDUCE_AXES = ("space", "tm", "rep")
+DEVICE_AXES = ("groups", "space", "tm", "rep")
+
+VMEM = pl.BlockSpec(memory_space=pltpu.VMEM)
+ANY = pl.BlockSpec(memory_space=pl.ANY)
+SMEM = pl.BlockSpec(memory_space=pltpu.SMEM)
+
+
+def dot(a, b, ca, cb):
+    return lax.dot_general(a, b, (((ca,), (cb,)), ((), ())), preferred_element_type=F32)
+
+
+def call(body, outs, in_specs, args, scratch=(), flops=0, limit=None):
+    size = sum(math.prod(o.shape) * o.dtype.itemsize for o in outs)
+    size += sum(math.prod(a.shape) * a.dtype.itemsize for a in args)
+    return pl.pallas_call(
+        body,
+        out_shape=tuple(outs),
+        in_specs=in_specs,
+        out_specs=(VMEM,) * len(outs),
+        scratch_shapes=scratch,
+        compiler_params=pltpu.CompilerParams(vmem_limit_bytes=limit),
+        cost_estimate=pl.CostEstimate(flops=flops, bytes_accessed=size, transcendentals=0),
+    )(*args)
+
+
+def shape(dims, dtype=BF16):
+    return jax.ShapeDtypeStruct(dims, dtype)
+
+
+def swap_x(a):
+    return lax.ppermute(a, "tm", [(0, 1), (1, 0)])
+
+
+def swap_y(a):
+    return lax.ppermute(a, "groups", [(0, 1), (1, 0)])
+
+
+def swap_core(a):
+    return lax.ppermute(a, "rep", [(0, 1), (1, 0)])
+
+
+def turn_z(a, step):
+    return lax.ppermute(a, "space", [(i, (i + step) % 4) for i in range(4)])
+
+
+def swap_z(a, bit):
+    return lax.ppermute(a, "space", [(i, i ^ bit) for i in range(4)])
+
+
+def cat(*parts):
+    return jnp.concatenate(parts, 0)
+
+
+def around(piece):
+    return cat(turn_z(piece, 1), turn_z(piece, 3), turn_z(piece, 2))
+
+
+def spread(mine, first, second):
+    pair = cat(mine, first(mine))
+    return pair, second(pair)
+
+
+def sum_over_chips(part):
+    for swap in (swap_x, lambda a: swap_z(a, 1), lambda a: swap_z(a, 2)):
+        part = part + swap(part.astype(BF16)).astype(F32)
+    return part
+
+
+def place(pos_ref, own_ref, pair_ref, far_ref, full_ref, sems, flips, base):
+    z, q = pos_ref[0], pos_ref[1]
+    rows = pair_ref.shape[0] // 6
+    whole = own_ref.shape[0]
+    copies = [
+        pltpu.make_async_copy(
+            own_ref, full_ref.at[pl.ds(pl.multiple_of(z * whole, whole), whole)], sems.at[base]
+        )
+    ]
+    order = ((pair_ref, 0), (pair_ref, flips[0]), (far_ref, flips[1]), (far_ref, 3))
+    for n, (ref, flip) in enumerate(order):
+        for k, step in enumerate((3, 1, 2)):
+            at = lax.rem(z + step, 4) * 4 + lax.bitwise_xor(q, flip)
+            copies.append(
+                pltpu.make_async_copy(
+                    ref.at[pl.ds((3 * (n % 2) + k) * rows, rows)],
+                    full_ref.at[pl.ds(pl.multiple_of(at * rows, rows), rows)],
+                    sems.at[base + 1 + 3 * n + k],
+                )
+            )
+    return copies
+
+
+def pack(block):
+    left = lax.broadcasted_iota(jnp.int32, (HEAD_DIM, 128), 1) < HEAD_DIM
+    return (
+        jnp.where(left, block[0:64, 0:128], block[64:128, 0:128]),
+        jnp.where(left, block[128:192, 128:256], block[192:256, 128:256]),
+    )
+
+
+def unpack(packed, full_ref):
+    left = lax.broadcasted_iota(jnp.int32, (HEAD_DIM, 128), 1) < HEAD_DIM
+    full_ref[...] = jnp.zeros_like(full_ref)
+    for n in range(2):
+        two = packed[64 * n : 64 * n + 64]
+        full_ref[128 * n : 128 * n + 64, 128 * n : 128 * n + 128] = jnp.where(
+            left, two, 0.0
+        ).astype(full_ref.dtype)
+        full_ref[128 * n + 64 : 128 * n + 128, 128 * n : 128 * n + 128] = jnp.where(
+            left, 0.0, two
+        ).astype(full_ref.dtype)
+
+
+def key_value_body(
+    pos, x_own, x_other, ko, kp, kf, vo, vp, vf, ks, vs, key, value, state, wk, wv, sems
+):
+    copies = place(pos, ko, kp, kf, wk, sems, (1, 2), 0)
+    copies += place(pos, vo, vp, vf, wv, sems, (2, 1), 13)
+    for one in copies:
+        one.start()
+    for one in copies:
+        one.wait()
+    half = x_own.shape[0]
+    for n, rows in enumerate((x_own, x_other)):
+        for t in range(0, half, 256):
+            tile = rows[t : t + 256, :]
+            at = slice(n * half + t, n * half + t + 256)
+            key[at, :] = (dot(tile, wk[...], 1, 0) * ks[...]).astype(BF16)
+            value[at, :] = (dot(tile, wv[...], 1, 0) * vs[...]).astype(BF16)
+    for g in range(2):
+        cols = slice(256 * g, 256 * g + 256)
+        a, b = pack(dot(key[:, cols], value[:, cols], 0, 0))
+        state[128 * g : 128 * g + 64, :] = a
+        state[128 * g + 64 : 128 * g + 128, :] = b
+
+
+def query_back_body(
+    scale, pos, x_own, x_other, g_own, g_other, qo, qp, qf, oo, op, of, qs,
+    query, back, term, wq, wo, sems,
+):
+    copies = place(pos, qo, qp, qf, wq, sems, (1, 2), 0)
+    copies += place(pos, oo, op, of, wo, sems, (2, 1), 13)
+    for one in copies:
+        one.start()
+    for one in copies:
+        one.wait()
+    half = x_own.shape[0]
+    for n, rows in enumerate((x_own, x_other)):
+        for t in range(0, half, 256):
+            at = slice(n * half + t, n * half + t + 256)
+            query[at, :] = (dot(rows[t : t + 256, :], wq[...], 1, 0) * qs[...]).astype(BF16)
+    for n, cols in enumerate((g_own, g_other)):
+        for t in range(0, half, 256):
+            at = slice(n * half + t, n * half + t + 256)
+            back[:, at] = dot(wo[...], cols[:, t : t + 256], 1, 0).astype(BF16)
+    for g in range(2):
+        part = slice(256 * g, 256 * g + 256)
+        a, b = pack(scale * dot(back[part, :], query[:, part], 1, 0))
+        term[128 * g : 128 * g + 64, :] = a
+        term[128 * g + 64 : 128 * g + 128, :] = b
+
+
+def middle_body(
+    scale, query, back, state, wq, wo, qs, out_own, out_other, in_own, in_other, diag, att, qb
+):
+    half = out_own.shape[0]
+    for g in range(2):
+        part = slice(256 * g, 256 * g + 256)
+        unpack(scale * state[128 * g : 128 * g + 128, :], diag)
+        att[:, part] = dot(query[:, part], diag[...], 1, 0).astype(BF16)
+        qb[part, :] = (dot(diag[...], back[part, :], 1, 0) * qs[part, :]).astype(BF16)
+    for n, (out, inp) in enumerate(((out_own, in_own), (out_other, in_other))):
+        for t in range(0, half, 256):
+            at = slice(n * half + t, n * half + t + 256)
+            out[t : t + 256, :] = dot(att[at, :], wo[...], 1, 0).astype(out.dtype)
+            inp[:, t : t + 256] = dot(wq[...], qb[:, at], 1, 0)
+
+
+def tail_body(key, value, term, wk, wv, ks, vs, in_own, in_other, res_own, res_other, diag, kb, vb):
+    half = in_own.shape[1]
+    for g in range(2):
+        part = slice(256 * g, 256 * g + 256)
+        unpack(term[128 * g : 128 * g + 128, :], diag)
+        kb[:, part] = (dot(value[:, part], diag[...], 1, 0) * ks[:, part]).astype(BF16)
+        vb[:, part] = (dot(key[:, part], diag[...], 1, 1) * vs[:, part]).astype(BF16)
+    for n, (inp, res) in enumerate(((in_own, res_own), (in_other, res_other))):
+        for t in range(0, half, 256):
+            at = slice(n * half + t, n * half + t + 256)
+            total = inp[:, t : t + 256] + dot(wk[...], kb[at, :], 1, 1)
+            total = total + dot(wv[...], vb[at, :], 1, 1)
+            res[:, t : t + 256] = total.astype(res.dtype)
+
+
+def per_device_split(
+    features,
+    grad_out,
+    query_weight,
+    key_weight,
+    value_weight,
+    out_weight,
+    query_scale,
+    key_scale,
+    value_scale,
+    out_scale,
+    active_blocks,
+    active_count,
+):
+    x, y, z, c = (lax.axis_index(a) for a in ("tm", "groups", "space", "rep"))
+    width, tokens = features.shape
+    mine = width // 2
+    both = 2 * tokens
+    quarter = 2 * y + x
+    slots = active_blocks.shape[1] * BLOCK
+    scale = 1.0 / math.sqrt(HEAD_DIM * slots * lax.axis_size(REDUCE_AXES))
+    pos = jnp.stack([z, quarter]).astype(jnp.int32)
+
+    def columns(shard):
+        split = shard.reshape(shard.shape[0], 4, 2, 128)
+        return lax.dynamic_index_in_dim(split, c, 2, keepdims=False).reshape(-1, mine)
+
+    def own_piece(own):
+        rows = own.shape[0] // 4
+        return lax.dynamic_slice_in_dim(own, quarter * rows, rows, 0)
+
+    def own_scale(v):
+        return lax.dynamic_index_in_dim(v.reshape(4, 2, 128), c, 1, keepdims=False).reshape(mine)
+
+    k_own, v_own, q_own = columns(key_weight), columns(value_weight), columns(query_weight)
+    o_own = lax.dynamic_slice_in_dim(out_weight, c * 128, 128, 0)
+    k_pair, k_far = spread(around(own_piece(k_own)), swap_x, swap_y)
+    v_pair, v_far = spread(around(own_piece(v_own)), swap_y, swap_x)
+    q_pair, q_far = spread(around(own_piece(q_own)), swap_x, swap_y)
+    o_pair, o_far = spread(around(own_piece(o_own)), swap_y, swap_x)
+
+    live = jnp.arange(active_blocks.shape[1], dtype=jnp.int32) < active_count[0]
+    named = jnp.where(live, active_blocks[0], -1)
+    block_of = jnp.arange(tokens, dtype=jnp.int32) // BLOCK
+    mask = jnp.any(named[:, None] == block_of[None, :], axis=0)
+    zero = jnp.zeros((), BF16)
+    x_own = jnp.where(mask[:, None], features.T, zero)
+    g_own = (grad_out.astype(F32) * out_scale[:, None]).astype(BF16)
+    g_own = jnp.where(mask[None, :], g_own, zero)
+    x_other, g_other = swap_core(x_own), swap_core(g_own)
+
+    ks, vs, qs = own_scale(key_scale), own_scale(value_scale), own_scale(query_scale)
+    sems = (pltpu.SemaphoreType.DMA((26,)),)
+    ff = 2 * both * width * mine
+    key, value, state, wk, wv = call(
+        key_value_body,
+        [shape((both, mine)), shape((both, mine)), shape((256, 128), F32),
+         shape((width, mine)), shape((width, mine))],
+        [SMEM, VMEM, VMEM] + [ANY] * 6 + [VMEM] * 2,
+        (pos, x_own, x_other, k_own, k_pair, k_far, v_own, v_pair, v_far, ks[None], vs[None]),
+        sems, 2 * ff, 24 << 20,
+    )
+    state = sum_over_chips(state)
+    query, back, term, wq, wo = call(
+        functools.partial(query_back_body, scale),
+        [shape((both, mine)), shape((mine, both)), shape((256, 128), F32),
+         shape((width, mine)), shape((mine, width))],
+        [SMEM] + [VMEM] * 4 + [ANY] * 6 + [VMEM],
+        (pos, x_own, x_other, g_own, g_other, q_own, q_pair, q_far, o_own, o_pair, o_far, qs[None]),
+        sems, 2 * ff, 24 << 20,
+    )
+    term = sum_over_chips(term)
+    diag = pltpu.VMEM((256, 256), BF16)
+    out_own, out_other, in_own, in_other = call(
+        functools.partial(middle_body, scale),
+        [shape((tokens, width), F32), shape((tokens, width)),
+         shape((width, tokens), F32), shape((width, tokens), F32)],
+        [VMEM] * 6,
+        (query, back, state, wq, wo, qs[:, None]),
+        (diag, pltpu.VMEM((both, mine), BF16), pltpu.VMEM((mine, both), BF16)),
+        2 * ff, 32 << 20,
+    )
+    out_sum = out_own + swap_core(out_other).astype(F32)
+    attention_out = (out_sum * out_scale[None, :]).astype(BF16).T
+    res_own, res_other = call(
+        tail_body,
+        [shape((width, tokens), F32), shape((width, tokens))],
+        [VMEM] * 9,
+        (key, value, term, wk, wv, ks[None], vs[None], in_own, in_other),
+        (diag, pltpu.VMEM((both, mine), BF16), pltpu.VMEM((both, mine), BF16)),
+        2 * ff, 32 << 20,
+    )
+    input_grad = (res_own + swap_core(res_other).astype(F32)).astype(BF16)
+    return attention_out, input_grad
 
 
 highest = lax.Precision.HIGHEST
@@ -29,7 +321,7 @@
     return target.at[:, blocks, :].set(shaped).reshape(feature_rows, total_blocks * BLOCK)
 
 
-def per_device(
+def per_device_whole(
     features,
     grad_out,
     query_weight,
@@ -126,9 +418,13 @@
 
 
 def solution(mesh):
+    fits = mesh.shape["space"] == 4 and all(
+        mesh.shape[a] == 2 for a in ("groups", "tm", "rep")
+    )
+    split = P(None, DEVICE_AXES)
     placed = (
-        P(None, ("groups", "space", "tm", "rep")),
-        P(None, ("groups", "space", "tm", "rep")),
+        split,
+        split,
         P("space", None),
         P("space", None),
         P("space", None),
@@ -137,16 +433,13 @@
         P(),
         P(),
         P(),
-        P(("groups", "space", "tm", "rep"), None),
-        P(("groups", "space", "tm", "rep")),
+        P(DEVICE_AXES, None),
+        P(DEVICE_AXES),
     )
     return jax.shard_map(
-        per_device,
+        per_device_split if fits else per_device_whole,
         mesh=mesh,
         in_specs=placed,
-        out_specs=(
-            P(None, ("groups", "space", "tm", "rep")),
-            P(None, ("groups", "space", "tm", "rep")),
-        ),
+        out_specs=(split, split),
         check_vma=False,
     )

time: 322 us -> 131 us (0.41)
  waiting for transfers between devices: 267 us -> 25 us
  starting transfers between devices: 0.19 us -> 39.6 us
  local copies, waits for them, and re-layouts: 11.8 us -> 37 us
  matrix products: 24.3 us -> 0 us
  Pallas kernels: 0 us -> 17.7 us
  between operations: 14.8 us -> 1.78 us
  other arithmetic: 3.19 us -> 8.69 us
    all_gather x4 -> x0, waiting for transfers between devices: 172 us -> none  [the longest x1 43.3 us: per_device(): lax.all_gather(key_weight, 'space', axis=0, tiled=True)]
    psum x1 -> x0, waiting for transfers between devices: 92.1 us -> none  [per_device(): lax.psum((state_local, grad_local), ('space', 'tm', 'rep'))]
    ppermute x0 -> x30, starting transfers between devices: none -> 39.6 us  [the longest x12 20.4 us: turn_z(): return lax.ppermute(a, 'space', [(i, (i + step) % 4) for i in range(4)])]
    ppermute x0 -> x30, waiting for transfers between devices: none -> 25 us  [the longest x6 14 us: swap_x(): return lax.ppermute(a, 'tm', [(0, 1), (1, 0)])]
    dot_general x14 -> x0, matrix products: 24.3 us -> none  [the longest x3 9.1 us: per_device(): lax.dot_general(piece_w, part_rows, contract_first, preferred_element_typ...]
    pallas_call x0 -> x4, Pallas kernels: none -> 17.7 us  [call(): pl.pallas_call(body, out_shape=tuple(outs), in_specs=in_specs, out_specs=...]
    unnamed x32 -> x64, local copies, waits for them, and re-layouts: 6.18 us -> 20.6 us
    dynamic_slice x0 -> x7, local copies, waits for them, and re-layouts: none -> 8.15 us  [the longest x2 4.89 us: columns(): lax.dynamic_index_in_dim(split, c, 2, keepdims=False).reshape(-1, mine)]
  transfers between devices with their start and end apart: 5 -> 30, of which waited for: 5 -> 11; matrix products, arithmetic and copies ran while one was open for 4% -> 27% of each run, Pallas kernels for 0% -> 14%
where the time goes in v1:
time: 131 us; the launch traced here: 130 us
  starting transfers between devices  39.6 us (30%)
  local copies, waits for them, and re-layouts  37 us (28%)
  waiting for transfers between devices  25 us (19%)
  Pallas kernels  17.7 us (14%)
  other arithmetic  8.69 us (7%)
  between operations  1.78 us (1%)
    unnamed x64, local copies, waits for them, and re-layouts  20.6 us
    ppermute x12, starting transfers between devices, turn_z(): return lax.ppermute(a, 'space', [(i, (i + step) % 4) for i in range(4)])  20.4 us
    pallas_call x4, Pallas kernels, call(): pl.pallas_call(body, out_shape=tuple(outs), in_specs=in_specs, out_specs=...  17.7 us
    ppermute x6, waiting for transfers between devices, swap_x(): return lax.ppermute(a, 'tm', [(0, 1), (1, 0)])  14 us
    ppermute x12, waiting for transfers between devices, turn_z(): return lax.ppermute(a, 'space', [(i, (i + step) % 4) for i in range(4)])  8.9 us
    ppermute x6, starting transfers between devices, swap_x(): return lax.ppermute(a, 'tm', [(0, 1), (1, 0)])  7.23 us
    ppermute x4, starting transfers between devices, swap_z(): return lax.ppermute(a, 'space', [(i, i ^ bit) for i in range(4)])  6.2 us
    ppermute x4, starting transfers between devices, swap_y(): return lax.ppermute(a, 'groups', [(0, 1), (1, 0)])  5.13 us
  transfers between devices with their start and end apart: 30, of which 11 were waited for; matrix products, arithmetic and copies ran while one was open for 27% of the time, Pallas kernels for 14%

profile of v1, /device:TPU:0, one launch (start us, length us, event | category | flops | bytes accessed | tf_op | source)
XLA Modules:
  0.0 129.7 jit_solution(14185581423869608879)
XLA Ops:
  2.3 4.0 %collective-permute-start.9 = (bf16[32,1024]{1,0:T(8,128)(2,1)}, bf16[32,1024]{1,0:T(8,128)(2,1)}, u32[]{:S(2)}, u32[]{:S(2)}) collective-permute-start(bf16[32,1024]{1,0:T(8,128)(2,1)} %constant_dynamic-slice_fusion.5), channel_id=1, source_target_pairs={{0,8},{4,12},{8,0},{12,4},{1,9},{5,13},{9,1},{13,5},{2,10},{6,14},... | collective-permute-start | bytes 196616 | tf_op jit(solution)/shard_map/ppermute | solution.py:59
  6.4 1.3 %collective-permute-start.8 = (bf16[32,1024]{1,0:T(8,128)(2,1)}, bf16[32,1024]{1,0:T(8,128)(2,1)}, u32[]{:S(2)}, u32[]{:S(2)}) collective-permute-start(bf16[32,1024]{1,0:T(8,128)(2,1)} %constant_dynamic-slice_fusion.5), channel_id=1, source_target_pairs={{0,12},{4,0},{8,4},{12,8},{1,13},{5,1},{9,5},{13,9},{2,14},{6,2},{... | collective-permute-start | bytes 196616 | tf_op jit(solution)/shard_map/ppermute | solution.py:59
  8.4 1.4 %reshape.64 = bf16[256,4,2,128]{3,2,1,0:T(2,128)(2,1)S(1)} reshape(bf16[256,1024]{1,0:T(8,128)(2,1)} %param.14) | data formatting | bytes 1048576 | tf_op jit(solution)/shard_map/reshape | solution.py:233
  9.8 1.6 %dynamic-slice_reduce_fusion.2 = bf16[256,4,128]{2,1,0:T(4,128)(2,1)S(1)} fusion(bf16[256,4,2,128]{3,2,1,0:T(2,128)(2,1)S(1)} %reshape.64, s32[]{:T(128)S(6)} %select_n.57), kind=kLoop, calls=%fused_computation.8 | loop fusion | bytes 524292 | tf_op jit(solution)/shard_map/jit(dynamic_index_in_dim)/dynamic_slice | solution.py:234
  12.1 1.0 collective-permute-start.4
  13.1 2.9 %collective-permute-start.3 = (bf16[64,512]{1,0:T(8,128)(2,1)}, bf16[64,512]{1,0:T(8,128)(2,1)}, u32[]{:S(2)}, u32[]{:S(2)}) collective-permute-start(bf16[64,512]{1,0:T(8,128)(2,1)} %constant_dynamic-slice_fusion.7), channel_id=1, source_target_pairs={{0,12},{4,0},{8,4},{12,8},{1,13},{5,1},{9,5},{13,9},{2,14},{6,2},{... | collective-permute-start | bytes 196616 | tf_op jit(solution)/shard_map/ppermute | solution.py:59
  18.3 3.3 %dynamic-slice_reduce_fusion = (bf16[256,4,128]{2,1,0:T(4,128)(2,1)S(1)}, bf16[256,4,128]{2,1,0:T(4,128)(2,1)S(1)}) fusion(bf16[256,4,2,128]{3,2,1,0:T(2,128)(2,1)S(1)} %reshape.69, s32[]{:T(128)S(6)} %select_n.57, bf16[256,4,2,128]{3,2,1,0:T(2,128)(2,1)S(1)} %reshape.67), kind=kLoop, calls=%fused_computation.6 | loop fusion | bytes 1048580 | tf_op jit(solution)/shard_map/jit(dynamic_index_in_dim)/dynamic_slice | solution.py:234
  23.0 1.5 %copy.31 = bf16[1024,512]{0,1:T(8,128)(2,1)S(1)} copy(bf16[1024,512]{1,0:T(8,128)(2,1)} %param.12) | data formatting | bytes 2097152 | tf_op args[0]
  24.5 1.3 %copy.32 = bf16[1024,512]{0,1:T(8,128)(2,1)} copy(bf16[1024,512]{1,0:T(8,128)(2,1)S(1)} %copy-done.14) | data formatting | bytes 2097152 | tf_op args[1]
  25.9 2.6 %fusion = (bf16[1024,512]{0,1:T(8,128)(2,1)}, bf16[512,1024]{1,0:T(8,128)(2,1)S(1)}) fusion(bf16[1024,512]{0,1:T(8,128)(2,1)} %copy.32, f32[1024]{0:T(1024)S(1)} %copy-done.17, pred[512]{0:T(512)(128)(4,1)S(1)} %compare_reduce_fusion, bf16[1024,512]{0,1:T(8,128)(2,1)S(1)} %copy.31), kind=kLoop, calls=%fused_computation.3 | loop fusion | flops 2621440 | bytes 4198912 | tf_op jit(solution)/shard_map/jit(_where)/select_n | solution.py:257
  28.6 1.5 %copy.34.g_own = bf16[1024,512]{1,0:T(8,128)(2,1)S(1)} copy(bf16[1024,512]{0,1:T(8,128)(2,1)} %get-tuple-element.42) | data formatting | bytes 2097152 | tf_op jit(solution)/shard_map/jit(_where)/select_n | solution.py:257
  30.2 1.3 %collective-permute-start.14 = (bf16[64,512]{1,0:T(8,128)(2,1)}, bf16[64,512]{1,0:T(8,128)(2,1)S(1)}, u32[]{:S(2)}, u32[]{:S(2)}) collective-permute-start(bf16[64,512]{1,0:T(8,128)(2,1)} %constant_dynamic-slice_fusion.3), channel_id=1, source_target_pairs={{0,8},{4,12},{8,0},{12,4},{1,9},{5,13},{9,1},{13,5},{2,10},{6,14},... | collective-permute-start | bytes 196616 | tf_op jit(solution)/shard_map/ppermute | solution.py:59
  31.5 3.1 %collective-permute-start.12 = (bf16[64,512]{1,0:T(8,128)(2,1)}, bf16[64,512]{1,0:T(8,128)(2,1)S(1)}, u32[]{:S(2)}, u32[]{:S(2)}) collective-permute-start(bf16[64,512]{1,0:T(8,128)(2,1)} %constant_dynamic-slice_fusion.3), channel_id=1, source_target_pairs={{0,4},{4,8},{8,12},{12,0},{1,5},{5,9},{9,13},{13,1},{2,6},{6,10},{... | collective-permute-start | bytes 196616 | tf_op jit(solution)/shard_map/ppermute | solution.py:59
  35.5 1.5 %constant_dynamic-update-slice_fusion.7 = bf16[192,1024]{1,0:T(8,128)(2,1)} fusion(bf16[32,1024]{1,0:T(8,128)(2,1)} %collective-permute-done.7), kind=kLoop, calls=%fused_computation.33 | loop fusion | bytes 131072
  37.9 1.7 %collective-permute-start.13 = (bf16[64,512]{1,0:T(8,128)(2,1)}, bf16[64,512]{1,0:T(8,128)(2,1)S(1)}, u32[]{:S(2)}, u32[]{:S(2)}) collective-permute-start(bf16[64,512]{1,0:T(8,128)(2,1)} %constant_dynamic-slice_fusion.3), channel_id=1, source_target_pairs={{0,12},{4,0},{8,4},{12,8},{1,13},{5,1},{9,5},{13,9},{2,14},{6,2},{... | collective-permute-start | bytes 196616 | tf_op jit(solution)/shard_map/ppermute | solution.py:59
  39.6 1.1 collective-permute-start.19
  40.7 1.7 %collective-permute-done.13 = bf16[64,512]{1,0:T(8,128)(2,1)S(1)} collective-permute-done((bf16[64,512]{1,0:T(8,128)(2,1)}, bf16[64,512]{1,0:T(8,128)(2,1)S(1)}, u32[]{:S(2)}, u32[]{:S(2)}) %collective-permute-start.13) | collective-permute-done | bytes 65568 | tf_op jit(solution)/shard_map/ppermute | solution.py:59
  42.4 1.2 collective-permute-start.17
  43.6 1.5 %constant_dynamic-update-slice_fusion.6 = bf16[192,1024]{1,0:T(8,128)(2,1)} fusion(bf16[192,1024]{1,0:T(8,128)(2,1)} %constant_dynamic-update-slice_fusion.7, bf16[32,1024]{1,0:T(8,128)(2,1)} %collective-permute-done.8), kind=kLoop, calls=%fused_computation.32 | loop fusion | bytes 131072
  45.1 3.9 %collective-permute-done.17 = bf16[64,512]{1,0:T(8,128)(2,1)S(1)} collective-permute-done((bf16[64,512]{1,0:T(8,128)(2,1)}, bf16[64,512]{1,0:T(8,128)(2,1)S(1)}, u32[]{:S(2)}, u32[]{:S(2)}) %collective-permute-start.17) | collective-permute-done | bytes 65568 | tf_op jit(solution)/shard_map/ppermute | solution.py:59
  48.9 2.0 %collective-permute-start.18 = (bf16[64,512]{1,0:T(8,128)(2,1)}, bf16[64,512]{1,0:T(8,128)(2,1)S(1)}, u32[]{:S(2)}, u32[]{:S(2)}) collective-permute-start(bf16[64,512]{1,0:T(8,128)(2,1)} %constant_dynamic-slice_fusion.2), channel_id=1, source_target_pairs={{0,12},{4,0},{8,4},{12,8},{1,13},{5,1},{9,5},{13,9},{2,14},{6,2},{... | collective-permute-start | bytes 196616 | tf_op jit(solution)/shard_map/ppermute | solution.py:59
  51.0 2.4 %collective-permute-done.18 = bf16[64,512]{1,0:T(8,128)(2,1)S(1)} collective-permute-done((bf16[64,512]{1,0:T(8,128)(2,1)}, bf16[64,512]{1,0:T(8,128)(2,1)S(1)}, u32[]{:S(2)}, u32[]{:S(2)}) %collective-permute-start.18) | collective-permute-done | bytes 65568 | tf_op jit(solution)/shard_map/ppermute | solution.py:59
  53.4 1.5 %constant_dynamic-update-slice_fusion.5 = bf16[192,1024]{1,0:T(8,128)(2,1)} fusion(bf16[192,1024]{1,0:T(8,128)(2,1)} %constant_dynamic-update-slice_fusion.6, bf16[32,1024]{1,0:T(8,128)(2,1)} %collective-permute-done.9), kind=kLoop, calls=%fused_computation.31 | loop fusion | bytes 131072
  54.9 1.5 %collective-permute-start.10 = (bf16[96,1024]{1,0:T(8,128)(2,1)S(1)}, bf16[96,1024]{1,0:T(8,128)(2,1)S(1)}, u32[]{:S(2)}, u32[]{:S(2)}) collective-permute-start(bf16[96,1024]{1,0:T(8,128)(2,1)S(1)} %pad_maximum_fusion.1), channel_id=1, source_target_pairs={{0,16},{16,0},{1,17},{17,1},{2,18},{18,2},{3,19},{19,3},{4,20},{20... | collective-permute-start | bytes 589832 | tf_op jit(solution)/shard_map/ppermute | solution.py:51
  57.6 1.5 %collective-permute-start.15 = (bf16[192,512]{1,0:T(8,128)(2,1)S(1)}, bf16[192,512]{1,0:T(8,128)(2,1)S(1)}, u32[]{:S(2)}, u32[]{:S(2)}) collective-permute-start(bf16[192,512]{1,0:T(8,128)(2,1)S(1)} %pad_maximum_fusion.2), channel_id=1, source_target_pairs={{0,2},{2,0},{1,3},{3,1},{4,6},{6,4},{5,7},{7,5},{8,10},{10,8},{9,1... | collective-permute-start | bytes 589832 | tf_op jit(solution)/shard_map/ppermute | solution.py:47
  60.0 1.5 %constant_dynamic-update-slice_fusion.2 = bf16[384,512]{1,0:T(8,128)(2,1)} fusion(bf16[384,512]{1,0:T(8,128)(2,1)} %constant_dynamic-update-slice_fusion.3, bf16[64,512]{1,0:T(8,128)(2,1)} %collective-permute-done.3), kind=kLoop, calls=%fused_computation.28 | loop fusion | bytes 131072
  61.4 1.5 %constant_dynamic-update-slice_fusion.1 = bf16[384,512]{1,0:T(8,128)(2,1)} fusion(bf16[384,512]{1,0:T(8,128)(2,1)} %constant_dynamic-update-slice_fusion.2, bf16[64,512]{1,0:T(8,128)(2,1)} %collective-permute-done.4), kind=kLoop, calls=%fused_computation.27 | loop fusion | bytes 131072
  62.9 1.4 %collective-permute-done.15 = bf16[192,512]{1,0:T(8,128)(2,1)S(1)} collective-permute-done((bf16[192,512]{1,0:T(8,128)(2,1)S(1)}, bf16[192,512]{1,0:T(8,128)(2,1)S(1)}, u32[]{:S(2)}, u32[]{:S(2)}) %collective-permute-start.15) | collective-permute-done | bytes 196640 | tf_op jit(solution)/shard_map/ppermute | solution.py:47
  64.3 1.6 %collective-permute-start.16 = (bf16[384,512]{1,0:T(8,128)(2,1)S(1)}, bf16[384,512]{1,0:T(8,128)(2,1)S(1)}, u32[]{:S(2)}, u32[]{:S(2)}) collective-permute-start(bf16[384,512]{1,0:T(8,128)(2,1)S(1)} %constant_dynamic-update-slice_fusion.8.kp), channel_id=1, source_target_pairs={{0,16},{16,0},{1,17},{17,1},{2,18},{18,2},{3,19},{19,3},{4,20},{20... | collective-permute-start | bytes 1179656 | tf_op jit(solution)/shard_map/ppermute | solution.py:51
  66.7 1.5 %collective-permute-start.5 = (bf16[192,512]{1,0:T(8,128)(2,1)S(1)}, bf16[192,512]{1,0:T(8,128)(2,1)S(1)}, u32[]{:S(2)}, u32[]{:S(2)}) collective-permute-start(bf16[192,512]{1,0:T(8,128)(2,1)S(1)} %pad_maximum_fusion), channel_id=1, source_target_pairs={{0,2},{2,0},{1,3},{3,1},{4,6},{6,4},{5,7},{7,5},{8,10},{10,8},{9,1... | collective-permute-start | bytes 589832 | tf_op jit(solution)/shard_map/ppermute | solution.py:47
  69.5 5.0 %collective-permute-done.5 = bf16[192,512]{1,0:T(8,128)(2,1)S(1)} collective-permute-done((bf16[192,512]{1,0:T(8,128)(2,1)S(1)}, bf16[192,512]{1,0:T(8,128)(2,1)S(1)}, u32[]{:S(2)}, u32[]{:S(2)}) %collective-permute-start.5) | collective-permute-done | bytes 196640 | tf_op jit(solution)/shard_map/ppermute | solution.py:47
  74.6 1.5 %collective-permute-start.11 = (bf16[192,1024]{1,0:T(8,128)(2,1)}, bf16[192,1024]{1,0:T(8,128)(2,1)}, u32[]{:S(2)}, u32[]{:S(2)}) collective-permute-start(bf16[192,1024]{1,0:T(8,128)(2,1)} %constant_dynamic-update-slice_fusion.4.op), channel_id=1, source_target_pairs={{0,2},{2,0},{1,3},{3,1},{4,6},{6,4},{5,7},{7,5},{8,10},{10,8},{9,1... | collective-permute-start | bytes 1179656 | tf_op jit(solution)/shard_map/ppermute | solution.py:47
  76.7 1.5 %collective-permute-start.6 = (bf16[384,512]{1,0:T(8,128)(2,1)}, bf16[384,512]{1,0:T(8,128)(2,1)}, u32[]{:S(2)}, u32[]{:S(2)}) collective-permute-start(bf16[384,512]{1,0:T(8,128)(2,1)} %constant_dynamic-update-slice_fusion.qp), channel_id=1, source_target_pairs={{0,16},{16,0},{1,17},{17,1},{2,18},{18,2},{3,19},{19,3},{4,20},{20... | collective-permute-start | bytes 1179656 | tf_op jit(solution)/shard_map/ppermute | solution.py:51
  79.1 3.9 %collective-permute-done.21.vf = bf16[384,512]{1,0:T(8,128)(2,1)S(1)} collective-permute-done((bf16[384,512]{1,0:T(8,128)(2,1)S(1)}, bf16[384,512]{1,0:T(8,128)(2,1)S(1)}, u32[]{:S(2)}, u32[]{:S(2)}) %collective-permute-start.21) | collective-permute-done | bytes 393248 | tf_op jit(solution)/shard_map/ppermute | solution.py:47
  83.0 6.0 %shard_map.132 = (bf16[1024,512]{1,0:T(8,128)(2,1)S(1)}, bf16[1024,512]{1,0:T(8,128)(2,1)S(1)}, f32[256,128]{1,0:T(8,128)S(1)}, bf16[1024,512]{1,0:T(8,128)(2,1)S(1)}, bf16[1024,512]{1,0:T(8,128)(2,1)S(1)}) custom-call(s32[2]{0:T(128)S(1)} %pad_add_fusion.pos, bf16[512,1024]{1,0:T(8,128)(2,1)S(1)} %get-tuple-element.43.x_own, ...), custom_call_target="tpu_custom_call" | custom-call | flops 2147483648 | bytes 8523784 | tf_op jit(solution)/shard_map/pallas_call | solution.py:31
  93.0 1.6 %collective-permute-start.22 = (bf16[256,128]{1,0:T(8,128)(2,1)S(1)}, bf16[256,128]{1,0:T(8,128)(2,1)S(1)}, u32[]{:S(2)}, u32[]{:S(2)}) collective-permute-start(bf16[256,128]{1,0:T(8,128)(2,1)S(1)} %convert_element_type.56), channel_id=1, source_target_pairs={{0,2},{2,0},{1,3},{3,1},{4,6},{6,4},{5,7},{7,5},{8,10},{10,8},{9,1... | collective-permute-start | bytes 196616 | tf_op jit(solution)/shard_map/ppermute | solution.py:47
  94.5 2.3 %copy.35.g_other = bf16[1024,512]{1,0:T(8,128)(2,1)} copy(bf16[1024,512]{0,1:T(8,128)(2,1)} %collective-permute-done.1) | data formatting | bytes 2097152 | tf_op jit(solution)/shard_map/ppermute | solution.py:55
  96.8 1.2 copy-done.1
  98.1 1.2 copy-done.13
  99.3 4.8 %shard_map.131 = (bf16[1024,512]{1,0:T(8,128)(2,1)S(1)}, bf16[512,1024]{1,0:T(8,128)(2,1)S(1)}, f32[256,128]{1,0:T(8,128)S(1)}, bf16[1024,512]{1,0:T(8,128)(2,1)S(1)}, bf16[512,1024]{1,0:T(8,128)(2,1)S(1)}) custom-call(s32[2]{0:T(128)S(1)} %pad_add_fusion.pos, bf16[512,1024]{1,0:T(8,128)(2,1)S(1)} %get-tuple-element.43.x_own, ...), custom_call_target="tpu_custom_call" | custom-call | flops 2147483648 | bytes 10618888 | tf_op jit(solution)/shard_map/pallas_call | solution.py:31
  104.8 3.6 %collective-permute-done.26 = bf16[256,128]{1,0:T(8,128)(2,1)S(1)} collective-permute-done((bf16[256,128]{1,0:T(8,128)(2,1)S(1)}, bf16[256,128]{1,0:T(8,128)(2,1)S(1)}, u32[]{:S(2)}, u32[]{:S(2)}) %collective-permute-start.26) | collective-permute-done | bytes 65568 | tf_op jit(solution)/shard_map/ppermute | solution.py:47
  109.1 3.9 %collective-permute-start.24 = (bf16[256,128]{1,0:T(8,128)(2,1)S(1)}, bf16[256,128]{1,0:T(8,128)(2,1)S(1)}, u32[]{:S(2)}, u32[]{:S(2)}) collective-permute-start(bf16[256,128]{1,0:T(8,128)(2,1)S(1)} %fusion.4), channel_id=1, source_target_pairs={{0,8},{4,12},{8,0},{12,4},{1,9},{5,13},{9,1},{13,5},{2,10},{6,14},... | collective-permute-start | bytes 196616 | tf_op jit(solution)/shard_map/ppermute | solution.py:63
  113.0 2.2 %collective-permute-start.28 = (bf16[256,128]{1,0:T(8,128)(2,1)S(1)}, bf16[256,128]{1,0:T(8,128)(2,1)S(1)}, u32[]{:S(2)}, u32[]{:S(2)}) collective-permute-start(bf16[256,128]{1,0:T(8,128)(2,1)S(1)} %fusion.5), channel_id=1, source_target_pairs={{0,8},{4,12},{8,0},{12,4},{1,9},{5,13},{9,1},{13,5},{2,10},{6,14},... | collective-permute-start | bytes 196616 | tf_op jit(solution)/shard_map/ppermute | solution.py:63
  116.0 2.9 %shard_map.133 = (f32[512,1024]{1,0:T(8,128)S(1)}, bf16[512,1024]{1,0:T(8,128)(2,1)S(1)}, f32[1024,512]{1,0:T(8,128)S(1)}, f32[1024,512]{1,0:T(8,128)S(1)}) custom-call(bf16[1024,512]{1,0:T(8,128)(2,1)S(1)} %get-tuple-element.18.query, bf16[512,1024]{1,0:T(8,128)(2,1)S(1)} %get-tuple-element.19.back, f32[256,128]{1,0:T(8,128)S(1)} %convert_add_fusion.3.state, ...), custom_call_target="tpu_custom_call" | custom-call | flops 2147483648 | bytes 11667456 | tf_op jit(solution)/shard_map/pallas_call | solution.py:31
  119.1 3.9 %shard_map.134 = (f32[1024,512]{1,0:T(8,128)S(1)}, bf16[1024,512]{1,0:T(8,128)(2,1)}) custom-call(bf16[1024,512]{1,0:T(8,128)(2,1)S(1)} %copy-done.3, bf16[1024,512]{1,0:T(8,128)(2,1)S(1)} %copy-done.5, f32[256,128]{1,0:T(8,128)S(1)} %convert_add_fusion.term, bf16[1024,512]{1,0:T(8,128)(2,1)S(1)} %copy-done.7, bf16[1024,512]{1,0:T(8,128)(2,1)S(1)} %copy-done.9, ...), custom_call_target="tpu_custom_call" | custom-call | flops 2147483648 | bytes 11669504 | tf_op jit(solution)/shard_map/pallas_call | solution.py:31
  123.5 1.3 %fusion.1 = bf16[1024,512]{0,1:T(8,128)(2,1)} fusion(f32[512,1024]{1,0:T(8,128)S(1)} %get-tuple-element.23, bf16[512,1024]{1,0:T(8,128)(2,1)S(1)} %collective-permute-done.25, f32[1024]{0:T(1024)S(1)} %copy-done.18), kind=kLoop, calls=%fused_computation.4 | loop fusion | flops 2097152 | bytes 4198400 | tf_op jit(solution)/shard_map/transpose | solution.py:292
  124.9 2.3 %copy.39 = bf16[1024,512]{1,0:T(8,128)(2,1)} copy(bf16[1024,512]{0,1:T(8,128)(2,1)} %fusion.1) | data formatting | bytes 2097152
  127.1 2.5 %add_convert_fusion = bf16[1024,512]{1,0:T(8,128)(2,1)} fusion(f32[1024,512]{1,0:T(8,128)S(1)} %get-tuple-element.32, bf16[1024,512]{1,0:T(8,128)(2,1)} %collective-permute-done.29), kind=kLoop, calls=%fused_computation | loop fusion | flops 1572864 | bytes 4194304 | tf_op jit(solution)/shard_map/convert_element_type | solution.py:301
  (118 shorter events, 20.4 us)
Async XLA Ops:
  0.6 16.1 %copy-start.21 = (f32[1024]{0:T(1024)S(1)}, f32[1024]{0:T(1024)}, u32[]{:S(2)}) copy-start(f32[1024]{0:T(1024)} %param.18) | copy-start | bytes 12292
  0.7 16.9 %copy-start.15 = (bf16[256,1024]{1,0:T(8,128)(2,1)S(1)}, bf16[256,1024]{1,0:T(8,128)(2,1)}, u32[]{:S(2)}) copy-start(bf16[256,1024]{1,0:T(8,128)(2,1)} %param.15) | copy-start | bytes 1572868
  0.7 17.3 %copy-start.16 = (bf16[256,1024]{1,0:T(8,128)(2,1)S(1)}, bf16[256,1024]{1,0:T(8,128)(2,1)}, u32[]{:S(2)}) copy-start(bf16[256,1024]{1,0:T(8,128)(2,1)} %param.16) | copy-start | bytes 1572868
  2.3 27.8 %collective-permute-start.9 = (bf16[32,1024]{1,0:T(8,128)(2,1)}, bf16[32,1024]{1,0:T(8,128)(2,1)}, u32[]{:S(2)}, u32[]{:S(2)}) collective-permute-start(bf16[32,1024]{1,0:T(8,128)(2,1)} %constant_dynamic-slice_fusion.5), channel_id=1, source_target_pairs={{0,8},{4,12},{8,0},{12,4},{1,9},{5,13},{9,1},{13,5},{2,10},{6,14},... | collective-permute-start | bytes 196616 | tf_op jit(solution)/shard_map/ppermute | solution.py:59
  6.4 23.9 %collective-permute-start.8 = (bf16[32,1024]{1,0:T(8,128)(2,1)}, bf16[32,1024]{1,0:T(8,128)(2,1)}, u32[]{:S(2)}, u32[]{:S(2)}) collective-permute-start(bf16[32,1024]{1,0:T(8,128)(2,1)} %constant_dynamic-slice_fusion.5), channel_id=1, source_target_pairs={{0,12},{4,0},{8,4},{12,8},{1,13},{5,1},{9,5},{13,9},{2,14},{6,2},{... | collective-permute-start | bytes 196616 | tf_op jit(solution)/shard_map/ppermute | solution.py:59
  7.7 23.8 %collective-permute-start.7 = (bf16[32,1024]{1,0:T(8,128)(2,1)}, bf16[32,1024]{1,0:T(8,128)(2,1)}, u32[]{:S(2)}, u32[]{:S(2)}) collective-permute-start(bf16[32,1024]{1,0:T(8,128)(2,1)} %constant_dynamic-slice_fusion.5), channel_id=1, source_target_pairs={{0,4},{4,8},{8,12},{12,0},{1,5},{5,9},{9,13},{13,1},{2,6},{6,10},{... | collective-permute-start | bytes 196616 | tf_op jit(solution)/shard_map/ppermute | solution.py:59
  12.1 45.0 %collective-permute-start.4 = (bf16[64,512]{1,0:T(8,128)(2,1)}, bf16[64,512]{1,0:T(8,128)(2,1)}, u32[]{:S(2)}, u32[]{:S(2)}) collective-permute-start(bf16[64,512]{1,0:T(8,128)(2,1)} %constant_dynamic-slice_fusion.7), channel_id=1, source_target_pairs={{0,8},{4,12},{8,0},{12,4},{1,9},{5,13},{9,1},{13,5},{2,10},{6,14},... | collective-permute-start | bytes 196616 | tf_op jit(solution)/shard_map/ppermute | solution.py:59
  13.1 44.4 %collective-permute-start.3 = (bf16[64,512]{1,0:T(8,128)(2,1)}, bf16[64,512]{1,0:T(8,128)(2,1)}, u32[]{:S(2)}, u32[]{:S(2)}) collective-permute-start(bf16[64,512]{1,0:T(8,128)(2,1)} %constant_dynamic-slice_fusion.7), channel_id=1, source_target_pairs={{0,12},{4,0},{8,4},{12,8},{1,13},{5,1},{9,5},{13,9},{2,14},{6,2},{... | collective-permute-start | bytes 196616 | tf_op jit(solution)/shard_map/ppermute | solution.py:59
  21.6 2.9 %copy-start.14 = (bf16[1024,512]{1,0:T(8,128)(2,1)S(1)}, bf16[1024,512]{1,0:T(8,128)(2,1)}, u32[]{:S(2)}) copy-start(bf16[1024,512]{1,0:T(8,128)(2,1)} %param.13) | copy-start | bytes 3145732
  23.0 2.8 %copy-start.22 = (s32[1,6]{1,0:T(1,128)S(1)}, s32[1,6]{1,0:T(1,128)}, u32[]{:S(2)}) copy-start(s32[1,6]{1,0:T(1,128)} %param.22) | copy-start | bytes 76
  23.0 2.9 %copy-start.17 = (f32[1024]{0:T(1024)S(1)}, f32[1024]{0:T(1024)}, u32[]{:S(2)}) copy-start(f32[1024]{0:T(1024)} %param.21) | copy-start | bytes 12292
  28.6 1.5 %copy-start.19 = (f32[1024]{0:T(1024)S(1)}, f32[1024]{0:T(1024)}, u32[]{:S(2)}) copy-start(f32[1024]{0:T(1024)} %param.19) | copy-start | bytes 12292
  28.6 1.5 %copy-start.20 = (f32[1024]{0:T(1024)S(1)}, f32[1024]{0:T(1024)}, u32[]{:S(2)}) copy-start(f32[1024]{0:T(1024)} %param.20) | copy-start | bytes 12292
  30.1 24.8 %collective-permute-start.2 = (bf16[64,512]{1,0:T(8,128)(2,1)}, bf16[64,512]{1,0:T(8,128)(2,1)S(1)}, u32[]{:S(2)}, u32[]{:S(2)}) collective-permute-start(bf16[64,512]{1,0:T(8,128)(2,1)} %constant_dynamic-slice_fusion.7), channel_id=1, source_target_pairs={{0,4},{4,8},{8,12},{12,0},{1,5},{5,9},{9,13},{13,1},{2,6},{6,10},{... | collective-permute-start | bytes 196616 | tf_op jit(solution)/shard_map/ppermute | solution.py:59
  30.2 9.3 %collective-permute-start.14 = (bf16[64,512]{1,0:T(8,128)(2,1)}, bf16[64,512]{1,0:T(8,128)(2,1)S(1)}, u32[]{:S(2)}, u32[]{:S(2)}) collective-permute-start(bf16[64,512]{1,0:T(8,128)(2,1)} %constant_dynamic-slice_fusion.3), channel_id=1, source_target_pairs={{0,8},{4,12},{8,0},{12,4},{1,9},{5,13},{9,1},{13,5},{2,10},{6,14},... | collective-permute-start | bytes 196616 | tf_op jit(solution)/shard_map/ppermute | solution.py:59
  31.5 6.4 %collective-permute-start.12 = (bf16[64,512]{1,0:T(8,128)(2,1)}, bf16[64,512]{1,0:T(8,128)(2,1)S(1)}, u32[]{:S(2)}, u32[]{:S(2)}) collective-permute-start(bf16[64,512]{1,0:T(8,128)(2,1)} %constant_dynamic-slice_fusion.3), channel_id=1, source_target_pairs={{0,4},{4,8},{8,12},{12,0},{1,5},{5,9},{9,13},{13,1},{2,6},{6,10},{... | collective-permute-start | bytes 196616 | tf_op jit(solution)/shard_map/ppermute | solution.py:59
  37.9 4.5 %collective-permute-start.13 = (bf16[64,512]{1,0:T(8,128)(2,1)}, bf16[64,512]{1,0:T(8,128)(2,1)S(1)}, u32[]{:S(2)}, u32[]{:S(2)}) collective-permute-start(bf16[64,512]{1,0:T(8,128)(2,1)} %constant_dynamic-slice_fusion.3), channel_id=1, source_target_pairs={{0,12},{4,0},{8,4},{12,8},{1,13},{5,1},{9,5},{13,9},{2,14},{6,2},{... | collective-permute-start | bytes 196616 | tf_op jit(solution)/shard_map/ppermute | solution.py:59
  39.6 11.4 %collective-permute-start.19 = (bf16[64,512]{1,0:T(8,128)(2,1)}, bf16[64,512]{1,0:T(8,128)(2,1)S(1)}, u32[]{:S(2)}, u32[]{:S(2)}) collective-permute-start(bf16[64,512]{1,0:T(8,128)(2,1)} %constant_dynamic-slice_fusion.2), channel_id=1, source_target_pairs={{0,8},{4,12},{8,0},{12,4},{1,9},{5,13},{9,1},{13,5},{2,10},{6,14},... | collective-permute-start | bytes 196616 | tf_op jit(solution)/shard_map/ppermute | solution.py:59
  42.4 6.6 %collective-permute-start.17 = (bf16[64,512]{1,0:T(8,128)(2,1)}, bf16[64,512]{1,0:T(8,128)(2,1)S(1)}, u32[]{:S(2)}, u32[]{:S(2)}) collective-permute-start(bf16[64,512]{1,0:T(8,128)(2,1)} %constant_dynamic-slice_fusion.2), channel_id=1, source_target_pairs={{0,4},{4,8},{8,12},{12,0},{1,5},{5,9},{9,13},{13,1},{2,6},{6,10},{... | collective-permute-start | bytes 196616 | tf_op jit(solution)/shard_map/ppermute | solution.py:59
  48.9 4.5 %collective-permute-start.18 = (bf16[64,512]{1,0:T(8,128)(2,1)}, bf16[64,512]{1,0:T(8,128)(2,1)S(1)}, u32[]{:S(2)}, u32[]{:S(2)}) collective-permute-start(bf16[64,512]{1,0:T(8,128)(2,1)} %constant_dynamic-slice_fusion.2), channel_id=1, source_target_pairs={{0,12},{4,0},{8,4},{12,8},{1,13},{5,1},{9,5},{13,9},{2,14},{6,2},{... | collective-permute-start | bytes 196616 | tf_op jit(solution)/shard_map/ppermute | solution.py:59
  50.9 43.6 %collective-permute-start.1 = (bf16[1024,512]{0,1:T(8,128)(2,1)}, bf16[1024,512]{0,1:T(8,128)(2,1)}, u32[]{:S(2)}, u32[]{:S(2)}) collective-permute-start(bf16[1024,512]{0,1:T(8,128)(2,1)} %get-tuple-element.42), channel_id=1, source_target_pairs={{0,1},{1,0},{2,3},{3,2},{4,5},{5,4},{6,7},{7,6},{8,9},{9,8},{10,11... | collective-permute-start | bytes 3145736 | tf_op jit(solution)/shard_map/ppermute | solution.py:55
  53.4 29.6 %collective-permute-start = (bf16[512,1024]{1,0:T(8,128)(2,1)S(1)}, bf16[512,1024]{1,0:T(8,128)(2,1)S(1)}, u32[]{:S(2)}, u32[]{:S(2)}) collective-permute-start(bf16[512,1024]{1,0:T(8,128)(2,1)S(1)} %get-tuple-element.43.x_own), channel_id=1, source_target_pairs={{0,1},{1,0},{2,3},{3,2},{4,5},{5,4},{6,7},{7,6},{8,9},{9,8},{10,11... | collective-permute-start | bytes 3145736 | tf_op jit(solution)/shard_map/ppermute | solution.py:55
  54.9 13.3 %collective-permute-start.10 = (bf16[96,1024]{1,0:T(8,128)(2,1)S(1)}, bf16[96,1024]{1,0:T(8,128)(2,1)S(1)}, u32[]{:S(2)}, u32[]{:S(2)}) collective-permute-start(bf16[96,1024]{1,0:T(8,128)(2,1)S(1)} %pad_maximum_fusion.1), channel_id=1, source_target_pairs={{0,16},{16,0},{1,17},{17,1},{2,18},{18,2},{3,19},{19,3},{4,20},{20... | collective-permute-start | bytes 589832 | tf_op jit(solution)/shard_map/ppermute | solution.py:51
  57.1 9.7 %collective-permute-start.20 = (bf16[192,512]{1,0:T(8,128)(2,1)S(1)}, bf16[192,512]{1,0:T(8,128)(2,1)S(1)}, u32[]{:S(2)}, u32[]{:S(2)}) collective-permute-start(bf16[192,512]{1,0:T(8,128)(2,1)S(1)} %pad_maximum_fusion.3), channel_id=1, source_target_pairs={{0,16},{16,0},{1,17},{17,1},{2,18},{18,2},{3,19},{19,3},{4,20},{20... | collective-permute-start | bytes 589832 | tf_op jit(solution)/shard_map/ppermute | solution.py:51
  57.6 6.8 %collective-permute-start.15 = (bf16[192,512]{1,0:T(8,128)(2,1)S(1)}, bf16[192,512]{1,0:T(8,128)(2,1)S(1)}, u32[]{:S(2)}, u32[]{:S(2)}) collective-permute-start(bf16[192,512]{1,0:T(8,128)(2,1)S(1)} %pad_maximum_fusion.2), channel_id=1, source_target_pairs={{0,2},{2,0},{1,3},{3,1},{4,6},{6,4},{5,7},{7,5},{8,10},{10,8},{9,1... | collective-permute-start | bytes 589832 | tf_op jit(solution)/shard_map/ppermute | solution.py:47
  64.3 12.4 %collective-permute-start.16 = (bf16[384,512]{1,0:T(8,128)(2,1)S(1)}, bf16[384,512]{1,0:T(8,128)(2,1)S(1)}, u32[]{:S(2)}, u32[]{:S(2)}) collective-permute-start(bf16[384,512]{1,0:T(8,128)(2,1)S(1)} %constant_dynamic-update-slice_fusion.8.kp), channel_id=1, source_target_pairs={{0,16},{16,0},{1,17},{17,1},{2,18},{18,2},{3,19},{19,3},{4,20},{20... | collective-permute-start | bytes 1179656 | tf_op jit(solution)/shard_map/ppermute | solution.py:51
  66.7 7.8 %collective-permute-start.5 = (bf16[192,512]{1,0:T(8,128)(2,1)S(1)}, bf16[192,512]{1,0:T(8,128)(2,1)S(1)}, u32[]{:S(2)}, u32[]{:S(2)}) collective-permute-start(bf16[192,512]{1,0:T(8,128)(2,1)S(1)} %pad_maximum_fusion), channel_id=1, source_target_pairs={{0,2},{2,0},{1,3},{3,1},{4,6},{6,4},{5,7},{7,5},{8,10},{10,8},{9,1... | collective-permute-start | bytes 589832 | tf_op jit(solution)/shard_map/ppermute | solution.py:47
  68.3 14.7 %collective-permute-start.21 = (bf16[384,512]{1,0:T(8,128)(2,1)S(1)}, bf16[384,512]{1,0:T(8,128)(2,1)S(1)}, u32[]{:S(2)}, u32[]{:S(2)}) collective-permute-start(bf16[384,512]{1,0:T(8,128)(2,1)S(1)} %constant_dynamic-update-slice_fusion.12.vp), channel_id=1, source_target_pairs={{0,2},{2,0},{1,3},{3,1},{4,6},{6,4},{5,7},{7,5},{8,10},{10,8},{9,1... | collective-permute-start | bytes 1179656 | tf_op jit(solution)/shard_map/ppermute | solution.py:47
  74.6 22.2 %collective-permute-start.11 = (bf16[192,1024]{1,0:T(8,128)(2,1)}, bf16[192,1024]{1,0:T(8,128)(2,1)}, u32[]{:S(2)}, u32[]{:S(2)}) collective-permute-start(bf16[192,1024]{1,0:T(8,128)(2,1)} %constant_dynamic-update-slice_fusion.4.op), channel_id=1, source_target_pairs={{0,2},{2,0},{1,3},{3,1},{4,6},{6,4},{5,7},{7,5},{8,10},{10,8},{9,1... | collective-permute-start | bytes 1179656 | tf_op jit(solution)/shard_map/ppermute | solution.py:47
  76.7 20.1 %collective-permute-start.6 = (bf16[384,512]{1,0:T(8,128)(2,1)}, bf16[384,512]{1,0:T(8,128)(2,1)}, u32[]{:S(2)}, u32[]{:S(2)}) collective-permute-start(bf16[384,512]{1,0:T(8,128)(2,1)} %constant_dynamic-update-slice_fusion.qp), channel_id=1, source_target_pairs={{0,16},{16,0},{1,17},{17,1},{2,18},{18,2},{3,19},{19,3},{4,20},{20... | collective-permute-start | bytes 1179656 | tf_op jit(solution)/shard_map/ppermute | solution.py:51
  83.0 6.0 %copy-start.12 = (bf16[512,1024]{1,0:T(8,128)(2,1)}, bf16[512,1024]{1,0:T(8,128)(2,1)S(1)}, u32[]{:S(2)}) copy-start(bf16[512,1024]{1,0:T(8,128)(2,1)S(1)} %collective-permute-done.x_other) | copy-start | bytes 3145732
  93.0 3.9 %copy-start.10 = (bf16[128,1024]{1,0:T(8,128)(2,1)S(1)}, bf16[128,1024]{1,0:T(8,128)(2,1)}, u32[]{:S(2)}) copy-start(bf16[128,1024]{1,0:T(8,128)(2,1)} %constant_dynamic-slice_fusion.6.oo) | copy-start | bytes 786436
  93.0 11.8 %collective-permute-start.22 = (bf16[256,128]{1,0:T(8,128)(2,1)S(1)}, bf16[256,128]{1,0:T(8,128)(2,1)S(1)}, u32[]{:S(2)}, u32[]{:S(2)}) collective-permute-start(bf16[256,128]{1,0:T(8,128)(2,1)S(1)} %convert_element_type.56), channel_id=1, source_target_pairs={{0,2},{2,0},{1,3},{3,1},{4,6},{6,4},{5,7},{7,5},{8,10},{10,8},{9,1... | collective-permute-start | bytes 196616 | tf_op jit(solution)/shard_map/ppermute | solution.py:47
  96.8 1.2 copy-start.1
  98.1 1.2 copy-start.13
  99.3 16.7 %copy-start.11 = (f32[512,1]{1,0:T(8,128)S(1)}, f32[512,1]{1,0:T(8,128)}, u32[]{:S(2)}) copy-start(f32[512,1]{1,0:T(8,128)} %copy.38.qs) | copy-start | bytes 6148
  104.1 4.3 %collective-permute-start.26 = (bf16[256,128]{1,0:T(8,128)(2,1)S(1)}, bf16[256,128]{1,0:T(8,128)(2,1)S(1)}, u32[]{:S(2)}, u32[]{:S(2)}) collective-permute-start(bf16[256,128]{1,0:T(8,128)(2,1)S(1)} %convert_element_type.64), channel_id=1, source_target_pairs={{0,2},{2,0},{1,3},{3,1},{4,6},{6,4},{5,7},{7,5},{8,10},{10,8},{9,1... | collective-permute-start | bytes 196616 | tf_op jit(solution)/shard_map/ppermute | solution.py:47
  104.8 4.3 %collective-permute-start.23 = (bf16[256,128]{1,0:T(8,128)(2,1)S(1)}, bf16[256,128]{1,0:T(8,128)(2,1)S(1)}, u32[]{:S(2)}, u32[]{:S(2)}) collective-permute-start(bf16[256,128]{1,0:T(8,128)(2,1)S(1)} %fusion.2), channel_id=1, source_target_pairs={{0,4},{4,0},{8,12},{12,8},{1,5},{5,1},{9,13},{13,9},{2,6},{6,2},{1... | collective-permute-start | bytes 196616 | tf_op jit(solution)/shard_map/ppermute | solution.py:63
  108.5 4.5 %collective-permute-start.27 = (bf16[256,128]{1,0:T(8,128)(2,1)S(1)}, bf16[256,128]{1,0:T(8,128)(2,1)S(1)}, u32[]{:S(2)}, u32[]{:S(2)}) collective-permute-start(bf16[256,128]{1,0:T(8,128)(2,1)S(1)} %fusion.3), channel_id=1, source_target_pairs={{0,4},{4,0},{8,12},{12,8},{1,5},{5,1},{9,13},{13,9},{2,6},{6,2},{1... | collective-permute-start | bytes 196616 | tf_op jit(solution)/shard_map/ppermute | solution.py:63
  109.1 6.8 %collective-permute-start.24 = (bf16[256,128]{1,0:T(8,128)(2,1)S(1)}, bf16[256,128]{1,0:T(8,128)(2,1)S(1)}, u32[]{:S(2)}, u32[]{:S(2)}) collective-permute-start(bf16[256,128]{1,0:T(8,128)(2,1)S(1)} %fusion.4), channel_id=1, source_target_pairs={{0,8},{4,12},{8,0},{12,4},{1,9},{5,13},{9,1},{13,5},{2,10},{6,14},... | collective-permute-start | bytes 196616 | tf_op jit(solution)/shard_map/ppermute | solution.py:63
  113.0 6.0 %collective-permute-start.28 = (bf16[256,128]{1,0:T(8,128)(2,1)S(1)}, bf16[256,128]{1,0:T(8,128)(2,1)S(1)}, u32[]{:S(2)}, u32[]{:S(2)}) collective-permute-start(bf16[256,128]{1,0:T(8,128)(2,1)S(1)} %fusion.5), channel_id=1, source_target_pairs={{0,8},{4,12},{8,0},{12,4},{1,9},{5,13},{9,1},{13,5},{2,10},{6,14},... | collective-permute-start | bytes 196616 | tf_op jit(solution)/shard_map/ppermute | solution.py:63
  116.0 3.1 %copy-start.3 = (bf16[1024,512]{1,0:T(8,128)(2,1)S(1)}, bf16[1024,512]{1,0:T(8,128)(2,1)}, u32[]{:S(2)}) copy-start(bf16[1024,512]{1,0:T(8,128)(2,1)} %copy-done.2) | copy-start | bytes 3145732
  116.0 3.1 %copy-start.5 = (bf16[1024,512]{1,0:T(8,128)(2,1)S(1)}, bf16[1024,512]{1,0:T(8,128)(2,1)}, u32[]{:S(2)}) copy-start(bf16[1024,512]{1,0:T(8,128)(2,1)} %copy-done.4) | copy-start | bytes 3145732
  116.0 3.1 %copy-start.7 = (bf16[1024,512]{1,0:T(8,128)(2,1)S(1)}, bf16[1024,512]{1,0:T(8,128)(2,1)}, u32[]{:S(2)}) copy-start(bf16[1024,512]{1,0:T(8,128)(2,1)} %copy-done.6) | copy-start | bytes 3145732
  116.0 3.1 %copy-start.9 = (bf16[1024,512]{1,0:T(8,128)(2,1)S(1)}, bf16[1024,512]{1,0:T(8,128)(2,1)}, u32[]{:S(2)}) copy-start(bf16[1024,512]{1,0:T(8,128)(2,1)} %copy-done.8) | copy-start | bytes 3145732
  118.9 4.6 %collective-permute-start.25 = (bf16[512,1024]{1,0:T(8,128)(2,1)S(1)}, bf16[512,1024]{1,0:T(8,128)(2,1)S(1)}, u32[]{:S(2)}, u32[]{:S(2)}) collective-permute-start(bf16[512,1024]{1,0:T(8,128)(2,1)S(1)} %get-tuple-element.24), channel_id=1, source_target_pairs={{0,1},{1,0},{2,3},{3,2},{4,5},{5,4},{6,7},{7,6},{8,9},{9,8},{10,11... | collective-permute-start | bytes 3145736 | tf_op jit(solution)/shard_map/ppermute | solution.py:55
  119.1 4.4 %copy-start.18 = (f32[1024]{0:T(1024)S(1)}, f32[1024]{0:T(1024)}, u32[]{:S(2)}) copy-start(f32[1024]{0:T(1024)} %param.21) | copy-start | bytes 12292
  123.0 4.1 %collective-permute-start.29 = (bf16[1024,512]{1,0:T(8,128)(2,1)}, bf16[1024,512]{1,0:T(8,128)(2,1)}, u32[]{:S(2)}, u32[]{:S(2)}) collective-permute-start(bf16[1024,512]{1,0:T(8,128)(2,1)} %get-tuple-element.33), channel_id=1, source_target_pairs={{0,1},{1,0},{2,3},{3,2},{4,5},{5,4},{6,7},{7,6},{8,9},{9,8},{10,11... | collective-permute-start | bytes 3145736 | tf_op jit(solution)/shard_map/ppermute | solution.py:55
  (5 other events, 5.0 us)

commit v2 on v1

--- a/solution.py
+++ b/solution.py
@@ -25,14 +25,14 @@
     return lax.dot_general(a, b, (((ca,), (cb,)), ((), ())), preferred_element_type=F32)
 
 
-def call(body, outs, in_specs, args, scratch=(), flops=0, limit=None):
+def call(body, outs, in_specs, args, scratch=(), flops=0, limit=None, out_specs=None):
     size = sum(math.prod(o.shape) * o.dtype.itemsize for o in outs)
     size += sum(math.prod(a.shape) * a.dtype.itemsize for a in args)
     return pl.pallas_call(
         body,
         out_shape=tuple(outs),
         in_specs=in_specs,
-        out_specs=(VMEM,) * len(outs),
+        out_specs=out_specs or (VMEM,) * len(outs),
         scratch_shapes=scratch,
         compiler_params=pltpu.CompilerParams(vmem_limit_bytes=limit),
         cost_estimate=pl.CostEstimate(flops=flops, bytes_accessed=size, transcendentals=0),
@@ -59,50 +59,84 @@
     return lax.ppermute(a, "space", [(i, (i + step) % 4) for i in range(4)])
 
 
-def swap_z(a, bit):
-    return lax.ppermute(a, "space", [(i, i ^ bit) for i in range(4)])
-
-
-def cat(*parts):
-    return jnp.concatenate(parts, 0)
-
-
-def around(piece):
-    return cat(turn_z(piece, 1), turn_z(piece, 3), turn_z(piece, 2))
-
-
-def spread(mine, first, second):
-    pair = cat(mine, first(mine))
-    return pair, second(pair)
+def pieces(half, swap):
+    near = tuple(turn_z(half, step) for step in (1, 3, 2))
+    return near + tuple(swap(a) for a in near)
 
 
 def sum_over_chips(part):
-    for swap in (swap_x, lambda a: swap_z(a, 1), lambda a: swap_z(a, 2)):
-        part = part + swap(part.astype(BF16)).astype(F32)
+    part = part + swap_x(part.astype(BF16)).astype(F32)
+    sent = part.astype(BF16)
+    for step in (1, 3, 2):
+        part = part + turn_z(sent, step).astype(F32)
     return part
 
 
-def place(pos_ref, own_ref, pair_ref, far_ref, full_ref, sems, flips, base):
-    z, q = pos_ref[0], pos_ref[1]
-    rows = pair_ref.shape[0] // 6
-    whole = own_ref.shape[0]
-    copies = [
-        pltpu.make_async_copy(
-            own_ref, full_ref.at[pl.ds(pl.multiple_of(z * whole, whole), whole)], sems.at[base]
-        )
-    ]
-    order = ((pair_ref, 0), (pair_ref, flips[0]), (far_ref, flips[1]), (far_ref, 3))
-    for n, (ref, flip) in enumerate(order):
-        for k, step in enumerate((3, 1, 2)):
-            at = lax.rem(z + step, 4) * 4 + lax.bitwise_xor(q, flip)
+def aligned(index, size):
+    return pl.ds(pl.multiple_of(index * size, size), size)
+
+
+def send_body(pos, q, k, v, o, q_half, k_half, v_half, o_half, sems):
+    c, x, y = pos[1], pos[2], pos[3]
+    copies = []
+    for n, (ref, half, bit) in enumerate(((q, q_half, x), (k, k_half, x), (v, v_half, y))):
+        for j in range(4):
+            cols = pl.ds(pl.multiple_of(256 * j + 128 * c, 128), 128)
             copies.append(
                 pltpu.make_async_copy(
-                    ref.at[pl.ds((3 * (n % 2) + k) * rows, rows)],
-                    full_ref.at[pl.ds(pl.multiple_of(at * rows, rows), rows)],
-                    sems.at[base + 1 + 3 * n + k],
+                    ref.at[aligned(bit, half.shape[0]), cols],
+                    half.at[:, 128 * j : 128 * j + 128],
+                    sems.at[4 * n + j],
                 )
             )
+    copies.append(
+        pltpu.make_async_copy(o.at[aligned(2 * c + y, o_half.shape[0])], o_half, sems.at[12])
+    )
+    for one in copies:
+        one.start()
+    for one in copies:
+        one.wait()
+
+
+def mask_body(blocks, count, features, grad, scale, rows, cols):
+    tokens = features.shape[1]
+    block_of = lax.broadcasted_iota(jnp.int32, (1, tokens), 1) // BLOCK
+    mask = jnp.zeros((1, tokens), F32)
+    for j in range(blocks.shape[1]):
+        named = jnp.where(j < count[0], blocks[0, j], -1)
+        mask = jnp.where(block_of == named, 1.0, mask)
+    for t in range(0, features.shape[0], 256):
+        at = slice(t, t + 256)
+        rows[:, at] = (features[at, :].astype(F32) * mask).astype(BF16).T
+        cols[at, :] = (grad[at, :].astype(F32) * scale[at, :] * mask).astype(BF16)
+
+
+def place(pos_ref, own_ref, parts, full_ref, sems, axis, base, by_rows=False):
+    z, c, bit = pos_ref[0], pos_ref[1], pos_ref[axis]
+    rows = parts[0].shape[0]
+    whole = 2 * rows
+    copies = []
+
+    def add(src, dst):
+        copies.append(pltpu.make_async_copy(src, dst, sems.at[base + len(copies)]))
+
+    if by_rows:
+        add(own_ref.at[aligned(c, whole)], full_ref.at[aligned(z, whole)])
+    else:
+        for j in range(4):
+            cols = pl.ds(pl.multiple_of(256 * j + 128 * c, 128), 128)
+            add(own_ref.at[:, cols], full_ref.at[aligned(z, whole), 128 * j : 128 * j + 128])
+    for n, ref in enumerate(parts):
+        at = lax.rem(z + (3, 1, 2)[n % 3], 4) * 2 + (bit if n < 3 else 1 - bit)
+        add(ref, full_ref.at[aligned(at, rows)])
+    for one in copies:
+        one.start()
     return copies
+
+
+def wait(copies):
+    for one in copies:
+        one.wait()
 
 
 def pack(block):
@@ -126,44 +160,43 @@
         ).astype(full_ref.dtype)
 
 
-def key_value_body(
-    pos, x_own, x_other, ko, kp, kf, vo, vp, vf, ks, vs, key, value, state, wk, wv, sems
-):
-    copies = place(pos, ko, kp, kf, wk, sems, (1, 2), 0)
-    copies += place(pos, vo, vp, vf, wv, sems, (2, 1), 13)
-    for one in copies:
-        one.start()
-    for one in copies:
-        one.wait()
+def key_value_body(pos, x_own, x_other, ks, vs, *refs):
+    k, v = refs[0:7], refs[7:14]
+    key_out, value_out, state, key, value, wk, wv, sems = refs[14:]
+    fetch_k = place(pos, k[0], k[1:], wk, sems, 2, 0)
+    fetch_v = place(pos, v[0], v[1:], wv, sems, 3, 10)
     half = x_own.shape[0]
-    for n, rows in enumerate((x_own, x_other)):
-        for t in range(0, half, 256):
-            tile = rows[t : t + 256, :]
-            at = slice(n * half + t, n * half + t + 256)
-            key[at, :] = (dot(tile, wk[...], 1, 0) * ks[...]).astype(BF16)
-            value[at, :] = (dot(tile, wv[...], 1, 0) * vs[...]).astype(BF16)
+    stores = []
+    for fetch, w, scale, dst, out in (
+        (fetch_k, wk, ks, key, key_out), (fetch_v, wv, vs, value, value_out)
+    ):
+        wait(fetch)
+        for n, rows in enumerate((x_own, x_other)):
+            for t in range(0, half, 256):
+                at = slice(n * half + t, n * half + t + 256)
+                dst[at, :] = (dot(rows[t : t + 256, :], w[...], 1, 0) * scale[...]).astype(BF16)
+        stores.append(pltpu.make_async_copy(dst, out, sems.at[20 + len(stores)]))
+        stores[-1].start()
     for g in range(2):
         cols = slice(256 * g, 256 * g + 256)
         a, b = pack(dot(key[:, cols], value[:, cols], 0, 0))
         state[128 * g : 128 * g + 64, :] = a
         state[128 * g + 64 : 128 * g + 128, :] = b
-
-
-def query_back_body(
-    scale, pos, x_own, x_other, g_own, g_other, qo, qp, qf, oo, op, of, qs,
-    query, back, term, wq, wo, sems,
-):
-    copies = place(pos, qo, qp, qf, wq, sems, (1, 2), 0)
-    copies += place(pos, oo, op, of, wo, sems, (2, 1), 13)
-    for one in copies:
-        one.start()
-    for one in copies:
-        one.wait()
+    wait(stores)
+
+
+def query_back_body(scale, pos, x_own, x_other, g_own, g_other, qs, *refs):
+    q, o = refs[0:7], refs[7:14]
+    query, back, term, wq, wo, sems = refs[14:]
+    fetch_q = place(pos, q[0], q[1:], wq, sems, 2, 0)
+    fetch_o = place(pos, o[0], o[1:], wo, sems, 3, 10, True)
     half = x_own.shape[0]
+    wait(fetch_q)
     for n, rows in enumerate((x_own, x_other)):
         for t in range(0, half, 256):
             at = slice(n * half + t, n * half + t + 256)
             query[at, :] = (dot(rows[t : t + 256, :], wq[...], 1, 0) * qs[...]).astype(BF16)
+    wait(fetch_o)
     for n, cols in enumerate((g_own, g_other)):
         for t in range(0, half, 256):
             at = slice(n * half + t, n * half + t + 256)
@@ -175,15 +208,19 @@
         term[128 * g + 64 : 128 * g + 128, :] = b
 
 
-def middle_body(
-    scale, query, back, state, wq, wo, qs, out_own, out_other, in_own, in_other, diag, att, qb
-):
+def middle_body(scale, pos, query, back, state, qs, *refs):
+    q, o = refs[0:7], refs[7:14]
+    out_own, out_other, in_own, in_other, diag, att, qb, wq, wo, sems = refs[14:]
+    fetch_o = place(pos, o[0], o[1:], wo, sems, 3, 10, True)
+    fetch_q = place(pos, q[0], q[1:], wq, sems, 2, 0)
     half = out_own.shape[0]
     for g in range(2):
         part = slice(256 * g, 256 * g + 256)
         unpack(scale * state[128 * g : 128 * g + 128, :], diag)
         att[:, part] = dot(query[:, part], diag[...], 1, 0).astype(BF16)
         qb[part, :] = (dot(diag[...], back[part, :], 1, 0) * qs[part, :]).astype(BF16)
+    wait(fetch_o)
+    wait(fetch_q)
     for n, (out, inp) in enumerate(((out_own, in_own), (out_other, in_other))):
         for t in range(0, half, 256):
             at = slice(n * half + t, n * half + t + 256)
@@ -191,13 +228,18 @@
             inp[:, t : t + 256] = dot(wq[...], qb[:, at], 1, 0)
 
 
-def tail_body(key, value, term, wk, wv, ks, vs, in_own, in_other, res_own, res_other, diag, kb, vb):
+def tail_body(pos, key, value, term, ks, vs, in_own, in_other, *refs):
+    k, v = refs[0:7], refs[7:14]
+    res_own, res_other, diag, kb, vb, wk, wv, sems = refs[14:]
+    fetch = place(pos, k[0], k[1:], wk, sems, 2, 0)
+    fetch += place(pos, v[0], v[1:], wv, sems, 3, 10)
     half = in_own.shape[1]
     for g in range(2):
         part = slice(256 * g, 256 * g + 256)
         unpack(term[128 * g : 128 * g + 128, :], diag)
         kb[:, part] = (dot(value[:, part], diag[...], 1, 0) * ks[:, part]).astype(BF16)
         vb[:, part] = (dot(key[:, part], diag[...], 1, 1) * vs[:, part]).astype(BF16)
+    wait(fetch)
     for n, (inp, res) in enumerate(((in_own, res_own), (in_other, res_other))):
         for t in range(0, half, 256):
             at = slice(n * half + t, n * half + t + 256)
@@ -224,58 +266,54 @@
     width, tokens = features.shape
     mine = width // 2
     both = 2 * tokens
-    quarter = 2 * y + x
     slots = active_blocks.shape[1] * BLOCK
     scale = 1.0 / math.sqrt(HEAD_DIM * slots * lax.axis_size(REDUCE_AXES))
-    pos = jnp.stack([z, quarter]).astype(jnp.int32)
-
-    def columns(shard):
-        split = shard.reshape(shard.shape[0], 4, 2, 128)
-        return lax.dynamic_index_in_dim(split, c, 2, keepdims=False).reshape(-1, mine)
-
-    def own_piece(own):
-        rows = own.shape[0] // 4
-        return lax.dynamic_slice_in_dim(own, quarter * rows, rows, 0)
+    pos = jnp.stack([z, c, x, y]).astype(jnp.int32)
 
     def own_scale(v):
         return lax.dynamic_index_in_dim(v.reshape(4, 2, 128), c, 1, keepdims=False).reshape(mine)
 
-    k_own, v_own, q_own = columns(key_weight), columns(value_weight), columns(query_weight)
-    o_own = lax.dynamic_slice_in_dim(out_weight, c * 128, 128, 0)
-    k_pair, k_far = spread(around(own_piece(k_own)), swap_x, swap_y)
-    v_pair, v_far = spread(around(own_piece(v_own)), swap_y, swap_x)
-    q_pair, q_far = spread(around(own_piece(q_own)), swap_x, swap_y)
-    o_pair, o_far = spread(around(own_piece(o_own)), swap_y, swap_x)
-
-    live = jnp.arange(active_blocks.shape[1], dtype=jnp.int32) < active_count[0]
-    named = jnp.where(live, active_blocks[0], -1)
-    block_of = jnp.arange(tokens, dtype=jnp.int32) // BLOCK
-    mask = jnp.any(named[:, None] == block_of[None, :], axis=0)
-    zero = jnp.zeros((), BF16)
-    x_own = jnp.where(mask[:, None], features.T, zero)
-    g_own = (grad_out.astype(F32) * out_scale[:, None]).astype(BF16)
-    g_own = jnp.where(mask[None, :], g_own, zero)
+    half = query_weight.shape[0] // 2
+    q_half, k_half, v_half, o_half = call(
+        send_body,
+        [shape((half, mine))] * 3 + [shape((half // 2, width))],
+        [SMEM] + [ANY] * 4,
+        (pos, query_weight, key_weight, value_weight, out_weight),
+        (pltpu.SemaphoreType.DMA((13,)),),
+        out_specs=(ANY,) * 4,
+    )
+    k = (key_weight,) + pieces(k_half, swap_x)
+    v = (value_weight,) + pieces(v_half, swap_y)
+    q = (query_weight,) + pieces(q_half, swap_x)
+    o = (out_weight,) + pieces(o_half, swap_y)
+    x_own, g_own = call(
+        mask_body,
+        [shape((tokens, width)), shape((width, tokens))],
+        [SMEM, SMEM] + [VMEM] * 3,
+        (active_blocks, active_count, features, grad_out, out_scale[:, None]),
+        limit=24 << 20,
+    )
     x_other, g_other = swap_core(x_own), swap_core(g_own)
 
     ks, vs, qs = own_scale(key_scale), own_scale(value_scale), own_scale(query_scale)
-    sems = (pltpu.SemaphoreType.DMA((26,)),)
+    sems = pltpu.SemaphoreType.DMA((22,))
+    tall, wide = pltpu.VMEM((width, mine), BF16), pltpu.VMEM((mine, width), BF16)
+    kept = pltpu.VMEM((both, mine), BF16)
     ff = 2 * both * width * mine
-    key, value, state, wk, wv = call(
+    key, value, state = call(
         key_value_body,
-        [shape((both, mine)), shape((both, mine)), shape((256, 128), F32),
-         shape((width, mine)), shape((width, mine))],
-        [SMEM, VMEM, VMEM] + [ANY] * 6 + [VMEM] * 2,
-        (pos, x_own, x_other, k_own, k_pair, k_far, v_own, v_pair, v_far, ks[None], vs[None]),
-        sems, 2 * ff, 24 << 20,
+        [shape((both, mine)), shape((both, mine)), shape((256, 128), F32)],
+        [SMEM] + [VMEM] * 4 + [ANY] * 14,
+        (pos, x_own, x_other, ks[None], vs[None], *k, *v),
+        (kept, kept, tall, tall, sems), 2 * ff, 24 << 20, (ANY, ANY, VMEM),
     )
     state = sum_over_chips(state)
-    query, back, term, wq, wo = call(
+    query, back, term = call(
         functools.partial(query_back_body, scale),
-        [shape((both, mine)), shape((mine, both)), shape((256, 128), F32),
-         shape((width, mine)), shape((mine, width))],
-        [SMEM] + [VMEM] * 4 + [ANY] * 6 + [VMEM],
-        (pos, x_own, x_other, g_own, g_other, q_own, q_pair, q_far, o_own, o_pair, o_far, qs[None]),
-        sems, 2 * ff, 24 << 20,
+        [shape((both, mine)), shape((mine, both)), shape((256, 128), F32)],
+        [SMEM] + [VMEM] * 5 + [ANY] * 14,
+        (pos, x_own, x_other, g_own, g_other, qs[None], *q, *o),
+        (tall, wide, sems), 2 * ff, 24 << 20,
     )
     term = sum_over_chips(term)
     diag = pltpu.VMEM((256, 256), BF16)
@@ -283,20 +321,18 @@
         functools.partial(middle_body, scale),
         [shape((tokens, width), F32), shape((tokens, width)),
          shape((width, tokens), F32), shape((width, tokens), F32)],
-        [VMEM] * 6,
-        (query, back, state, wq, wo, qs[:, None]),
-        (diag, pltpu.VMEM((both, mine), BF16), pltpu.VMEM((mine, both), BF16)),
-        2 * ff, 32 << 20,
+        [SMEM] + [VMEM] * 4 + [ANY] * 14,
+        (pos, query, back, state, qs[:, None], *q, *o),
+        (diag, kept, pltpu.VMEM((mine, both), BF16), tall, wide, sems), 2 * ff, 32 << 20,
     )
     out_sum = out_own + swap_core(out_other).astype(F32)
     attention_out = (out_sum * out_scale[None, :]).astype(BF16).T
     res_own, res_other = call(
         tail_body,
         [shape((width, tokens), F32), shape((width, tokens))],
-        [VMEM] * 9,
-        (key, value, term, wk, wv, ks[None], vs[None], in_own, in_other),
-        (diag, pltpu.VMEM((both, mine), BF16), pltpu.VMEM((both, mine), BF16)),
-        2 * ff, 32 << 20,
+        [SMEM] + [VMEM] * 7 + [ANY] * 14,
+        (pos, key, value, term, ks[None], vs[None], in_own, in_other, *k, *v),
+        (diag, kept, kept, tall, tall, sems), 2 * ff, 32 << 20,
     )
     input_grad = (res_own + swap_core(res_other).astype(F32)).astype(BF16)
     return attention_out, input_grad

time: 131 us -> 147 us (1.12)
  Pallas kernels: 17.7 us -> 48.5 us
  local copies, waits for them, and re-layouts: 37 us -> 6.91 us
  starting transfers between devices: 39.6 us -> 68.9 us
  waiting for transfers between devices: 25 us -> 16.8 us
  other arithmetic: 8.69 us -> 3.71 us
    ppermute x12 -> x18, starting transfers between devices: 20.4 us -> 51.9 us  [turn_z(): return lax.ppermute(a, 'space', [(i, (i + step) % 4) for i in range(4)])]
    pallas_call x4 -> x6, Pallas kernels: 17.7 us -> 48.5 us  [call(): pl.pallas_call(body, out_shape=tuple(outs), in_specs=in_specs, out_specs=...]
    unnamed x64 -> x69, local copies, waits for them, and re-layouts: 20.6 us -> 5.84 us
    ppermute x6 -> x8, waiting for transfers between devices: 14 us -> 4.58 us  [swap_x(): return lax.ppermute(a, 'tm', [(0, 1), (1, 0)])]
    dynamic_slice x7 -> x0, local copies, waits for them, and re-layouts: 8.15 us -> none  [the longest x2 4.89 us: columns(): lax.dynamic_index_in_dim(split, c, 2, keepdims=False).reshape(-1, mine)]
    ppermute x4 -> x0, starting transfers between devices: 6.2 us -> none  [swap_z(): return lax.ppermute(a, 'space', [(i, i ^ bit) for i in range(4)])]
    ppermute x4 -> x6, waiting for transfers between devices: 0.8 us -> 3.71 us  [swap_y(): return lax.ppermute(a, 'groups', [(0, 1), (1, 0)])]
    select_n x3 -> x0, other arithmetic: 2.64 us -> none  [the longest x1 2.63 us: per_device_split(): g_own = jnp.where(mask[None, :], g_own, zero)]
  transfers between devices with their start and end apart: 30 -> 36, of which waited for: 11 -> 11; matrix products, arithmetic and copies ran while one was open for 27% -> 2% of each run, Pallas kernels for 14% -> 32%
where the time goes in v2:
time: 147 us
  starting transfers between devices  68.9 us (47%)
  Pallas kernels  48.5 us (33%)
  waiting for transfers between devices  16.8 us (11%)
  local copies, waits for them, and re-layouts  6.91 us (5%)
  other arithmetic  3.71 us (3%)
  between operations  1.8 us (1%)
    ppermute x18, starting transfers between devices, turn_z(): return lax.ppermute(a, 'space', [(i, (i + step) % 4) for i in range(4)])  51.9 us
    pallas_call x6, Pallas kernels, call(): pl.pallas_call(body, out_shape=tuple(outs), in_specs=in_specs, out_specs=...  48.5 us
    ppermute x8, starting transfers between devices, swap_x(): return lax.ppermute(a, 'tm', [(0, 1), (1, 0)])  9.49 us
    ppermute x18, waiting for transfers between devices, turn_z(): return lax.ppermute(a, 'space', [(i, (i + step) % 4) for i in range(4)])  7.58 us
    ppermute x6, starting transfers between devices, swap_y(): return lax.ppermute(a, 'groups', [(0, 1), (1, 0)])  6.39 us
    unnamed x69, local copies, waits for them, and re-layouts  5.84 us
    ppermute x8, waiting for transfers between devices, swap_x(): return lax.ppermute(a, 'tm', [(0, 1), (1, 0)])  4.58 us
    ppermute x6, waiting for transfers between devices, swap_y(): return lax.ppermute(a, 'groups', [(0, 1), (1, 0)])  3.71 us
  transfers between devices with their start and end apart: 36, of which 11 were waited for; matrix products, arithmetic and copies ran while one was open for 2% of the time, Pallas kernels for 32%

profile of v2, /device:TPU:0, one launch (start us, length us, event | category | flops | bytes accessed | tf_op | source)
XLA Modules:
  0.0 146.6 jit_solution(9802113714181520788)
XLA Ops:
  1.3 0.9 copy.15.scale
  2.2 1.2 copy-done.2
  3.4 1.2 copy-done.3
  4.6 0.7 copy-done.25
  5.3 2.2 %shard_map.131 = (bf16[512,1024]{1,0:T(8,128)(2,1)}, bf16[1024,512]{1,0:T(8,128)(2,1)}) custom-call(s32[1,6]{1,0:T(1,128)S(1)} %copy-done.25, s32[1]{0:T(128)S(6)} %copy.18.count, bf16[1024,512]{1,0:T(8,128)(2,1)S(1)} %copy-done.2, bf16[1024,512]{1,0:T(8,128)(2,1)S(1)} %copy-done.3, f32[1024,1]{1,0:T(8,128)S(1)} %copy.15.scale), custom_call_target="tpu_custom_call" | custom-call | bytes 4198428 | tf_op jit(solution)/shard_map/pallas_call | solution.py:31
  8.7 17.9 %shard_map.132 = (bf16[128,512]{1,0:T(8,128)(2,1)}, bf16[128,512]{1,0:T(8,128)(2,1)}, bf16[128,512]{1,0:T(8,128)(2,1)}, bf16[64,1024]{1,0:T(8,128)(2,1)}) custom-call(s32[4]{0:T(128)} %pad_add_fusion.pos, bf16[256,1024]{1,0:T(8,128)(2,1)} %refs_0_.6, bf16[256,1024]{1,0:T(8,128)(2,1)} %refs_0_.7, bf16[256,1024]{1,0:T(8,128)(2,1)} %refs_7_.7, ...), custom_call_target="tpu_custom_call" | custom-call | bytes 2621456 | tf_op jit(solution)/shard_map/pallas_call | solution.py:31
  26.6 3.7 %collective-permute-start.4 = (bf16[128,512]{1,0:T(8,128)(2,1)}, bf16[128,512]{1,0:T(8,128)(2,1)S(1)}, u32[]{:S(2)}, u32[]{:S(2)}) collective-permute-start(bf16[128,512]{1,0:T(8,128)(2,1)} %get-tuple-element.22), channel_id=1, source_target_pairs={{0,8},{4,12},{8,0},{12,4},{1,9},{5,13},{9,1},{13,5},{2,10},{6,14},... | collective-permute-start | bytes 393224 | tf_op jit(solution)/shard_map/ppermute | solution.py:59
  30.2 1.3 collective-permute-start.3
  31.6 0.7 collective-permute-start.2
  32.2 1.0 collective-permute-start.10
  33.2 4.4 %collective-permute-done.4.refs_3_ = bf16[128,512]{1,0:T(8,128)(2,1)S(1)} collective-permute-done((bf16[128,512]{1,0:T(8,128)(2,1)}, bf16[128,512]{1,0:T(8,128)(2,1)S(1)}, u32[]{:S(2)}, u32[]{:S(2)}) %collective-permute-start.4) | collective-permute-done | bytes 131104 | tf_op jit(solution)/shard_map/ppermute | solution.py:59
  37.6 6.6 %collective-permute-start.9 = (bf16[64,1024]{1,0:T(8,128)(2,1)}, bf16[64,1024]{1,0:T(8,128)(2,1)}, u32[]{:S(2)}, u32[]{:S(2)}) collective-permute-start(bf16[64,1024]{1,0:T(8,128)(2,1)} %get-tuple-element.23), channel_id=1, source_target_pairs={{0,12},{4,0},{8,4},{12,8},{1,13},{5,1},{9,5},{13,9},{2,14},{6,2},{... | collective-permute-start | bytes 393224 | tf_op jit(solution)/shard_map/ppermute | solution.py:59
  44.2 5.3 %collective-permute-start.8 = (bf16[64,1024]{1,0:T(8,128)(2,1)}, bf16[64,1024]{1,0:T(8,128)(2,1)}, u32[]{:S(2)}, u32[]{:S(2)}) collective-permute-start(bf16[64,1024]{1,0:T(8,128)(2,1)} %get-tuple-element.23), channel_id=1, source_target_pairs={{0,4},{4,8},{8,12},{12,0},{1,5},{5,9},{9,13},{13,1},{2,6},{6,10},{... | collective-permute-start | bytes 393224 | tf_op jit(solution)/shard_map/ppermute | solution.py:59
  49.5 1.8 %collective-permute-start.16 = (bf16[128,512]{1,0:T(8,128)(2,1)}, bf16[128,512]{1,0:T(8,128)(2,1)S(1)}, u32[]{:S(2)}, u32[]{:S(2)}) collective-permute-start(bf16[128,512]{1,0:T(8,128)(2,1)} %get-tuple-element.26), channel_id=1, source_target_pairs={{0,8},{4,12},{8,0},{12,4},{1,9},{5,13},{9,1},{13,5},{2,10},{6,14},... | collective-permute-start | bytes 393224 | tf_op jit(solution)/shard_map/ppermute | solution.py:59
  51.4 3.8 %collective-permute-start.15 = (bf16[128,512]{1,0:T(8,128)(2,1)}, bf16[128,512]{1,0:T(8,128)(2,1)S(1)}, u32[]{:S(2)}, u32[]{:S(2)}) collective-permute-start(bf16[128,512]{1,0:T(8,128)(2,1)} %get-tuple-element.26), channel_id=1, source_target_pairs={{0,12},{4,0},{8,4},{12,8},{1,13},{5,1},{9,5},{13,9},{2,14},{6,2},{... | collective-permute-start | bytes 393224 | tf_op jit(solution)/shard_map/ppermute | solution.py:59
  55.1 6.6 %collective-permute-start.14 = (bf16[128,512]{1,0:T(8,128)(2,1)}, bf16[128,512]{1,0:T(8,128)(2,1)S(1)}, u32[]{:S(2)}, u32[]{:S(2)}) collective-permute-start(bf16[128,512]{1,0:T(8,128)(2,1)} %get-tuple-element.26), channel_id=1, source_target_pairs={{0,4},{4,8},{8,12},{12,0},{1,5},{5,9},{9,13},{13,1},{2,6},{6,10},{... | collective-permute-start | bytes 393224 | tf_op jit(solution)/shard_map/ppermute | solution.py:59
  61.7 1.9 %collective-permute-start.22 = (bf16[128,512]{1,0:T(8,128)(2,1)}, bf16[128,512]{1,0:T(8,128)(2,1)S(1)}, u32[]{:S(2)}, u32[]{:S(2)}) collective-permute-start(bf16[128,512]{1,0:T(8,128)(2,1)} %get-tuple-element.27), channel_id=1, source_target_pairs={{0,8},{4,12},{8,0},{12,4},{1,9},{5,13},{9,1},{13,5},{2,10},{6,14},... | collective-permute-start | bytes 393224 | tf_op jit(solution)/shard_map/ppermute | solution.py:59
  63.6 5.1 %collective-permute-start.21 = (bf16[128,512]{1,0:T(8,128)(2,1)}, bf16[128,512]{1,0:T(8,128)(2,1)S(1)}, u32[]{:S(2)}, u32[]{:S(2)}) collective-permute-start(bf16[128,512]{1,0:T(8,128)(2,1)} %get-tuple-element.27), channel_id=1, source_target_pairs={{0,12},{4,0},{8,4},{12,8},{1,13},{5,1},{9,5},{13,9},{2,14},{6,2},{... | collective-permute-start | bytes 393224 | tf_op jit(solution)/shard_map/ppermute | solution.py:59
  68.7 3.1 %collective-permute-start.20 = (bf16[128,512]{1,0:T(8,128)(2,1)}, bf16[128,512]{1,0:T(8,128)(2,1)S(1)}, u32[]{:S(2)}, u32[]{:S(2)}) collective-permute-start(bf16[128,512]{1,0:T(8,128)(2,1)} %get-tuple-element.27), channel_id=1, source_target_pairs={{0,4},{4,8},{8,12},{12,0},{1,5},{5,9},{9,13},{13,1},{2,6},{6,10},{... | collective-permute-start | bytes 393224 | tf_op jit(solution)/shard_map/ppermute | solution.py:59
  71.8 1.7 %collective-permute-done.22.refs_10_ = bf16[128,512]{1,0:T(8,128)(2,1)S(1)} collective-permute-done((bf16[128,512]{1,0:T(8,128)(2,1)}, bf16[128,512]{1,0:T(8,128)(2,1)S(1)}, u32[]{:S(2)}, u32[]{:S(2)}) %collective-permute-start.22) | collective-permute-done | bytes 131104 | tf_op jit(solution)/shard_map/ppermute | solution.py:59
  73.5 1.5 %collective-permute-start.7 = (bf16[128,512]{1,0:T(8,128)(2,1)S(1)}, bf16[128,512]{1,0:T(8,128)(2,1)S(1)}, u32[]{:S(2)}, u32[]{:S(2)}) collective-permute-start(bf16[128,512]{1,0:T(8,128)(2,1)S(1)} %collective-permute-done.4.refs_3_), channel_id=1, source_target_pairs={{0,2},{2,0},{1,3},{3,1},{4,6},{6,4},{5,7},{7,5},{8,10},{10,8},{9,1... | collective-permute-start | bytes 393224 | tf_op jit(solution)/shard_map/ppermute | solution.py:47
  75.8 1.5 %collective-permute-start.19 = (bf16[128,512]{1,0:T(8,128)(2,1)S(1)}, bf16[128,512]{1,0:T(8,128)(2,1)S(1)}, u32[]{:S(2)}, u32[]{:S(2)}) collective-permute-start(bf16[128,512]{1,0:T(8,128)(2,1)S(1)} %collective-permute-done.16.refs_3_), channel_id=1, source_target_pairs={{0,2},{2,0},{1,3},{3,1},{4,6},{6,4},{5,7},{7,5},{8,10},{10,8},{9,1... | collective-permute-start | bytes 393224 | tf_op jit(solution)/shard_map/ppermute | solution.py:47
  77.3 2.5 %collective-permute-done.7.refs_6_ = bf16[128,512]{1,0:T(8,128)(2,1)S(1)} collective-permute-done((bf16[128,512]{1,0:T(8,128)(2,1)S(1)}, bf16[128,512]{1,0:T(8,128)(2,1)S(1)}, u32[]{:S(2)}, u32[]{:S(2)}) %collective-permute-start.7) | collective-permute-done | bytes 131104 | tf_op jit(solution)/shard_map/ppermute | solution.py:47
  80.4 1.5 %collective-permute-start.18 = (bf16[128,512]{1,0:T(8,128)(2,1)S(1)}, bf16[128,512]{1,0:T(8,128)(2,1)S(1)}, u32[]{:S(2)}, u32[]{:S(2)}) collective-permute-start(bf16[128,512]{1,0:T(8,128)(2,1)S(1)} %collective-permute-done.15.refs_2_), channel_id=1, source_target_pairs={{0,2},{2,0},{1,3},{3,1},{4,6},{6,4},{5,7},{7,5},{8,10},{10,8},{9,1... | collective-permute-start | bytes 393224 | tf_op jit(solution)/shard_map/ppermute | solution.py:47
  82.9 1.3 collective-permute-start.17
  84.2 1.5 %collective-permute-start.25 = (bf16[128,512]{1,0:T(8,128)(2,1)S(1)}, bf16[128,512]{1,0:T(8,128)(2,1)S(1)}, u32[]{:S(2)}, u32[]{:S(2)}) collective-permute-start(bf16[128,512]{1,0:T(8,128)(2,1)S(1)} %collective-permute-done.22.refs_10_), channel_id=1, source_target_pairs={{0,16},{16,0},{1,17},{17,1},{2,18},{18,2},{3,19},{19,3},{4,20},{20... | collective-permute-start | bytes 393224 | tf_op jit(solution)/shard_map/ppermute | solution.py:51
  85.7 1.5 %collective-permute-start.24 = (bf16[128,512]{1,0:T(8,128)(2,1)S(1)}, bf16[128,512]{1,0:T(8,128)(2,1)S(1)}, u32[]{:S(2)}, u32[]{:S(2)}) collective-permute-start(bf16[128,512]{1,0:T(8,128)(2,1)S(1)} %collective-permute-done.21.refs_9_), channel_id=1, source_target_pairs={{0,16},{16,0},{1,17},{17,1},{2,18},{18,2},{3,19},{19,3},{4,20},{20... | collective-permute-start | bytes 393224 | tf_op jit(solution)/shard_map/ppermute | solution.py:51
  87.2 1.8 %collective-permute-done.17.refs_4_ = bf16[128,512]{1,0:T(8,128)(2,1)S(1)} collective-permute-done((bf16[128,512]{1,0:T(8,128)(2,1)S(1)}, bf16[128,512]{1,0:T(8,128)(2,1)S(1)}, u32[]{:S(2)}, u32[]{:S(2)}) %collective-permute-start.17) | collective-permute-done | bytes 131104 | tf_op jit(solution)/shard_map/ppermute | solution.py:47
  89.0 0.8 collective-permute-start.23
  90.5 1.0 collective-permute-start.5
  91.5 1.8 %collective-permute-done.24.refs_12_ = bf16[128,512]{1,0:T(8,128)(2,1)S(1)} collective-permute-done((bf16[128,512]{1,0:T(8,128)(2,1)S(1)}, bf16[128,512]{1,0:T(8,128)(2,1)S(1)}, u32[]{:S(2)}, u32[]{:S(2)}) %collective-permute-start.24) | collective-permute-done | bytes 131104 | tf_op jit(solution)/shard_map/ppermute | solution.py:51
  93.9 1.3 collective-permute-done.23.refs_11_
  95.3 1.0 collective-permute-start.12
  96.2 1.0 collective-permute-start.11
  97.3 7.5 %shard_map.134 = (bf16[1024,512]{1,0:T(8,128)(2,1)S(1)}, bf16[1024,512]{1,0:T(8,128)(2,1)S(1)}, f32[256,128]{1,0:T(8,128)S(1)}) custom-call(s32[4]{0:T(128)S(1)} %copy-done.24, bf16[512,1024]{1,0:T(8,128)(2,1)} %get-tuple-element.20.x_own, bf16[512,1024]{1,0:T(8,128)(2,1)} %collective-permute-done.x_other, f32[1,512]{1,0:T(1,128)S(1)} %get-tuple-element.45.ks, ...), custom_call_target="tpu_custom_call" | custom-call | flops 2147483648 | bytes 6950928 | tf_op jit(solution)/shard_map/pallas_call | solution.py:31
  104.9 1.1 collective-permute-start.26
  106.1 7.2 %shard_map.133 = (bf16[1024,512]{1,0:T(8,128)(2,1)S(1)}, bf16[512,1024]{1,0:T(8,128)(2,1)S(1)}, f32[256,128]{1,0:T(8,128)S(1)}) custom-call(s32[4]{0:T(128)S(1)} %copy-done.24, bf16[512,1024]{1,0:T(8,128)(2,1)} %get-tuple-element.20.x_own, bf16[512,1024]{1,0:T(8,128)(2,1)} %collective-permute-done.x_other, bf16[1024,512]{1,0:T(8,128)(2,1)} %get-tuple-element.21.g_own, ...), custom_call_target="tpu_custom_call" | custom-call | flops 2147483648 | bytes 9046032 | tf_op jit(solution)/shard_map/pallas_call | solution.py:31
  113.3 1.0 collective-permute-start.31
  114.4 2.4 %collective-permute-start.29 = (bf16[256,128]{1,0:T(8,128)(2,1)S(1)}, bf16[256,128]{1,0:T(8,128)(2,1)S(1)}, u32[]{:S(2)}, u32[]{:S(2)}) collective-permute-start(bf16[256,128]{1,0:T(8,128)(2,1)S(1)} %fusion.1), channel_id=1, source_target_pairs={{0,8},{4,12},{8,0},{12,4},{1,9},{5,13},{9,1},{13,5},{2,10},{6,14},... | collective-permute-start | bytes 196616 | tf_op jit(solution)/shard_map/ppermute | solution.py:59
  116.7 3.8 %collective-permute-start.28 = (bf16[256,128]{1,0:T(8,128)(2,1)S(1)}, bf16[256,128]{1,0:T(8,128)(2,1)S(1)}, u32[]{:S(2)}, u32[]{:S(2)}) collective-permute-start(bf16[256,128]{1,0:T(8,128)(2,1)S(1)} %fusion.1), channel_id=1, source_target_pairs={{0,12},{4,0},{8,4},{12,8},{1,13},{5,1},{9,5},{13,9},{2,14},{6,2},{... | collective-permute-start | bytes 196616 | tf_op jit(solution)/shard_map/ppermute | solution.py:59
  121.1 1.5 %collective-permute-start.34 = (bf16[256,128]{1,0:T(8,128)(2,1)S(1)}, bf16[256,128]{1,0:T(8,128)(2,1)S(1)}, u32[]{:S(2)}, u32[]{:S(2)}) collective-permute-start(bf16[256,128]{1,0:T(8,128)(2,1)S(1)} %fusion.2), channel_id=1, source_target_pairs={{0,8},{4,12},{8,0},{12,4},{1,9},{5,13},{9,1},{13,5},{2,10},{6,14},... | collective-permute-start | bytes 196616 | tf_op jit(solution)/shard_map/ppermute | solution.py:59
  122.6 2.9 %collective-permute-start.33 = (bf16[256,128]{1,0:T(8,128)(2,1)S(1)}, bf16[256,128]{1,0:T(8,128)(2,1)S(1)}, u32[]{:S(2)}, u32[]{:S(2)}) collective-permute-start(bf16[256,128]{1,0:T(8,128)(2,1)S(1)} %fusion.2), channel_id=1, source_target_pairs={{0,12},{4,0},{8,4},{12,8},{1,13},{5,1},{9,5},{13,9},{2,14},{6,2},{... | collective-permute-start | bytes 196616 | tf_op jit(solution)/shard_map/ppermute | solution.py:59
  125.5 1.2 collective-permute-done.27
  126.8 6.4 %shard_map.135 = (f32[512,1024]{1,0:T(8,128)S(1)}, bf16[512,1024]{1,0:T(8,128)(2,1)S(1)}, f32[1024,512]{1,0:T(8,128)S(1)}, f32[1024,512]{1,0:T(8,128)S(1)}) custom-call(s32[4]{0:T(128)S(1)} %copy-done.24, bf16[1024,512]{1,0:T(8,128)(2,1)S(1)} %get-tuple-element.24.query, bf16[512,1024]{1,0:T(8,128)(2,1)S(1)} %get-tuple-element.25.back, ...), custom_call_target="tpu_custom_call" | custom-call | flops 2147483648 | bytes 12191760 | tf_op jit(solution)/shard_map/pallas_call | solution.py:31
  133.5 7.3 %shard_map.136 = (f32[1024,512]{1,0:T(8,128)S(1)}, bf16[1024,512]{1,0:T(8,128)(2,1)}) custom-call(s32[4]{0:T(128)S(1)} %copy-done.24, bf16[1024,512]{1,0:T(8,128)(2,1)S(1)} %get-tuple-element.31.key, bf16[1024,512]{1,0:T(8,128)(2,1)S(1)} %get-tuple-element.32.value, f32[256,128]{1,0:T(8,128)S(1)} %convert_add_fusion.term, ...), custom_call_target="tpu_custom_call" | custom-call | flops 2147483648 | bytes 12193808 | tf_op jit(solution)/shard_map/pallas_call | solution.py:31
  141.8 1.3 copy.17
  143.1 0.9 collective-permute-done.35
  144.0 2.5 %add_convert_fusion = bf16[1024,512]{1,0:T(8,128)(2,1)} fusion(f32[1024,512]{1,0:T(8,128)S(1)} %get-tuple-element.36, bf16[1024,512]{1,0:T(8,128)(2,1)} %collective-permute-done.35), kind=kLoop, calls=%fused_computation | loop fusion | flops 1572864 | bytes 4194304 | tf_op jit(solution)/shard_map/convert_element_type | solution.py:337
  (112 shorter events, 6.6 us)
Async XLA Ops:
  5.3 84.4 %copy-start.33 = (f32[1024]{0:T(1024)S(1)}, f32[1024]{0:T(1024)}, u32[]{:S(2)}) copy-start(f32[1024]{0:T(1024)} %param.18) | copy-start | bytes 12292
  5.3 84.6 %copy-start.31 = (f32[1024]{0:T(1024)S(1)}, f32[1024]{0:T(1024)}, u32[]{:S(2)}) copy-start(f32[1024]{0:T(1024)} %param.20) | copy-start | bytes 12292
  5.3 84.6 %copy-start.32 = (f32[1024]{0:T(1024)S(1)}, f32[1024]{0:T(1024)}, u32[]{:S(2)}) copy-start(f32[1024]{0:T(1024)} %param.19) | copy-start | bytes 12292
  5.3 92.0 %copy-start = (bf16[256,1024]{1,0:T(8,128)(2,1)S(1)}, bf16[256,1024]{1,0:T(8,128)(2,1)}, u32[]{:S(2)}) copy-start(bf16[256,1024]{1,0:T(8,128)(2,1)} %refs_0_.7) | copy-start | bytes 1572868
  5.3 92.0 %copy-start.1 = (bf16[256,1024]{1,0:T(8,128)(2,1)S(1)}, bf16[256,1024]{1,0:T(8,128)(2,1)}, u32[]{:S(2)}) copy-start(bf16[256,1024]{1,0:T(8,128)(2,1)} %refs_7_.7) | copy-start | bytes 1572868
  7.6 88.7 %collective-permute-start = (bf16[512,1024]{1,0:T(8,128)(2,1)}, bf16[512,1024]{1,0:T(8,128)(2,1)}, u32[]{:S(2)}, u32[]{:S(2)}) collective-permute-start(bf16[512,1024]{1,0:T(8,128)(2,1)} %get-tuple-element.20.x_own), channel_id=1, source_target_pairs={{0,1},{1,0},{2,3},{3,2},{4,5},{5,4},{6,7},{7,6},{8,9},{9,8},{10,11... | collective-permute-start | bytes 3145736 | tf_op jit(solution)/shard_map/ppermute | solution.py:55
  8.6 88.6 %copy-start.24 = (s32[4]{0:T(128)S(1)}, s32[4]{0:T(128)}, u32[]{:S(2)}) copy-start(s32[4]{0:T(128)} %pad_add_fusion.pos) | copy-start | bytes 52
  26.6 11.1 %collective-permute-start.4 = (bf16[128,512]{1,0:T(8,128)(2,1)}, bf16[128,512]{1,0:T(8,128)(2,1)S(1)}, u32[]{:S(2)}, u32[]{:S(2)}) collective-permute-start(bf16[128,512]{1,0:T(8,128)(2,1)} %get-tuple-element.22), channel_id=1, source_target_pairs={{0,8},{4,12},{8,0},{12,4},{1,9},{5,13},{9,1},{13,5},{2,10},{6,14},... | collective-permute-start | bytes 393224 | tf_op jit(solution)/shard_map/ppermute | solution.py:59
  30.2 14.0 %collective-permute-start.3 = (bf16[128,512]{1,0:T(8,128)(2,1)}, bf16[128,512]{1,0:T(8,128)(2,1)S(1)}, u32[]{:S(2)}, u32[]{:S(2)}) collective-permute-start(bf16[128,512]{1,0:T(8,128)(2,1)} %get-tuple-element.22), channel_id=1, source_target_pairs={{0,12},{4,0},{8,4},{12,8},{1,13},{5,1},{9,5},{13,9},{2,14},{6,2},{... | collective-permute-start | bytes 393224 | tf_op jit(solution)/shard_map/ppermute | solution.py:59
  31.6 12.7 %collective-permute-start.2 = (bf16[128,512]{1,0:T(8,128)(2,1)}, bf16[128,512]{1,0:T(8,128)(2,1)S(1)}, u32[]{:S(2)}, u32[]{:S(2)}) collective-permute-start(bf16[128,512]{1,0:T(8,128)(2,1)} %get-tuple-element.22), channel_id=1, source_target_pairs={{0,4},{4,8},{8,12},{12,0},{1,5},{5,9},{9,13},{13,1},{2,6},{6,10},{... | collective-permute-start | bytes 393224 | tf_op jit(solution)/shard_map/ppermute | solution.py:59
  32.2 17.3 %collective-permute-start.10 = (bf16[64,1024]{1,0:T(8,128)(2,1)}, bf16[64,1024]{1,0:T(8,128)(2,1)S(1)}, u32[]{:S(2)}, u32[]{:S(2)}) collective-permute-start(bf16[64,1024]{1,0:T(8,128)(2,1)} %get-tuple-element.23), channel_id=1, source_target_pairs={{0,8},{4,12},{8,0},{12,4},{1,9},{5,13},{9,1},{13,5},{2,10},{6,14},... | collective-permute-start | bytes 393224 | tf_op jit(solution)/shard_map/ppermute | solution.py:59
  37.6 13.7 %collective-permute-start.9 = (bf16[64,1024]{1,0:T(8,128)(2,1)}, bf16[64,1024]{1,0:T(8,128)(2,1)}, u32[]{:S(2)}, u32[]{:S(2)}) collective-permute-start(bf16[64,1024]{1,0:T(8,128)(2,1)} %get-tuple-element.23), channel_id=1, source_target_pairs={{0,12},{4,0},{8,4},{12,8},{1,13},{5,1},{9,5},{13,9},{2,14},{6,2},{... | collective-permute-start | bytes 393224 | tf_op jit(solution)/shard_map/ppermute | solution.py:59
  44.2 61.8 %collective-permute-start.1 = (bf16[1024,512]{1,0:T(8,128)(2,1)}, bf16[1024,512]{1,0:T(8,128)(2,1)}, u32[]{:S(2)}, u32[]{:S(2)}) collective-permute-start(bf16[1024,512]{1,0:T(8,128)(2,1)} %get-tuple-element.21.g_own), channel_id=1, source_target_pairs={{0,1},{1,0},{2,3},{3,2},{4,5},{5,4},{6,7},{7,6},{8,9},{9,8},{10,11... | collective-permute-start | bytes 3145736 | tf_op jit(solution)/shard_map/ppermute | solution.py:55
  44.2 10.9 %collective-permute-start.8 = (bf16[64,1024]{1,0:T(8,128)(2,1)}, bf16[64,1024]{1,0:T(8,128)(2,1)}, u32[]{:S(2)}, u32[]{:S(2)}) collective-permute-start(bf16[64,1024]{1,0:T(8,128)(2,1)} %get-tuple-element.23), channel_id=1, source_target_pairs={{0,4},{4,8},{8,12},{12,0},{1,5},{5,9},{9,13},{13,1},{2,6},{6,10},{... | collective-permute-start | bytes 393224 | tf_op jit(solution)/shard_map/ppermute | solution.py:59
  49.5 12.2 %collective-permute-start.16 = (bf16[128,512]{1,0:T(8,128)(2,1)}, bf16[128,512]{1,0:T(8,128)(2,1)S(1)}, u32[]{:S(2)}, u32[]{:S(2)}) collective-permute-start(bf16[128,512]{1,0:T(8,128)(2,1)} %get-tuple-element.26), channel_id=1, source_target_pairs={{0,8},{4,12},{8,0},{12,4},{1,9},{5,13},{9,1},{13,5},{2,10},{6,14},... | collective-permute-start | bytes 393224 | tf_op jit(solution)/shard_map/ppermute | solution.py:59
  51.4 12.3 %collective-permute-start.15 = (bf16[128,512]{1,0:T(8,128)(2,1)}, bf16[128,512]{1,0:T(8,128)(2,1)S(1)}, u32[]{:S(2)}, u32[]{:S(2)}) collective-permute-start(bf16[128,512]{1,0:T(8,128)(2,1)} %get-tuple-element.26), channel_id=1, source_target_pairs={{0,12},{4,0},{8,4},{12,8},{1,13},{5,1},{9,5},{13,9},{2,14},{6,2},{... | collective-permute-start | bytes 393224 | tf_op jit(solution)/shard_map/ppermute | solution.py:59
  55.1 13.6 %collective-permute-start.14 = (bf16[128,512]{1,0:T(8,128)(2,1)}, bf16[128,512]{1,0:T(8,128)(2,1)S(1)}, u32[]{:S(2)}, u32[]{:S(2)}) collective-permute-start(bf16[128,512]{1,0:T(8,128)(2,1)} %get-tuple-element.26), channel_id=1, source_target_pairs={{0,4},{4,8},{8,12},{12,0},{1,5},{5,9},{9,13},{13,1},{2,6},{6,10},{... | collective-permute-start | bytes 393224 | tf_op jit(solution)/shard_map/ppermute | solution.py:59
  61.7 11.8 %collective-permute-start.22 = (bf16[128,512]{1,0:T(8,128)(2,1)}, bf16[128,512]{1,0:T(8,128)(2,1)S(1)}, u32[]{:S(2)}, u32[]{:S(2)}) collective-permute-start(bf16[128,512]{1,0:T(8,128)(2,1)} %get-tuple-element.27), channel_id=1, source_target_pairs={{0,8},{4,12},{8,0},{12,4},{1,9},{5,13},{9,1},{13,5},{2,10},{6,14},... | collective-permute-start | bytes 393224 | tf_op jit(solution)/shard_map/ppermute | solution.py:59
  63.6 11.3 %collective-permute-start.21 = (bf16[128,512]{1,0:T(8,128)(2,1)}, bf16[128,512]{1,0:T(8,128)(2,1)S(1)}, u32[]{:S(2)}, u32[]{:S(2)}) collective-permute-start(bf16[128,512]{1,0:T(8,128)(2,1)} %get-tuple-element.27), channel_id=1, source_target_pairs={{0,12},{4,0},{8,4},{12,8},{1,13},{5,1},{9,5},{13,9},{2,14},{6,2},{... | collective-permute-start | bytes 393224 | tf_op jit(solution)/shard_map/ppermute | solution.py:59
  68.7 7.1 %collective-permute-start.20 = (bf16[128,512]{1,0:T(8,128)(2,1)}, bf16[128,512]{1,0:T(8,128)(2,1)S(1)}, u32[]{:S(2)}, u32[]{:S(2)}) collective-permute-start(bf16[128,512]{1,0:T(8,128)(2,1)} %get-tuple-element.27), channel_id=1, source_target_pairs={{0,4},{4,8},{8,12},{12,0},{1,5},{5,9},{9,13},{13,1},{2,6},{6,10},{... | collective-permute-start | bytes 393224 | tf_op jit(solution)/shard_map/ppermute | solution.py:59
  73.5 31.3 %copy-start.6 = (bf16[128,512]{1,0:T(8,128)(2,1)}, bf16[128,512]{1,0:T(8,128)(2,1)S(1)}, u32[]{:S(2)}) copy-start(bf16[128,512]{1,0:T(8,128)(2,1)S(1)} %collective-permute-done.22.refs_10_) | copy-start | bytes 393220
  73.5 6.3 %collective-permute-start.7 = (bf16[128,512]{1,0:T(8,128)(2,1)S(1)}, bf16[128,512]{1,0:T(8,128)(2,1)S(1)}, u32[]{:S(2)}, u32[]{:S(2)}) collective-permute-start(bf16[128,512]{1,0:T(8,128)(2,1)S(1)} %collective-permute-done.4.refs_3_), channel_id=1, source_target_pairs={{0,2},{2,0},{1,3},{3,1},{4,6},{6,4},{5,7},{7,5},{8,10},{10,8},{9,1... | collective-permute-start | bytes 393224 | tf_op jit(solution)/shard_map/ppermute | solution.py:47
  75.0 29.8 %copy-start.8 = (bf16[128,512]{1,0:T(8,128)(2,1)}, bf16[128,512]{1,0:T(8,128)(2,1)S(1)}, u32[]{:S(2)}) copy-start(bf16[128,512]{1,0:T(8,128)(2,1)S(1)} %collective-permute-done.21.refs_9_) | copy-start | bytes 393220
  75.0 7.3 %collective-permute-start.6 = (bf16[128,512]{1,0:T(8,128)(2,1)S(1)}, bf16[128,512]{1,0:T(8,128)(2,1)S(1)}, u32[]{:S(2)}, u32[]{:S(2)}) collective-permute-start(bf16[128,512]{1,0:T(8,128)(2,1)S(1)} %collective-permute-done.3.refs_2_), channel_id=1, source_target_pairs={{0,2},{2,0},{1,3},{3,1},{4,6},{6,4},{5,7},{7,5},{8,10},{10,8},{9,1... | collective-permute-start | bytes 393224 | tf_op jit(solution)/shard_map/ppermute | solution.py:47
  75.8 29.0 %copy-start.10 = (bf16[128,512]{1,0:T(8,128)(2,1)}, bf16[128,512]{1,0:T(8,128)(2,1)S(1)}, u32[]{:S(2)}) copy-start(bf16[128,512]{1,0:T(8,128)(2,1)S(1)} %collective-permute-done.20.refs_8_) | copy-start | bytes 393220
  75.8 8.4 %collective-permute-start.19 = (bf16[128,512]{1,0:T(8,128)(2,1)S(1)}, bf16[128,512]{1,0:T(8,128)(2,1)S(1)}, u32[]{:S(2)}, u32[]{:S(2)}) collective-permute-start(bf16[128,512]{1,0:T(8,128)(2,1)S(1)} %collective-permute-done.16.refs_3_), channel_id=1, source_target_pairs={{0,2},{2,0},{1,3},{3,1},{4,6},{6,4},{5,7},{7,5},{8,10},{10,8},{9,1... | collective-permute-start | bytes 393224 | tf_op jit(solution)/shard_map/ppermute | solution.py:47
  80.4 5.2 %collective-permute-start.18 = (bf16[128,512]{1,0:T(8,128)(2,1)S(1)}, bf16[128,512]{1,0:T(8,128)(2,1)S(1)}, u32[]{:S(2)}, u32[]{:S(2)}) collective-permute-start(bf16[128,512]{1,0:T(8,128)(2,1)S(1)} %collective-permute-done.15.refs_2_), channel_id=1, source_target_pairs={{0,2},{2,0},{1,3},{3,1},{4,6},{6,4},{5,7},{7,5},{8,10},{10,8},{9,1... | collective-permute-start | bytes 393224 | tf_op jit(solution)/shard_map/ppermute | solution.py:47
  82.9 6.1 %collective-permute-start.17 = (bf16[128,512]{1,0:T(8,128)(2,1)S(1)}, bf16[128,512]{1,0:T(8,128)(2,1)S(1)}, u32[]{:S(2)}, u32[]{:S(2)}) collective-permute-start(bf16[128,512]{1,0:T(8,128)(2,1)S(1)} %collective-permute-done.14.refs_1_), channel_id=1, source_target_pairs={{0,2},{2,0},{1,3},{3,1},{4,6},{6,4},{5,7},{7,5},{8,10},{10,8},{9,1... | collective-permute-start | bytes 393224 | tf_op jit(solution)/shard_map/ppermute | solution.py:47
  84.2 20.7 %copy-start.12 = (bf16[128,512]{1,0:T(8,128)(2,1)}, bf16[128,512]{1,0:T(8,128)(2,1)S(1)}, u32[]{:S(2)}) copy-start(bf16[128,512]{1,0:T(8,128)(2,1)S(1)} %collective-permute-done.19.refs_6_) | copy-start | bytes 393220
  84.2 6.4 %collective-permute-start.25 = (bf16[128,512]{1,0:T(8,128)(2,1)S(1)}, bf16[128,512]{1,0:T(8,128)(2,1)S(1)}, u32[]{:S(2)}, u32[]{:S(2)}) collective-permute-start(bf16[128,512]{1,0:T(8,128)(2,1)S(1)} %collective-permute-done.22.refs_10_), channel_id=1, source_target_pairs={{0,16},{16,0},{1,17},{17,1},{2,18},{18,2},{3,19},{19,3},{4,20},{20... | collective-permute-start | bytes 393224 | tf_op jit(solution)/shard_map/ppermute | solution.py:51
  85.7 19.2 %copy-start.14 = (bf16[128,512]{1,0:T(8,128)(2,1)}, bf16[128,512]{1,0:T(8,128)(2,1)S(1)}, u32[]{:S(2)}) copy-start(bf16[128,512]{1,0:T(8,128)(2,1)S(1)} %collective-permute-done.18.refs_5_) | copy-start | bytes 393220
  85.7 7.7 %collective-permute-start.24 = (bf16[128,512]{1,0:T(8,128)(2,1)S(1)}, bf16[128,512]{1,0:T(8,128)(2,1)S(1)}, u32[]{:S(2)}, u32[]{:S(2)}) collective-permute-start(bf16[128,512]{1,0:T(8,128)(2,1)S(1)} %collective-permute-done.21.refs_9_), channel_id=1, source_target_pairs={{0,16},{16,0},{1,17},{17,1},{2,18},{18,2},{3,19},{19,3},{4,20},{20... | collective-permute-start | bytes 393224 | tf_op jit(solution)/shard_map/ppermute | solution.py:51
  88.9 15.9 %copy-start.16 = (bf16[128,512]{1,0:T(8,128)(2,1)}, bf16[128,512]{1,0:T(8,128)(2,1)S(1)}, u32[]{:S(2)}) copy-start(bf16[128,512]{1,0:T(8,128)(2,1)S(1)} %collective-permute-done.17.refs_4_) | copy-start | bytes 393220
  89.0 6.3 %collective-permute-start.23 = (bf16[128,512]{1,0:T(8,128)(2,1)S(1)}, bf16[128,512]{1,0:T(8,128)(2,1)S(1)}, u32[]{:S(2)}, u32[]{:S(2)}) collective-permute-start(bf16[128,512]{1,0:T(8,128)(2,1)S(1)} %collective-permute-done.20.refs_8_), channel_id=1, source_target_pairs={{0,16},{16,0},{1,17},{17,1},{2,18},{18,2},{3,19},{19,3},{4,20},{20... | collective-permute-start | bytes 393224 | tf_op jit(solution)/shard_map/ppermute | solution.py:51
  90.5 14.4 %collective-permute-start.5 = (bf16[128,512]{1,0:T(8,128)(2,1)S(1)}, bf16[128,512]{1,0:T(8,128)(2,1)S(1)}, u32[]{:S(2)}, u32[]{:S(2)}) collective-permute-start(bf16[128,512]{1,0:T(8,128)(2,1)S(1)} %collective-permute-done.2.refs_1_), channel_id=1, source_target_pairs={{0,2},{2,0},{1,3},{3,1},{4,6},{6,4},{5,7},{7,5},{8,10},{10,8},{9,1... | collective-permute-start | bytes 393224 | tf_op jit(solution)/shard_map/ppermute | solution.py:47
  93.3 12.7 %collective-permute-start.13 = (bf16[64,1024]{1,0:T(8,128)(2,1)S(1)}, bf16[64,1024]{1,0:T(8,128)(2,1)S(1)}, u32[]{:S(2)}, u32[]{:S(2)}) collective-permute-start(bf16[64,1024]{1,0:T(8,128)(2,1)S(1)} %collective-permute-done.10.refs_10_), channel_id=1, source_target_pairs={{0,16},{16,0},{1,17},{17,1},{2,18},{18,2},{3,19},{19,3},{4,20},{20... | collective-permute-start | bytes 393224 | tf_op jit(solution)/shard_map/ppermute | solution.py:51
  95.3 10.8 %collective-permute-start.12 = (bf16[64,1024]{1,0:T(8,128)(2,1)}, bf16[64,1024]{1,0:T(8,128)(2,1)S(1)}, u32[]{:S(2)}, u32[]{:S(2)}) collective-permute-start(bf16[64,1024]{1,0:T(8,128)(2,1)} %collective-permute-done.9.refs_9_), channel_id=1, source_target_pairs={{0,16},{16,0},{1,17},{17,1},{2,18},{18,2},{3,19},{19,3},{4,20},{20... | collective-permute-start | bytes 393224 | tf_op jit(solution)/shard_map/ppermute | solution.py:51
  96.2 9.8 %collective-permute-start.11 = (bf16[64,1024]{1,0:T(8,128)(2,1)}, bf16[64,1024]{1,0:T(8,128)(2,1)S(1)}, u32[]{:S(2)}, u32[]{:S(2)}) collective-permute-start(bf16[64,1024]{1,0:T(8,128)(2,1)} %collective-permute-done.8.refs_8_), channel_id=1, source_target_pairs={{0,16},{16,0},{1,17},{17,1},{2,18},{18,2},{3,19},{19,3},{4,20},{20... | collective-permute-start | bytes 393224 | tf_op jit(solution)/shard_map/ppermute | solution.py:51
  104.9 9.4 %collective-permute-start.26 = (bf16[256,128]{1,0:T(8,128)(2,1)S(1)}, bf16[256,128]{1,0:T(8,128)(2,1)S(1)}, u32[]{:S(2)}, u32[]{:S(2)}) collective-permute-start(bf16[256,128]{1,0:T(8,128)(2,1)S(1)} %convert_element_type.48), channel_id=1, source_target_pairs={{0,2},{2,0},{1,3},{3,1},{4,6},{6,4},{5,7},{7,5},{8,10},{10,8},{9,1... | collective-permute-start | bytes 196616 | tf_op jit(solution)/shard_map/ppermute | solution.py:47
  113.3 7.7 %collective-permute-start.31 = (bf16[256,128]{1,0:T(8,128)(2,1)S(1)}, bf16[256,128]{1,0:T(8,128)(2,1)S(1)}, u32[]{:S(2)}, u32[]{:S(2)}) collective-permute-start(bf16[256,128]{1,0:T(8,128)(2,1)S(1)} %convert_element_type.56), channel_id=1, source_target_pairs={{0,2},{2,0},{1,3},{3,1},{4,6},{6,4},{5,7},{7,5},{8,10},{10,8},{9,1... | collective-permute-start | bytes 196616 | tf_op jit(solution)/shard_map/ppermute | solution.py:47
  114.4 11.2 %collective-permute-start.29 = (bf16[256,128]{1,0:T(8,128)(2,1)S(1)}, bf16[256,128]{1,0:T(8,128)(2,1)S(1)}, u32[]{:S(2)}, u32[]{:S(2)}) collective-permute-start(bf16[256,128]{1,0:T(8,128)(2,1)S(1)} %fusion.1), channel_id=1, source_target_pairs={{0,8},{4,12},{8,0},{12,4},{1,9},{5,13},{9,1},{13,5},{2,10},{6,14},... | collective-permute-start | bytes 196616 | tf_op jit(solution)/shard_map/ppermute | solution.py:59
  116.7 8.8 %collective-permute-start.28 = (bf16[256,128]{1,0:T(8,128)(2,1)S(1)}, bf16[256,128]{1,0:T(8,128)(2,1)S(1)}, u32[]{:S(2)}, u32[]{:S(2)}) collective-permute-start(bf16[256,128]{1,0:T(8,128)(2,1)S(1)} %fusion.1), channel_id=1, source_target_pairs={{0,12},{4,0},{8,4},{12,8},{1,13},{5,1},{9,5},{13,9},{2,14},{6,2},{... | collective-permute-start | bytes 196616 | tf_op jit(solution)/shard_map/ppermute | solution.py:59
  120.5 6.2 %collective-permute-start.27 = (bf16[256,128]{1,0:T(8,128)(2,1)S(1)}, bf16[256,128]{1,0:T(8,128)(2,1)S(1)}, u32[]{:S(2)}, u32[]{:S(2)}) collective-permute-start(bf16[256,128]{1,0:T(8,128)(2,1)S(1)} %fusion.1), channel_id=1, source_target_pairs={{0,4},{4,8},{8,12},{12,0},{1,5},{5,9},{9,13},{13,1},{2,6},{6,10},{... | collective-permute-start | bytes 196616 | tf_op jit(solution)/shard_map/ppermute | solution.py:59
  121.1 12.3 %collective-permute-start.34 = (bf16[256,128]{1,0:T(8,128)(2,1)S(1)}, bf16[256,128]{1,0:T(8,128)(2,1)S(1)}, u32[]{:S(2)}, u32[]{:S(2)}) collective-permute-start(bf16[256,128]{1,0:T(8,128)(2,1)S(1)} %fusion.2), channel_id=1, source_target_pairs={{0,8},{4,12},{8,0},{12,4},{1,9},{5,13},{9,1},{13,5},{2,10},{6,14},... | collective-permute-start | bytes 196616 | tf_op jit(solution)/shard_map/ppermute | solution.py:59
  122.6 10.8 %collective-permute-start.33 = (bf16[256,128]{1,0:T(8,128)(2,1)S(1)}, bf16[256,128]{1,0:T(8,128)(2,1)S(1)}, u32[]{:S(2)}, u32[]{:S(2)}) collective-permute-start(bf16[256,128]{1,0:T(8,128)(2,1)S(1)} %fusion.2), channel_id=1, source_target_pairs={{0,12},{4,0},{8,4},{12,8},{1,13},{5,1},{9,5},{13,9},{2,14},{6,2},{... | collective-permute-start | bytes 196616 | tf_op jit(solution)/shard_map/ppermute | solution.py:59
  125.5 7.9 %collective-permute-start.32 = (bf16[256,128]{1,0:T(8,128)(2,1)S(1)}, bf16[256,128]{1,0:T(8,128)(2,1)S(1)}, u32[]{:S(2)}, u32[]{:S(2)}) collective-permute-start(bf16[256,128]{1,0:T(8,128)(2,1)S(1)} %fusion.2), channel_id=1, source_target_pairs={{0,4},{4,8},{8,12},{12,0},{1,5},{5,9},{9,13},{13,1},{2,6},{6,10},{... | collective-permute-start | bytes 196616 | tf_op jit(solution)/shard_map/ppermute | solution.py:59
  133.3 8.2 %collective-permute-start.30 = (bf16[512,1024]{1,0:T(8,128)(2,1)S(1)}, bf16[512,1024]{1,0:T(8,128)(2,1)S(1)}, u32[]{:S(2)}, u32[]{:S(2)}) collective-permute-start(bf16[512,1024]{1,0:T(8,128)(2,1)S(1)} %get-tuple-element.30), channel_id=1, source_target_pairs={{0,1},{1,0},{2,3},{3,2},{4,5},{5,4},{6,7},{7,6},{8,9},{9,8},{10,11... | collective-permute-start | bytes 3145736 | tf_op jit(solution)/shard_map/ppermute | solution.py:55
  140.9 3.2 %collective-permute-start.35 = (bf16[1024,512]{1,0:T(8,128)(2,1)}, bf16[1024,512]{1,0:T(8,128)(2,1)}, u32[]{:S(2)}, u32[]{:S(2)}) collective-permute-start(bf16[1024,512]{1,0:T(8,128)(2,1)} %get-tuple-element.37), channel_id=1, source_target_pairs={{0,1},{1,0},{2,3},{3,2},{4,5},{5,4},{6,7},{7,6},{8,9},{9,8},{10,11... | collective-permute-start | bytes 3145736 | tf_op jit(solution)/shard_map/ppermute | solution.py:55
  (22 other events, 143.0 us)

commit v3 on v2

--- a/solution.py
+++ b/solution.py
@@ -59,9 +59,10 @@
     return lax.ppermute(a, "space", [(i, (i + step) % 4) for i in range(4)])
 
 
-def pieces(half, swap):
-    near = tuple(turn_z(half, step) for step in (1, 3, 2))
-    return near + tuple(swap(a) for a in near)
+def pieces(quarter, first, second):
+    near = tuple(turn_z(quarter, step) for step in (1, 3, 2))
+    side = tuple(first(a) for a in near)
+    return near + side + tuple(second(a) for a in near) + tuple(second(a) for a in side)
 
 
 def sum_over_chips(part):
@@ -76,22 +77,21 @@
     return pl.ds(pl.multiple_of(index * size, size), size)
 
 
-def send_body(pos, q, k, v, o, q_half, k_half, v_half, o_half, sems):
-    c, x, y = pos[1], pos[2], pos[3]
+def send_body(pos, q, k, v, o, kv, qo, sems):
+    c, part = pos[1], pos[2]
     copies = []
-    for n, (ref, half, bit) in enumerate(((q, q_half, x), (k, k_half, x), (v, v_half, y))):
+
+    def add(src, dst):
+        copies.append(pltpu.make_async_copy(src, dst, sems.at[len(copies)]))
+
+    for ref, out, base in ((k, kv, 0), (v, kv, 64), (q, qo, 0)):
         for j in range(4):
             cols = pl.ds(pl.multiple_of(256 * j + 128 * c, 128), 128)
-            copies.append(
-                pltpu.make_async_copy(
-                    ref.at[aligned(bit, half.shape[0]), cols],
-                    half.at[:, 128 * j : 128 * j + 128],
-                    sems.at[4 * n + j],
-                )
-            )
-    copies.append(
-        pltpu.make_async_copy(o.at[aligned(2 * c + y, o_half.shape[0])], o_half, sems.at[12])
-    )
+            dst = out.at[base : base + 64, 128 * j : 128 * j + 128]
+            add(ref.at[aligned(part, 64), cols], dst)
+    for n in range(2):
+        src = o.at[aligned(4 * c + part, 32), 512 * n : 512 * n + 512]
+        add(src, qo.at[64 + 32 * n : 96 + 32 * n])
     for one in copies:
         one.start()
     for one in copies:
@@ -111,24 +111,28 @@
         cols[at, :] = (grad[at, :].astype(F32) * scale[at, :] * mask).astype(BF16)
 
 
-def place(pos_ref, own_ref, parts, full_ref, sems, axis, base, by_rows=False):
-    z, c, bit = pos_ref[0], pos_ref[1], pos_ref[axis]
-    rows = parts[0].shape[0]
-    whole = 2 * rows
+def place(pos_ref, own_ref, parts, full_ref, sems, flips, base, begin, by_rows=False):
+    z, c, part = pos_ref[0], pos_ref[1], pos_ref[2]
     copies = []
 
     def add(src, dst):
         copies.append(pltpu.make_async_copy(src, dst, sems.at[base + len(copies)]))
 
     if by_rows:
-        add(own_ref.at[aligned(c, whole)], full_ref.at[aligned(z, whole)])
+        add(own_ref.at[aligned(c, 128)], full_ref.at[aligned(z, 128)])
     else:
         for j in range(4):
             cols = pl.ds(pl.multiple_of(256 * j + 128 * c, 128), 128)
-            add(own_ref.at[:, cols], full_ref.at[aligned(z, whole), 128 * j : 128 * j + 128])
+            add(own_ref.at[:, cols], full_ref.at[aligned(z, 256), 128 * j : 128 * j + 128])
     for n, ref in enumerate(parts):
-        at = lax.rem(z + (3, 1, 2)[n % 3], 4) * 2 + (bit if n < 3 else 1 - bit)
-        add(ref, full_ref.at[aligned(at, rows)])
+        flip = (0,) + flips + (3,)
+        at = lax.rem(z + (3, 1, 2)[n % 3], 4) * 4 + lax.bitwise_xor(part, flip[n // 3])
+        if by_rows:
+            for m in range(2):
+                dst = full_ref.at[aligned(at, 32), 512 * m : 512 * m + 512]
+                add(ref.at[begin + 32 * m : begin + 32 * m + 32], dst)
+        else:
+            add(ref.at[begin : begin + 64], full_ref.at[aligned(at, 64)])
     for one in copies:
         one.start()
     return copies
@@ -161,10 +165,10 @@
 
 
 def key_value_body(pos, x_own, x_other, ks, vs, *refs):
-    k, v = refs[0:7], refs[7:14]
+    k, v, parts = refs[0], refs[1], refs[2:14]
     key_out, value_out, state, key, value, wk, wv, sems = refs[14:]
-    fetch_k = place(pos, k[0], k[1:], wk, sems, 2, 0)
-    fetch_v = place(pos, v[0], v[1:], wv, sems, 3, 10)
+    fetch_k = place(pos, k, parts, wk, sems, (1, 2), 0, 0)
+    fetch_v = place(pos, v, parts, wv, sems, (1, 2), 16, 64)
     half = x_own.shape[0]
     stores = []
     for fetch, w, scale, dst, out in (
@@ -175,7 +179,7 @@
             for t in range(0, half, 256):
                 at = slice(n * half + t, n * half + t + 256)
                 dst[at, :] = (dot(rows[t : t + 256, :], w[...], 1, 0) * scale[...]).astype(BF16)
-        stores.append(pltpu.make_async_copy(dst, out, sems.at[20 + len(stores)]))
+        stores.append(pltpu.make_async_copy(dst, out, sems.at[41 + len(stores)]))
         stores[-1].start()
     for g in range(2):
         cols = slice(256 * g, 256 * g + 256)
@@ -186,10 +190,10 @@
 
 
 def query_back_body(scale, pos, x_own, x_other, g_own, g_other, qs, *refs):
-    q, o = refs[0:7], refs[7:14]
+    q, o, parts = refs[0], refs[1], refs[2:14]
     query, back, term, wq, wo, sems = refs[14:]
-    fetch_q = place(pos, q[0], q[1:], wq, sems, 2, 0)
-    fetch_o = place(pos, o[0], o[1:], wo, sems, 3, 10, True)
+    fetch_q = place(pos, q, parts, wq, sems, (2, 1), 0, 0)
+    fetch_o = place(pos, o, parts, wo, sems, (2, 1), 16, 64, True)
     half = x_own.shape[0]
     wait(fetch_q)
     for n, rows in enumerate((x_own, x_other)):
@@ -209,10 +213,10 @@
 
 
 def middle_body(scale, pos, query, back, state, qs, *refs):
-    q, o = refs[0:7], refs[7:14]
+    q, o, parts = refs[0], refs[1], refs[2:14]
     out_own, out_other, in_own, in_other, diag, att, qb, wq, wo, sems = refs[14:]
-    fetch_o = place(pos, o[0], o[1:], wo, sems, 3, 10, True)
-    fetch_q = place(pos, q[0], q[1:], wq, sems, 2, 0)
+    fetch_o = place(pos, o, parts, wo, sems, (2, 1), 16, 64, True)
+    fetch_q = place(pos, q, parts, wq, sems, (2, 1), 0, 0)
     half = out_own.shape[0]
     for g in range(2):
         part = slice(256 * g, 256 * g + 256)
@@ -229,10 +233,10 @@
 
 
 def tail_body(pos, key, value, term, ks, vs, in_own, in_other, *refs):
-    k, v = refs[0:7], refs[7:14]
+    k, v, parts = refs[0], refs[1], refs[2:14]
     res_own, res_other, diag, kb, vb, wk, wv, sems = refs[14:]
-    fetch = place(pos, k[0], k[1:], wk, sems, 2, 0)
-    fetch += place(pos, v[0], v[1:], wv, sems, 3, 10)
+    fetch = place(pos, k, parts, wk, sems, (1, 2), 0, 0)
+    fetch += place(pos, v, parts, wv, sems, (1, 2), 16, 64)
     half = in_own.shape[1]
     for g in range(2):
         part = slice(256 * g, 256 * g + 256)
@@ -268,24 +272,20 @@
     both = 2 * tokens
     slots = active_blocks.shape[1] * BLOCK
     scale = 1.0 / math.sqrt(HEAD_DIM * slots * lax.axis_size(REDUCE_AXES))
-    pos = jnp.stack([z, c, x, y]).astype(jnp.int32)
+    pos = jnp.stack([z, c, 2 * y + x]).astype(jnp.int32)
 
     def own_scale(v):
         return lax.dynamic_index_in_dim(v.reshape(4, 2, 128), c, 1, keepdims=False).reshape(mine)
 
-    half = query_weight.shape[0] // 2
-    q_half, k_half, v_half, o_half = call(
+    kv, qo = call(
         send_body,
-        [shape((half, mine))] * 3 + [shape((half // 2, width))],
+        [shape((128, mine))] * 2,
         [SMEM] + [ANY] * 4,
         (pos, query_weight, key_weight, value_weight, out_weight),
-        (pltpu.SemaphoreType.DMA((13,)),),
-        out_specs=(ANY,) * 4,
-    )
-    k = (key_weight,) + pieces(k_half, swap_x)
-    v = (value_weight,) + pieces(v_half, swap_y)
-    q = (query_weight,) + pieces(q_half, swap_x)
-    o = (out_weight,) + pieces(o_half, swap_y)
+        (pltpu.SemaphoreType.DMA((14,)),),
+    )
+    kv = (key_weight, value_weight) + pieces(kv, swap_x, swap_y)
+    qo = (query_weight, out_weight) + pieces(qo, swap_y, swap_x)
     x_own, g_own = call(
         mask_body,
         [shape((tokens, width)), shape((width, tokens))],
@@ -296,7 +296,7 @@
     x_other, g_other = swap_core(x_own), swap_core(g_own)
 
     ks, vs, qs = own_scale(key_scale), own_scale(value_scale), own_scale(query_scale)
-    sems = pltpu.SemaphoreType.DMA((22,))
+    sems = pltpu.SemaphoreType.DMA((43,))
     tall, wide = pltpu.VMEM((width, mine), BF16), pltpu.VMEM((mine, width), BF16)
     kept = pltpu.VMEM((both, mine), BF16)
     ff = 2 * both * width * mine
@@ -304,7 +304,7 @@
         key_value_body,
         [shape((both, mine)), shape((both, mine)), shape((256, 128), F32)],
         [SMEM] + [VMEM] * 4 + [ANY] * 14,
-        (pos, x_own, x_other, ks[None], vs[None], *k, *v),
+        (pos, x_own, x_other, ks[None], vs[None], *kv),
         (kept, kept, tall, tall, sems), 2 * ff, 24 << 20, (ANY, ANY, VMEM),
     )
     state = sum_over_chips(state)
@@ -312,7 +312,7 @@
         functools.partial(query_back_body, scale),
         [shape((both, mine)), shape((mine, both)), shape((256, 128), F32)],
         [SMEM] + [VMEM] * 5 + [ANY] * 14,
-        (pos, x_own, x_other, g_own, g_other, qs[None], *q, *o),
+        (pos, x_own, x_other, g_own, g_other, qs[None], *qo),
         (tall, wide, sems), 2 * ff, 24 << 20,
     )
     term = sum_over_chips(term)
@@ -322,7 +322,7 @@
         [shape((tokens, width), F32), shape((tokens, width)),
          shape((width, tokens), F32), shape((width, tokens), F32)],
         [SMEM] + [VMEM] * 4 + [ANY] * 14,
-        (pos, query, back, state, qs[:, None], *q, *o),
+        (pos, query, back, state, qs[:, None], *qo),
         (diag, kept, pltpu.VMEM((mine, both), BF16), tall, wide, sems), 2 * ff, 32 << 20,
     )
     out_sum = out_own + swap_core(out_other).astype(F32)
@@ -331,7 +331,7 @@
         tail_body,
         [shape((width, tokens), F32), shape((width, tokens))],
         [SMEM] + [VMEM] * 7 + [ANY] * 14,
-        (pos, key, value, term, ks[None], vs[None], in_own, in_other, *k, *v),
+        (pos, key, value, term, ks[None], vs[None], in_own, in_other, *kv),
         (diag, kept, kept, tall, tall, sems), 2 * ff, 32 << 20,
     )
     input_grad = (res_own + swap_core(res_other).astype(F32)).astype(BF16)

time: 147 us -> 116 us (0.79)
  Pallas kernels: 48.5 us -> 32.8 us
  starting transfers between devices: 68.9 us -> 56.5 us
  waiting for transfers between devices: 16.8 us -> 14.8 us
    ppermute x18 -> x12, starting transfers between devices: 51.9 us -> 30 us  [turn_z(): return lax.ppermute(a, 'space', [(i, (i + step) % 4) for i in range(4)])]
    pallas_call x6, Pallas kernels: 48.5 us -> 32.8 us  [call(): pl.pallas_call(body, out_shape=tuple(outs), in_specs=in_specs, out_specs=...]
    ppermute x6 -> x9, starting transfers between devices: 6.39 us -> 12.3 us  [swap_y(): return lax.ppermute(a, 'groups', [(0, 1), (1, 0)])]
    ppermute x8 -> x11, starting transfers between devices: 9.49 us -> 13.1 us  [swap_x(): return lax.ppermute(a, 'tm', [(0, 1), (1, 0)])]
    ppermute x8 -> x11, waiting for transfers between devices: 4.58 us -> 1.54 us  [swap_x(): return lax.ppermute(a, 'tm', [(0, 1), (1, 0)])]
    ppermute x6 -> x9, waiting for transfers between devices: 3.71 us -> 6.62 us  [swap_y(): return lax.ppermute(a, 'groups', [(0, 1), (1, 0)])]
    ppermute x18 -> x12, waiting for transfers between devices: 7.58 us -> 5.7 us  [turn_z(): return lax.ppermute(a, 'space', [(i, (i + step) % 4) for i in range(4)])]
    unnamed x69 -> x65, local copies, waits for them, and re-layouts: 5.84 us -> 5.19 us
  transfers between devices with their start and end apart: 36 -> 36, of which waited for: 11 -> 16; matrix products, arithmetic and copies ran while one was open for 2% -> 2% of each run, Pallas kernels for 32% -> 26%
where the time goes in v3:
time: 116 us
  starting transfers between devices  56.5 us (49%)
  Pallas kernels  32.8 us (28%)
  waiting for transfers between devices  14.8 us (13%)
  local copies, waits for them, and re-layouts  6.26 us (5%)
  other arithmetic  3.74 us (3%)
  between operations  1.78 us (2%)
    pallas_call x6, Pallas kernels, call(): pl.pallas_call(body, out_shape=tuple(outs), in_specs=in_specs, out_specs=...  32.8 us
    ppermute x12, starting transfers between devices, turn_z(): return lax.ppermute(a, 'space', [(i, (i + step) % 4) for i in range(4)])  30 us
    ppermute x11, starting transfers between devices, swap_x(): return lax.ppermute(a, 'tm', [(0, 1), (1, 0)])  13.1 us
    ppermute x9, starting transfers between devices, swap_y(): return lax.ppermute(a, 'groups', [(0, 1), (1, 0)])  12.3 us
    ppermute x9, waiting for transfers between devices, swap_y(): return lax.ppermute(a, 'groups', [(0, 1), (1, 0)])  6.62 us
    ppermute x12, waiting for transfers between devices, turn_z(): return lax.ppermute(a, 'space', [(i, (i + step) % 4) for i in range(4)])  5.7 us
    unnamed x65, local copies, waits for them, and re-layouts  5.19 us
    convert_element_type x1, other arithmetic, per_device_split(): input_grad = (res_own + swap_core(res_other).astype(F32)).astype(BF16)  2.54 us
  transfers between devices with their start and end apart: 36, of which 16 were waited for; matrix products, arithmetic and copies ran while one was open for 2% of the time, Pallas kernels for 26%

profile of v3, /device:TPU:0, one launch (start us, length us, event | category | flops | bytes accessed | tf_op | source)
XLA Modules:
  0.0 115.9 jit_solution(3724616472144828962)
XLA Ops:
  1.3 0.9 copy.15.scale
  2.2 1.2 %copy-done.2 = bf16[1024,512]{1,0:T(8,128)(2,1)S(1)} copy-done((bf16[1024,512]{1,0:T(8,128)(2,1)S(1)}, bf16[1024,512]{1,0:T(8,128)(2,1)}, u32[]{:S(2)}) %copy-start.2) | copy-done | bytes 1048600
  3.4 1.2 %copy-done.3 = bf16[1024,512]{1,0:T(8,128)(2,1)S(1)} copy-done((bf16[1024,512]{1,0:T(8,128)(2,1)S(1)}, bf16[1024,512]{1,0:T(8,128)(2,1)}, u32[]{:S(2)}) %copy-start.3) | copy-done | bytes 1048600
  5.3 2.2 %shard_map.131 = (bf16[512,1024]{1,0:T(8,128)(2,1)}, bf16[1024,512]{1,0:T(8,128)(2,1)}) custom-call(s32[1,6]{1,0:T(1,128)S(1)} %copy-done.25, s32[1]{0:T(128)S(6)} %copy.18.count, bf16[1024,512]{1,0:T(8,128)(2,1)S(1)} %copy-done.2, bf16[1024,512]{1,0:T(8,128)(2,1)S(1)} %copy-done.3, f32[1024,1]{1,0:T(8,128)S(1)} %copy.15.scale), custom_call_target="tpu_custom_call" | custom-call | bytes 4198428 | tf_op jit(solution)/shard_map/pallas_call | solution.py:31
  8.7 2.5 %shard_map.132 = (bf16[128,512]{1,0:T(8,128)(2,1)}, bf16[128,512]{1,0:T(8,128)(2,1)}) custom-call(s32[3]{0:T(128)} %pad_add_fusion.pos, bf16[256,1024]{1,0:T(8,128)(2,1)} %refs_0_.6, bf16[256,1024]{1,0:T(8,128)(2,1)} %refs_0_.7, bf16[256,1024]{1,0:T(8,128)(2,1)} %refs_1_.7, bf16[256,1024]{1,0:T(8,128)(2,1)} %refs_1_.6), custom_call_target="tpu_custom_call" | custom-call | bytes 2359308 | tf_op jit(solution)/shard_map/pallas_call | solution.py:31
  11.2 3.7 %collective-permute-start.4 = (bf16[128,512]{1,0:T(8,128)(2,1)}, bf16[128,512]{1,0:T(8,128)(2,1)S(1)}, u32[]{:S(2)}, u32[]{:S(2)}) collective-permute-start(bf16[128,512]{1,0:T(8,128)(2,1)} %get-tuple-element.20), channel_id=1, source_target_pairs={{0,8},{4,12},{8,0},{12,4},{1,9},{5,13},{9,1},{13,5},{2,10},{6,14},... | collective-permute-start | bytes 393224 | tf_op jit(solution)/shard_map/ppermute | solution.py:59
  14.9 1.3 %collective-permute-start.3 = (bf16[128,512]{1,0:T(8,128)(2,1)}, bf16[128,512]{1,0:T(8,128)(2,1)S(1)}, u32[]{:S(2)}, u32[]{:S(2)}) collective-permute-start(bf16[128,512]{1,0:T(8,128)(2,1)} %get-tuple-element.20), channel_id=1, source_target_pairs={{0,12},{4,0},{8,4},{12,8},{1,13},{5,1},{9,5},{13,9},{2,14},{6,2},{... | collective-permute-start | bytes 393224 | tf_op jit(solution)/shard_map/ppermute | solution.py:59
  16.2 0.7 collective-permute-start.2
  16.9 1.0 collective-permute-start.16
  17.9 4.4 %collective-permute-done.4.refs_4_ = bf16[128,512]{1,0:T(8,128)(2,1)S(1)} collective-permute-done((bf16[128,512]{1,0:T(8,128)(2,1)}, bf16[128,512]{1,0:T(8,128)(2,1)S(1)}, u32[]{:S(2)}, u32[]{:S(2)}) %collective-permute-start.4) | collective-permute-done | bytes 131104 | tf_op jit(solution)/shard_map/ppermute | solution.py:59
  22.3 6.6 %collective-permute-start.15 = (bf16[128,512]{1,0:T(8,128)(2,1)}, bf16[128,512]{1,0:T(8,128)(2,1)S(1)}, u32[]{:S(2)}, u32[]{:S(2)}) collective-permute-start(bf16[128,512]{1,0:T(8,128)(2,1)} %get-tuple-element.23), channel_id=1, source_target_pairs={{0,12},{4,0},{8,4},{12,8},{1,13},{5,1},{9,5},{13,9},{2,14},{6,2},{... | collective-permute-start | bytes 393224 | tf_op jit(solution)/shard_map/ppermute | solution.py:59
  28.9 5.3 %collective-permute-start.14 = (bf16[128,512]{1,0:T(8,128)(2,1)}, bf16[128,512]{1,0:T(8,128)(2,1)S(1)}, u32[]{:S(2)}, u32[]{:S(2)}) collective-permute-start(bf16[128,512]{1,0:T(8,128)(2,1)} %get-tuple-element.23), channel_id=1, source_target_pairs={{0,4},{4,8},{8,12},{12,0},{1,5},{5,9},{9,13},{13,1},{2,6},{6,10},{... | collective-permute-start | bytes 393224 | tf_op jit(solution)/shard_map/ppermute | solution.py:59
  34.2 1.5 %collective-permute-start.10 = (bf16[128,512]{1,0:T(8,128)(2,1)S(1)}, bf16[128,512]{1,0:T(8,128)(2,1)S(1)}, u32[]{:S(2)}, u32[]{:S(2)}) collective-permute-start(bf16[128,512]{1,0:T(8,128)(2,1)S(1)} %collective-permute-done.4.refs_4_), channel_id=1, source_target_pairs={{0,2},{2,0},{1,3},{3,1},{4,6},{6,4},{5,7},{7,5},{8,10},{10,8},{9,1... | collective-permute-start | bytes 393224 | tf_op jit(solution)/shard_map/ppermute | solution.py:47
  35.7 1.5 %collective-permute-start.7 = (bf16[128,512]{1,0:T(8,128)(2,1)S(1)}, bf16[128,512]{1,0:T(8,128)(2,1)}, u32[]{:S(2)}, u32[]{:S(2)}) collective-permute-start(bf16[128,512]{1,0:T(8,128)(2,1)S(1)} %collective-permute-done.4.refs_4_), channel_id=1, source_target_pairs={{0,16},{16,0},{1,17},{17,1},{2,18},{18,2},{3,19},{19,3},{4,20},{20... | collective-permute-start | bytes 393224 | tf_op jit(solution)/shard_map/ppermute | solution.py:51
  37.3 1.5 %collective-permute-start.9 = (bf16[128,512]{1,0:T(8,128)(2,1)S(1)}, bf16[128,512]{1,0:T(8,128)(2,1)S(1)}, u32[]{:S(2)}, u32[]{:S(2)}) collective-permute-start(bf16[128,512]{1,0:T(8,128)(2,1)S(1)} %collective-permute-done.3.refs_3_), channel_id=1, source_target_pairs={{0,2},{2,0},{1,3},{3,1},{4,6},{6,4},{5,7},{7,5},{8,10},{10,8},{9,1... | collective-permute-start | bytes 393224 | tf_op jit(solution)/shard_map/ppermute | solution.py:47
  39.3 1.5 %collective-permute-start.6 = (bf16[128,512]{1,0:T(8,128)(2,1)S(1)}, bf16[128,512]{1,0:T(8,128)(2,1)}, u32[]{:S(2)}, u32[]{:S(2)}) collective-permute-start(bf16[128,512]{1,0:T(8,128)(2,1)S(1)} %collective-permute-done.3.refs_3_), channel_id=1, source_target_pairs={{0,16},{16,0},{1,17},{17,1},{2,18},{18,2},{3,19},{19,3},{4,20},{20... | collective-permute-start | bytes 393224 | tf_op jit(solution)/shard_map/ppermute | solution.py:51
  41.1 1.5 %collective-permute-start.5 = (bf16[128,512]{1,0:T(8,128)(2,1)S(1)}, bf16[128,512]{1,0:T(8,128)(2,1)}, u32[]{:S(2)}, u32[]{:S(2)}) collective-permute-start(bf16[128,512]{1,0:T(8,128)(2,1)S(1)} %collective-permute-done.2.refs_2_), channel_id=1, source_target_pairs={{0,16},{16,0},{1,17},{17,1},{2,18},{18,2},{3,19},{19,3},{4,20},{20... | collective-permute-start | bytes 393224 | tf_op jit(solution)/shard_map/ppermute | solution.py:51
  43.3 1.2 %collective-permute-start.22 = (bf16[128,512]{1,0:T(8,128)(2,1)S(1)}, bf16[128,512]{1,0:T(8,128)(2,1)S(1)}, u32[]{:S(2)}, u32[]{:S(2)}) collective-permute-start(bf16[128,512]{1,0:T(8,128)(2,1)S(1)} %collective-permute-done.16.refs_4_), channel_id=1, source_target_pairs={{0,16},{16,0},{1,17},{17,1},{2,18},{18,2},{3,19},{19,3},{4,20},{20... | collective-permute-start | bytes 393224 | tf_op jit(solution)/shard_map/ppermute | solution.py:51
  44.5 1.3 %collective-permute-done.6.refs_6_ = bf16[128,512]{1,0:T(8,128)(2,1)} collective-permute-done((bf16[128,512]{1,0:T(8,128)(2,1)S(1)}, bf16[128,512]{1,0:T(8,128)(2,1)}, u32[]{:S(2)}, u32[]{:S(2)}) %collective-permute-start.6) | collective-permute-done | bytes 131104 | tf_op jit(solution)/shard_map/ppermute | solution.py:51
  45.7 1.1 collective-permute-start.19
  46.8 1.7 %collective-permute-done.5.refs_5_ = bf16[128,512]{1,0:T(8,128)(2,1)} collective-permute-done((bf16[128,512]{1,0:T(8,128)(2,1)S(1)}, bf16[128,512]{1,0:T(8,128)(2,1)}, u32[]{:S(2)}, u32[]{:S(2)}) %collective-permute-start.5) | collective-permute-done | bytes 131104 | tf_op jit(solution)/shard_map/ppermute | solution.py:51
  48.6 1.5 %collective-permute-start.21 = (bf16[128,512]{1,0:T(8,128)(2,1)S(1)}, bf16[128,512]{1,0:T(8,128)(2,1)S(1)}, u32[]{:S(2)}, u32[]{:S(2)}) collective-permute-start(bf16[128,512]{1,0:T(8,128)(2,1)S(1)} %collective-permute-done.15.refs_3_), channel_id=1, source_target_pairs={{0,16},{16,0},{1,17},{17,1},{2,18},{18,2},{3,19},{19,3},{4,20},{20... | collective-permute-start | bytes 393224 | tf_op jit(solution)/shard_map/ppermute | solution.py:51
  50.5 1.1 collective-permute-start.18
  51.8 1.5 %collective-permute-start.20 = (bf16[128,512]{1,0:T(8,128)(2,1)S(1)}, bf16[128,512]{1,0:T(8,128)(2,1)S(1)}, u32[]{:S(2)}, u32[]{:S(2)}) collective-permute-start(bf16[128,512]{1,0:T(8,128)(2,1)S(1)} %collective-permute-done.14.refs_2_), channel_id=1, source_target_pairs={{0,16},{16,0},{1,17},{17,1},{2,18},{18,2},{3,19},{19,3},{4,20},{20... | collective-permute-start | bytes 393224 | tf_op jit(solution)/shard_map/ppermute | solution.py:51
  53.5 1.1 collective-permute-start.17
  54.6 0.9 collective-permute-done.18.refs_6_
  55.5 1.5 %collective-permute-start.25 = (bf16[128,512]{1,0:T(8,128)(2,1)S(1)}, bf16[128,512]{1,0:T(8,128)(2,1)S(1)}, u32[]{:S(2)}, u32[]{:S(2)}) collective-permute-start(bf16[128,512]{1,0:T(8,128)(2,1)S(1)} %collective-permute-done.19.refs_7_), channel_id=1, source_target_pairs={{0,16},{16,0},{1,17},{17,1},{2,18},{18,2},{3,19},{19,3},{4,20},{20... | collective-permute-start | bytes 393224 | tf_op jit(solution)/shard_map/ppermute | solution.py:51
  57.0 1.1 collective-permute-done.20.refs_8_
  58.1 1.5 %collective-permute-start.24 = (bf16[128,512]{1,0:T(8,128)(2,1)S(1)}, bf16[128,512]{1,0:T(8,128)(2,1)S(1)}, u32[]{:S(2)}, u32[]{:S(2)}) collective-permute-start(bf16[128,512]{1,0:T(8,128)(2,1)S(1)} %collective-permute-done.18.refs_6_), channel_id=1, source_target_pairs={{0,16},{16,0},{1,17},{17,1},{2,18},{18,2},{3,19},{19,3},{4,20},{20... | collective-permute-start | bytes 393224 | tf_op jit(solution)/shard_map/ppermute | solution.py:51
  60.3 1.2 %collective-permute-done.25.refs_13_ = bf16[128,512]{1,0:T(8,128)(2,1)S(1)} collective-permute-done((bf16[128,512]{1,0:T(8,128)(2,1)S(1)}, bf16[128,512]{1,0:T(8,128)(2,1)S(1)}, u32[]{:S(2)}, u32[]{:S(2)}) %collective-permute-start.25) | collective-permute-done | bytes 131104 | tf_op jit(solution)/shard_map/ppermute | solution.py:51
  61.6 1.4 %collective-permute-start.8 = (bf16[128,512]{1,0:T(8,128)(2,1)S(1)}, bf16[128,512]{1,0:T(8,128)(2,1)S(1)}, u32[]{:S(2)}, u32[]{:S(2)}) collective-permute-start(bf16[128,512]{1,0:T(8,128)(2,1)S(1)} %collective-permute-done.2.refs_2_), channel_id=1, source_target_pairs={{0,2},{2,0},{1,3},{3,1},{4,6},{6,4},{5,7},{7,5},{8,10},{10,8},{9,1... | collective-permute-start | bytes 393224 | tf_op jit(solution)/shard_map/ppermute | solution.py:47
  63.1 1.3 %collective-permute-start.13 = (bf16[128,512]{1,0:T(8,128)(2,1)}, bf16[128,512]{1,0:T(8,128)(2,1)S(1)}, u32[]{:S(2)}, u32[]{:S(2)}) collective-permute-start(bf16[128,512]{1,0:T(8,128)(2,1)} %collective-permute-done.7.refs_7_), channel_id=1, source_target_pairs={{0,2},{2,0},{1,3},{3,1},{4,6},{6,4},{5,7},{7,5},{8,10},{10,8},{9,1... | collective-permute-start | bytes 393224 | tf_op jit(solution)/shard_map/ppermute | solution.py:47
  64.6 1.2 %collective-permute-start.12 = (bf16[128,512]{1,0:T(8,128)(2,1)}, bf16[128,512]{1,0:T(8,128)(2,1)S(1)}, u32[]{:S(2)}, u32[]{:S(2)}) collective-permute-start(bf16[128,512]{1,0:T(8,128)(2,1)} %collective-permute-done.6.refs_6_), channel_id=1, source_target_pairs={{0,2},{2,0},{1,3},{3,1},{4,6},{6,4},{5,7},{7,5},{8,10},{10,8},{9,1... | collective-permute-start | bytes 393224 | tf_op jit(solution)/shard_map/ppermute | solution.py:47
  65.8 0.9 collective-permute-start.11
  66.7 7.8 %shard_map.134 = (bf16[1024,512]{1,0:T(8,128)(2,1)S(1)}, bf16[1024,512]{1,0:T(8,128)(2,1)S(1)}, f32[256,128]{1,0:T(8,128)S(1)}) custom-call(s32[3]{0:T(128)S(1)} %copy-done.24, bf16[512,1024]{1,0:T(8,128)(2,1)} %get-tuple-element.18.x_own, bf16[512,1024]{1,0:T(8,128)(2,1)} %collective-permute-done.x_other, f32[1,512]{1,0:T(1,128)S(1)} %get-tuple-element.41.ks, ...), custom_call_target="tpu_custom_call" | custom-call | flops 2147483648 | bytes 6950924 | tf_op jit(solution)/shard_map/pallas_call | solution.py:31
  74.6 1.2 %collective-permute-start.26 = (bf16[256,128]{1,0:T(8,128)(2,1)S(1)}, bf16[256,128]{1,0:T(8,128)(2,1)S(1)}, u32[]{:S(2)}, u32[]{:S(2)}) collective-permute-start(bf16[256,128]{1,0:T(8,128)(2,1)S(1)} %convert_element_type.48), channel_id=1, source_target_pairs={{0,2},{2,0},{1,3},{3,1},{4,6},{6,4},{5,7},{7,5},{8,10},{10,8},{9,1... | collective-permute-start | bytes 196616 | tf_op jit(solution)/shard_map/ppermute | solution.py:47
  75.8 6.7 %shard_map.133 = (bf16[1024,512]{1,0:T(8,128)(2,1)S(1)}, bf16[512,1024]{1,0:T(8,128)(2,1)S(1)}, f32[256,128]{1,0:T(8,128)S(1)}) custom-call(s32[3]{0:T(128)S(1)} %copy-done.24, bf16[512,1024]{1,0:T(8,128)(2,1)} %get-tuple-element.18.x_own, bf16[512,1024]{1,0:T(8,128)(2,1)} %collective-permute-done.x_other, bf16[1024,512]{1,0:T(8,128)(2,1)} %get-tuple-element.19.g_own, ...), custom_call_target="tpu_custom_call" | custom-call | flops 2147483648 | bytes 9046028 | tf_op jit(solution)/shard_map/pallas_call | solution.py:31
  82.6 0.9 collective-permute-start.31
  83.5 4.1 %collective-permute-start.29 = (bf16[256,128]{1,0:T(8,128)(2,1)S(1)}, bf16[256,128]{1,0:T(8,128)(2,1)S(1)}, u32[]{:S(2)}, u32[]{:S(2)}) collective-permute-start(bf16[256,128]{1,0:T(8,128)(2,1)S(1)} %fusion.1), channel_id=1, source_target_pairs={{0,8},{4,12},{8,0},{12,4},{1,9},{5,13},{9,1},{13,5},{2,10},{6,14},... | collective-permute-start | bytes 196616 | tf_op jit(solution)/shard_map/ppermute | solution.py:59
  87.6 2.4 %collective-permute-start.28 = (bf16[256,128]{1,0:T(8,128)(2,1)S(1)}, bf16[256,128]{1,0:T(8,128)(2,1)S(1)}, u32[]{:S(2)}, u32[]{:S(2)}) collective-permute-start(bf16[256,128]{1,0:T(8,128)(2,1)S(1)} %fusion.1), channel_id=1, source_target_pairs={{0,12},{4,0},{8,4},{12,8},{1,13},{5,1},{9,5},{13,9},{2,14},{6,2},{... | collective-permute-start | bytes 196616 | tf_op jit(solution)/shard_map/ppermute | solution.py:59
  90.5 1.5 %collective-permute-start.34 = (bf16[256,128]{1,0:T(8,128)(2,1)S(1)}, bf16[256,128]{1,0:T(8,128)(2,1)S(1)}, u32[]{:S(2)}, u32[]{:S(2)}) collective-permute-start(bf16[256,128]{1,0:T(8,128)(2,1)S(1)} %fusion.2), channel_id=1, source_target_pairs={{0,8},{4,12},{8,0},{12,4},{1,9},{5,13},{9,1},{13,5},{2,10},{6,14},... | collective-permute-start | bytes 196616 | tf_op jit(solution)/shard_map/ppermute | solution.py:59
  92.0 2.9 %collective-permute-start.33 = (bf16[256,128]{1,0:T(8,128)(2,1)S(1)}, bf16[256,128]{1,0:T(8,128)(2,1)S(1)}, u32[]{:S(2)}, u32[]{:S(2)}) collective-permute-start(bf16[256,128]{1,0:T(8,128)(2,1)S(1)} %fusion.2), channel_id=1, source_target_pairs={{0,12},{4,0},{8,4},{12,8},{1,13},{5,1},{9,5},{13,9},{2,14},{6,2},{... | collective-permute-start | bytes 196616 | tf_op jit(solution)/shard_map/ppermute | solution.py:59
  95.0 1.2 %collective-permute-done.27 = bf16[256,128]{1,0:T(8,128)(2,1)S(1)} collective-permute-done((bf16[256,128]{1,0:T(8,128)(2,1)S(1)}, bf16[256,128]{1,0:T(8,128)(2,1)S(1)}, u32[]{:S(2)}, u32[]{:S(2)}) %collective-permute-start.27) | collective-permute-done | bytes 65568 | tf_op jit(solution)/shard_map/ppermute | solution.py:59
  96.3 5.9 %shard_map.135 = (f32[512,1024]{1,0:T(8,128)S(1)}, bf16[512,1024]{1,0:T(8,128)(2,1)S(1)}, f32[1024,512]{1,0:T(8,128)S(1)}, f32[1024,512]{1,0:T(8,128)S(1)}) custom-call(s32[3]{0:T(128)S(1)} %copy-done.24, bf16[1024,512]{1,0:T(8,128)(2,1)S(1)} %get-tuple-element.21.query, bf16[512,1024]{1,0:T(8,128)(2,1)S(1)} %get-tuple-element.22.back, ...), custom_call_target="tpu_custom_call" | custom-call | flops 2147483648 | bytes 12191756 | tf_op jit(solution)/shard_map/pallas_call | solution.py:31
  102.5 7.7 %shard_map.136 = (f32[1024,512]{1,0:T(8,128)S(1)}, bf16[1024,512]{1,0:T(8,128)(2,1)}) custom-call(s32[3]{0:T(128)S(1)} %copy-done.24, bf16[1024,512]{1,0:T(8,128)(2,1)S(1)} %get-tuple-element.27.key, bf16[1024,512]{1,0:T(8,128)(2,1)S(1)} %get-tuple-element.28.value, f32[256,128]{1,0:T(8,128)S(1)} %convert_add_fusion.term, ...), custom_call_target="tpu_custom_call" | custom-call | flops 2147483648 | bytes 12193804 | tf_op jit(solution)/shard_map/pallas_call | solution.py:31
  111.1 1.3 %copy.17 = bf16[1024,512]{1,0:T(8,128)(2,1)} copy(bf16[1024,512]{0,1:T(8,128)(2,1)S(1)} %fusion) | data formatting | bytes 2097152
  112.4 0.9 collective-permute-done.35
  113.3 2.5 %add_convert_fusion = bf16[1024,512]{1,0:T(8,128)(2,1)} fusion(f32[1024,512]{1,0:T(8,128)S(1)} %get-tuple-element.32, bf16[1024,512]{1,0:T(8,128)(2,1)} %collective-permute-done.35), kind=kLoop, calls=%fused_computation | loop fusion | flops 1572864 | bytes 4194304 | tf_op jit(solution)/shard_map/convert_element_type | solution.py:337
  (108 shorter events, 7.0 us)
Async XLA Ops:
  5.3 54.8 %copy-start.31 = (f32[1024]{0:T(1024)S(1)}, f32[1024]{0:T(1024)}, u32[]{:S(2)}) copy-start(f32[1024]{0:T(1024)} %param.18) | copy-start | bytes 12292
  5.3 55.0 %copy-start.29 = (f32[1024]{0:T(1024)S(1)}, f32[1024]{0:T(1024)}, u32[]{:S(2)}) copy-start(f32[1024]{0:T(1024)} %param.20) | copy-start | bytes 12292
  5.3 55.0 %copy-start.30 = (f32[1024]{0:T(1024)S(1)}, f32[1024]{0:T(1024)}, u32[]{:S(2)}) copy-start(f32[1024]{0:T(1024)} %param.19) | copy-start | bytes 12292
  5.3 61.3 %copy-start = (bf16[256,1024]{1,0:T(8,128)(2,1)S(1)}, bf16[256,1024]{1,0:T(8,128)(2,1)}, u32[]{:S(2)}) copy-start(bf16[256,1024]{1,0:T(8,128)(2,1)} %refs_0_.7) | copy-start | bytes 1572868
  5.3 61.3 %copy-start.1 = (bf16[256,1024]{1,0:T(8,128)(2,1)S(1)}, bf16[256,1024]{1,0:T(8,128)(2,1)}, u32[]{:S(2)}) copy-start(bf16[256,1024]{1,0:T(8,128)(2,1)} %refs_1_.7) | copy-start | bytes 1572868
  7.6 58.2 %collective-permute-start = (bf16[512,1024]{1,0:T(8,128)(2,1)}, bf16[512,1024]{1,0:T(8,128)(2,1)}, u32[]{:S(2)}, u32[]{:S(2)}) collective-permute-start(bf16[512,1024]{1,0:T(8,128)(2,1)} %get-tuple-element.18.x_own), channel_id=1, source_target_pairs={{0,1},{1,0},{2,3},{3,2},{4,5},{5,4},{6,7},{7,6},{8,9},{9,8},{10,11... | collective-permute-start | bytes 3145736 | tf_op jit(solution)/shard_map/ppermute | solution.py:55
  8.7 57.9 %copy-start.24 = (s32[3]{0:T(128)S(1)}, s32[3]{0:T(128)}, u32[]{:S(2)}) copy-start(s32[3]{0:T(128)} %pad_add_fusion.pos) | copy-start | bytes 40
  11.2 11.1 %collective-permute-start.4 = (bf16[128,512]{1,0:T(8,128)(2,1)}, bf16[128,512]{1,0:T(8,128)(2,1)S(1)}, u32[]{:S(2)}, u32[]{:S(2)}) collective-permute-start(bf16[128,512]{1,0:T(8,128)(2,1)} %get-tuple-element.20), channel_id=1, source_target_pairs={{0,8},{4,12},{8,0},{12,4},{1,9},{5,13},{9,1},{13,5},{2,10},{6,14},... | collective-permute-start | bytes 393224 | tf_op jit(solution)/shard_map/ppermute | solution.py:59
  14.9 14.0 %collective-permute-start.3 = (bf16[128,512]{1,0:T(8,128)(2,1)}, bf16[128,512]{1,0:T(8,128)(2,1)S(1)}, u32[]{:S(2)}, u32[]{:S(2)}) collective-permute-start(bf16[128,512]{1,0:T(8,128)(2,1)} %get-tuple-element.20), channel_id=1, source_target_pairs={{0,12},{4,0},{8,4},{12,8},{1,13},{5,1},{9,5},{13,9},{2,14},{6,2},{... | collective-permute-start | bytes 393224 | tf_op jit(solution)/shard_map/ppermute | solution.py:59
  16.2 12.7 %collective-permute-start.2 = (bf16[128,512]{1,0:T(8,128)(2,1)}, bf16[128,512]{1,0:T(8,128)(2,1)S(1)}, u32[]{:S(2)}, u32[]{:S(2)}) collective-permute-start(bf16[128,512]{1,0:T(8,128)(2,1)} %get-tuple-element.20), channel_id=1, source_target_pairs={{0,4},{4,8},{8,12},{12,0},{1,5},{5,9},{9,13},{13,1},{2,6},{6,10},{... | collective-permute-start | bytes 393224 | tf_op jit(solution)/shard_map/ppermute | solution.py:59
  16.9 17.3 %collective-permute-start.16 = (bf16[128,512]{1,0:T(8,128)(2,1)}, bf16[128,512]{1,0:T(8,128)(2,1)S(1)}, u32[]{:S(2)}, u32[]{:S(2)}) collective-permute-start(bf16[128,512]{1,0:T(8,128)(2,1)} %get-tuple-element.23), channel_id=1, source_target_pairs={{0,8},{4,12},{8,0},{12,4},{1,9},{5,13},{9,1},{13,5},{2,10},{6,14},... | collective-permute-start | bytes 393224 | tf_op jit(solution)/shard_map/ppermute | solution.py:59
  22.3 13.4 %collective-permute-start.15 = (bf16[128,512]{1,0:T(8,128)(2,1)}, bf16[128,512]{1,0:T(8,128)(2,1)S(1)}, u32[]{:S(2)}, u32[]{:S(2)}) collective-permute-start(bf16[128,512]{1,0:T(8,128)(2,1)} %get-tuple-element.23), channel_id=1, source_target_pairs={{0,12},{4,0},{8,4},{12,8},{1,13},{5,1},{9,5},{13,9},{2,14},{6,2},{... | collective-permute-start | bytes 393224 | tf_op jit(solution)/shard_map/ppermute | solution.py:59
  28.9 46.9 %collective-permute-start.1 = (bf16[1024,512]{1,0:T(8,128)(2,1)}, bf16[1024,512]{1,0:T(8,128)(2,1)}, u32[]{:S(2)}, u32[]{:S(2)}) collective-permute-start(bf16[1024,512]{1,0:T(8,128)(2,1)} %get-tuple-element.19.g_own), channel_id=1, source_target_pairs={{0,1},{1,0},{2,3},{3,2},{4,5},{5,4},{6,7},{7,6},{8,9},{9,8},{10,11... | collective-permute-start | bytes 3145736 | tf_op jit(solution)/shard_map/ppermute | solution.py:55
  28.9 8.5 %collective-permute-start.14 = (bf16[128,512]{1,0:T(8,128)(2,1)}, bf16[128,512]{1,0:T(8,128)(2,1)S(1)}, u32[]{:S(2)}, u32[]{:S(2)}) collective-permute-start(bf16[128,512]{1,0:T(8,128)(2,1)} %get-tuple-element.23), channel_id=1, source_target_pairs={{0,4},{4,8},{8,12},{12,0},{1,5},{5,9},{9,13},{13,1},{2,6},{6,10},{... | collective-permute-start | bytes 393224 | tf_op jit(solution)/shard_map/ppermute | solution.py:59
  34.2 5.1 %collective-permute-start.10 = (bf16[128,512]{1,0:T(8,128)(2,1)S(1)}, bf16[128,512]{1,0:T(8,128)(2,1)S(1)}, u32[]{:S(2)}, u32[]{:S(2)}) collective-permute-start(bf16[128,512]{1,0:T(8,128)(2,1)S(1)} %collective-permute-done.4.refs_4_), channel_id=1, source_target_pairs={{0,2},{2,0},{1,3},{3,1},{4,6},{6,4},{5,7},{7,5},{8,10},{10,8},{9,1... | collective-permute-start | bytes 393224 | tf_op jit(solution)/shard_map/ppermute | solution.py:47
  35.7 5.4 %collective-permute-start.7 = (bf16[128,512]{1,0:T(8,128)(2,1)S(1)}, bf16[128,512]{1,0:T(8,128)(2,1)}, u32[]{:S(2)}, u32[]{:S(2)}) collective-permute-start(bf16[128,512]{1,0:T(8,128)(2,1)S(1)} %collective-permute-done.4.refs_4_), channel_id=1, source_target_pairs={{0,16},{16,0},{1,17},{17,1},{2,18},{18,2},{3,19},{19,3},{4,20},{20... | collective-permute-start | bytes 393224 | tf_op jit(solution)/shard_map/ppermute | solution.py:51
  37.3 5.3 %collective-permute-start.9 = (bf16[128,512]{1,0:T(8,128)(2,1)S(1)}, bf16[128,512]{1,0:T(8,128)(2,1)S(1)}, u32[]{:S(2)}, u32[]{:S(2)}) collective-permute-start(bf16[128,512]{1,0:T(8,128)(2,1)S(1)} %collective-permute-done.3.refs_3_), channel_id=1, source_target_pairs={{0,2},{2,0},{1,3},{3,1},{4,6},{6,4},{5,7},{7,5},{8,10},{10,8},{9,1... | collective-permute-start | bytes 393224 | tf_op jit(solution)/shard_map/ppermute | solution.py:47
  39.3 6.4 %collective-permute-start.6 = (bf16[128,512]{1,0:T(8,128)(2,1)S(1)}, bf16[128,512]{1,0:T(8,128)(2,1)}, u32[]{:S(2)}, u32[]{:S(2)}) collective-permute-start(bf16[128,512]{1,0:T(8,128)(2,1)S(1)} %collective-permute-done.3.refs_3_), channel_id=1, source_target_pairs={{0,16},{16,0},{1,17},{17,1},{2,18},{18,2},{3,19},{19,3},{4,20},{20... | collective-permute-start | bytes 393224 | tf_op jit(solution)/shard_map/ppermute | solution.py:51
  41.1 7.4 %collective-permute-start.5 = (bf16[128,512]{1,0:T(8,128)(2,1)S(1)}, bf16[128,512]{1,0:T(8,128)(2,1)}, u32[]{:S(2)}, u32[]{:S(2)}) collective-permute-start(bf16[128,512]{1,0:T(8,128)(2,1)S(1)} %collective-permute-done.2.refs_2_), channel_id=1, source_target_pairs={{0,16},{16,0},{1,17},{17,1},{2,18},{18,2},{3,19},{19,3},{4,20},{20... | collective-permute-start | bytes 393224 | tf_op jit(solution)/shard_map/ppermute | solution.py:51
  43.3 7.2 %collective-permute-start.22 = (bf16[128,512]{1,0:T(8,128)(2,1)S(1)}, bf16[128,512]{1,0:T(8,128)(2,1)S(1)}, u32[]{:S(2)}, u32[]{:S(2)}) collective-permute-start(bf16[128,512]{1,0:T(8,128)(2,1)S(1)} %collective-permute-done.16.refs_4_), channel_id=1, source_target_pairs={{0,16},{16,0},{1,17},{17,1},{2,18},{18,2},{3,19},{19,3},{4,20},{20... | collective-permute-start | bytes 393224 | tf_op jit(solution)/shard_map/ppermute | solution.py:51
  45.7 6.0 %collective-permute-start.19 = (bf16[128,512]{1,0:T(8,128)(2,1)S(1)}, bf16[128,512]{1,0:T(8,128)(2,1)S(1)}, u32[]{:S(2)}, u32[]{:S(2)}) collective-permute-start(bf16[128,512]{1,0:T(8,128)(2,1)S(1)} %collective-permute-done.16.refs_4_), channel_id=1, source_target_pairs={{0,2},{2,0},{1,3},{3,1},{4,6},{6,4},{5,7},{7,5},{8,10},{10,8},{9,1... | collective-permute-start | bytes 393224 | tf_op jit(solution)/shard_map/ppermute | solution.py:47
  48.6 5.0 %collective-permute-start.21 = (bf16[128,512]{1,0:T(8,128)(2,1)S(1)}, bf16[128,512]{1,0:T(8,128)(2,1)S(1)}, u32[]{:S(2)}, u32[]{:S(2)}) collective-permute-start(bf16[128,512]{1,0:T(8,128)(2,1)S(1)} %collective-permute-done.15.refs_3_), channel_id=1, source_target_pairs={{0,16},{16,0},{1,17},{17,1},{2,18},{18,2},{3,19},{19,3},{4,20},{20... | collective-permute-start | bytes 393224 | tf_op jit(solution)/shard_map/ppermute | solution.py:51
  50.5 23.9 %copy-start.6 = (bf16[128,512]{1,0:T(8,128)(2,1)}, bf16[128,512]{1,0:T(8,128)(2,1)S(1)}, u32[]{:S(2)}) copy-start(bf16[128,512]{1,0:T(8,128)(2,1)S(1)} %collective-permute-done.22.refs_10_) | copy-start | bytes 393220
  50.5 5.0 %collective-permute-start.18 = (bf16[128,512]{1,0:T(8,128)(2,1)S(1)}, bf16[128,512]{1,0:T(8,128)(2,1)S(1)}, u32[]{:S(2)}, u32[]{:S(2)}) collective-permute-start(bf16[128,512]{1,0:T(8,128)(2,1)S(1)} %collective-permute-done.15.refs_3_), channel_id=1, source_target_pairs={{0,2},{2,0},{1,3},{3,1},{4,6},{6,4},{5,7},{7,5},{8,10},{10,8},{9,1... | collective-permute-start | bytes 393224 | tf_op jit(solution)/shard_map/ppermute | solution.py:47
  51.8 22.7 %copy-start.8 = (bf16[128,512]{1,0:T(8,128)(2,1)}, bf16[128,512]{1,0:T(8,128)(2,1)S(1)}, u32[]{:S(2)}) copy-start(bf16[128,512]{1,0:T(8,128)(2,1)S(1)} %collective-permute-done.19.refs_7_) | copy-start | bytes 393220
  51.8 6.3 %collective-permute-start.20 = (bf16[128,512]{1,0:T(8,128)(2,1)S(1)}, bf16[128,512]{1,0:T(8,128)(2,1)S(1)}, u32[]{:S(2)}, u32[]{:S(2)}) collective-permute-start(bf16[128,512]{1,0:T(8,128)(2,1)S(1)} %collective-permute-done.14.refs_2_), channel_id=1, source_target_pairs={{0,16},{16,0},{1,17},{17,1},{2,18},{18,2},{3,19},{19,3},{4,20},{20... | collective-permute-start | bytes 393224 | tf_op jit(solution)/shard_map/ppermute | solution.py:51
  53.5 20.9 %copy-start.10 = (bf16[128,512]{1,0:T(8,128)(2,1)}, bf16[128,512]{1,0:T(8,128)(2,1)S(1)}, u32[]{:S(2)}) copy-start(bf16[128,512]{1,0:T(8,128)(2,1)S(1)} %collective-permute-done.21.refs_9_) | copy-start | bytes 393220
  53.5 6.1 %collective-permute-start.17 = (bf16[128,512]{1,0:T(8,128)(2,1)S(1)}, bf16[128,512]{1,0:T(8,128)(2,1)S(1)}, u32[]{:S(2)}, u32[]{:S(2)}) collective-permute-start(bf16[128,512]{1,0:T(8,128)(2,1)S(1)} %collective-permute-done.14.refs_2_), channel_id=1, source_target_pairs={{0,2},{2,0},{1,3},{3,1},{4,6},{6,4},{5,7},{7,5},{8,10},{10,8},{9,1... | collective-permute-start | bytes 393224 | tf_op jit(solution)/shard_map/ppermute | solution.py:47
  55.5 19.0 %copy-start.12 = (bf16[128,512]{1,0:T(8,128)(2,1)}, bf16[128,512]{1,0:T(8,128)(2,1)S(1)}, u32[]{:S(2)}) copy-start(bf16[128,512]{1,0:T(8,128)(2,1)S(1)} %collective-permute-done.18.refs_6_) | copy-start | bytes 393220
  55.5 6.1 %collective-permute-start.25 = (bf16[128,512]{1,0:T(8,128)(2,1)S(1)}, bf16[128,512]{1,0:T(8,128)(2,1)S(1)}, u32[]{:S(2)}, u32[]{:S(2)}) collective-permute-start(bf16[128,512]{1,0:T(8,128)(2,1)S(1)} %collective-permute-done.19.refs_7_), channel_id=1, source_target_pairs={{0,16},{16,0},{1,17},{17,1},{2,18},{18,2},{3,19},{19,3},{4,20},{20... | collective-permute-start | bytes 393224 | tf_op jit(solution)/shard_map/ppermute | solution.py:51
  58.1 16.4 %copy-start.14 = (bf16[128,512]{1,0:T(8,128)(2,1)}, bf16[128,512]{1,0:T(8,128)(2,1)S(1)}, u32[]{:S(2)}) copy-start(bf16[128,512]{1,0:T(8,128)(2,1)S(1)} %collective-permute-done.20.refs_8_) | copy-start | bytes 393220
  58.1 5.0 %collective-permute-start.24 = (bf16[128,512]{1,0:T(8,128)(2,1)S(1)}, bf16[128,512]{1,0:T(8,128)(2,1)S(1)}, u32[]{:S(2)}, u32[]{:S(2)}) collective-permute-start(bf16[128,512]{1,0:T(8,128)(2,1)S(1)} %collective-permute-done.18.refs_6_), channel_id=1, source_target_pairs={{0,16},{16,0},{1,17},{17,1},{2,18},{18,2},{3,19},{19,3},{4,20},{20... | collective-permute-start | bytes 393224 | tf_op jit(solution)/shard_map/ppermute | solution.py:51
  59.6 14.9 %copy-start.16 = (bf16[128,512]{1,0:T(8,128)(2,1)}, bf16[128,512]{1,0:T(8,128)(2,1)S(1)}, u32[]{:S(2)}) copy-start(bf16[128,512]{1,0:T(8,128)(2,1)S(1)} %collective-permute-done.17.refs_5_) | copy-start | bytes 393220
  59.6 5.0 %collective-permute-start.23 = (bf16[128,512]{1,0:T(8,128)(2,1)S(1)}, bf16[128,512]{1,0:T(8,128)(2,1)S(1)}, u32[]{:S(2)}, u32[]{:S(2)}) collective-permute-start(bf16[128,512]{1,0:T(8,128)(2,1)S(1)} %collective-permute-done.17.refs_5_), channel_id=1, source_target_pairs={{0,16},{16,0},{1,17},{17,1},{2,18},{18,2},{3,19},{19,3},{4,20},{20... | collective-permute-start | bytes 393224 | tf_op jit(solution)/shard_map/ppermute | solution.py:51
  61.6 13.0 %collective-permute-start.8 = (bf16[128,512]{1,0:T(8,128)(2,1)S(1)}, bf16[128,512]{1,0:T(8,128)(2,1)S(1)}, u32[]{:S(2)}, u32[]{:S(2)}) collective-permute-start(bf16[128,512]{1,0:T(8,128)(2,1)S(1)} %collective-permute-done.2.refs_2_), channel_id=1, source_target_pairs={{0,2},{2,0},{1,3},{3,1},{4,6},{6,4},{5,7},{7,5},{8,10},{10,8},{9,1... | collective-permute-start | bytes 393224 | tf_op jit(solution)/shard_map/ppermute | solution.py:47
  63.1 12.7 %collective-permute-start.13 = (bf16[128,512]{1,0:T(8,128)(2,1)}, bf16[128,512]{1,0:T(8,128)(2,1)S(1)}, u32[]{:S(2)}, u32[]{:S(2)}) collective-permute-start(bf16[128,512]{1,0:T(8,128)(2,1)} %collective-permute-done.7.refs_7_), channel_id=1, source_target_pairs={{0,2},{2,0},{1,3},{3,1},{4,6},{6,4},{5,7},{7,5},{8,10},{10,8},{9,1... | collective-permute-start | bytes 393224 | tf_op jit(solution)/shard_map/ppermute | solution.py:47
  64.6 11.2 %collective-permute-start.12 = (bf16[128,512]{1,0:T(8,128)(2,1)}, bf16[128,512]{1,0:T(8,128)(2,1)S(1)}, u32[]{:S(2)}, u32[]{:S(2)}) collective-permute-start(bf16[128,512]{1,0:T(8,128)(2,1)} %collective-permute-done.6.refs_6_), channel_id=1, source_target_pairs={{0,2},{2,0},{1,3},{3,1},{4,6},{6,4},{5,7},{7,5},{8,10},{10,8},{9,1... | collective-permute-start | bytes 393224 | tf_op jit(solution)/shard_map/ppermute | solution.py:47
  65.8 10.0 %collective-permute-start.11 = (bf16[128,512]{1,0:T(8,128)(2,1)}, bf16[128,512]{1,0:T(8,128)(2,1)S(1)}, u32[]{:S(2)}, u32[]{:S(2)}) collective-permute-start(bf16[128,512]{1,0:T(8,128)(2,1)} %collective-permute-done.5.refs_5_), channel_id=1, source_target_pairs={{0,2},{2,0},{1,3},{3,1},{4,6},{6,4},{5,7},{7,5},{8,10},{10,8},{9,1... | collective-permute-start | bytes 393224 | tf_op jit(solution)/shard_map/ppermute | solution.py:47
  74.6 8.9 %collective-permute-start.26 = (bf16[256,128]{1,0:T(8,128)(2,1)S(1)}, bf16[256,128]{1,0:T(8,128)(2,1)S(1)}, u32[]{:S(2)}, u32[]{:S(2)}) collective-permute-start(bf16[256,128]{1,0:T(8,128)(2,1)S(1)} %convert_element_type.48), channel_id=1, source_target_pairs={{0,2},{2,0},{1,3},{3,1},{4,6},{6,4},{5,7},{7,5},{8,10},{10,8},{9,1... | collective-permute-start | bytes 196616 | tf_op jit(solution)/shard_map/ppermute | solution.py:47
  82.6 7.9 %collective-permute-start.31 = (bf16[256,128]{1,0:T(8,128)(2,1)S(1)}, bf16[256,128]{1,0:T(8,128)(2,1)S(1)}, u32[]{:S(2)}, u32[]{:S(2)}) collective-permute-start(bf16[256,128]{1,0:T(8,128)(2,1)S(1)} %convert_element_type.56), channel_id=1, source_target_pairs={{0,2},{2,0},{1,3},{3,1},{4,6},{6,4},{5,7},{7,5},{8,10},{10,8},{9,1... | collective-permute-start | bytes 196616 | tf_op jit(solution)/shard_map/ppermute | solution.py:47
  83.5 11.4 %collective-permute-start.29 = (bf16[256,128]{1,0:T(8,128)(2,1)S(1)}, bf16[256,128]{1,0:T(8,128)(2,1)S(1)}, u32[]{:S(2)}, u32[]{:S(2)}) collective-permute-start(bf16[256,128]{1,0:T(8,128)(2,1)S(1)} %fusion.1), channel_id=1, source_target_pairs={{0,8},{4,12},{8,0},{12,4},{1,9},{5,13},{9,1},{13,5},{2,10},{6,14},... | collective-permute-start | bytes 196616 | tf_op jit(solution)/shard_map/ppermute | solution.py:59
  87.6 7.3 %collective-permute-start.28 = (bf16[256,128]{1,0:T(8,128)(2,1)S(1)}, bf16[256,128]{1,0:T(8,128)(2,1)S(1)}, u32[]{:S(2)}, u32[]{:S(2)}) collective-permute-start(bf16[256,128]{1,0:T(8,128)(2,1)S(1)} %fusion.1), channel_id=1, source_target_pairs={{0,12},{4,0},{8,4},{12,8},{1,13},{5,1},{9,5},{13,9},{2,14},{6,2},{... | collective-permute-start | bytes 196616 | tf_op jit(solution)/shard_map/ppermute | solution.py:59
  90.0 6.2 %collective-permute-start.27 = (bf16[256,128]{1,0:T(8,128)(2,1)S(1)}, bf16[256,128]{1,0:T(8,128)(2,1)S(1)}, u32[]{:S(2)}, u32[]{:S(2)}) collective-permute-start(bf16[256,128]{1,0:T(8,128)(2,1)S(1)} %fusion.1), channel_id=1, source_target_pairs={{0,4},{4,8},{8,12},{12,0},{1,5},{5,9},{9,13},{13,1},{2,6},{6,10},{... | collective-permute-start | bytes 196616 | tf_op jit(solution)/shard_map/ppermute | solution.py:59
  90.5 11.8 %collective-permute-start.34 = (bf16[256,128]{1,0:T(8,128)(2,1)S(1)}, bf16[256,128]{1,0:T(8,128)(2,1)S(1)}, u32[]{:S(2)}, u32[]{:S(2)}) collective-permute-start(bf16[256,128]{1,0:T(8,128)(2,1)S(1)} %fusion.2), channel_id=1, source_target_pairs={{0,8},{4,12},{8,0},{12,4},{1,9},{5,13},{9,1},{13,5},{2,10},{6,14},... | collective-permute-start | bytes 196616 | tf_op jit(solution)/shard_map/ppermute | solution.py:59
  92.0 10.3 %collective-permute-start.33 = (bf16[256,128]{1,0:T(8,128)(2,1)S(1)}, bf16[256,128]{1,0:T(8,128)(2,1)S(1)}, u32[]{:S(2)}, u32[]{:S(2)}) collective-permute-start(bf16[256,128]{1,0:T(8,128)(2,1)S(1)} %fusion.2), channel_id=1, source_target_pairs={{0,12},{4,0},{8,4},{12,8},{1,13},{5,1},{9,5},{13,9},{2,14},{6,2},{... | collective-permute-start | bytes 196616 | tf_op jit(solution)/shard_map/ppermute | solution.py:59
  95.0 7.3 %collective-permute-start.32 = (bf16[256,128]{1,0:T(8,128)(2,1)S(1)}, bf16[256,128]{1,0:T(8,128)(2,1)S(1)}, u32[]{:S(2)}, u32[]{:S(2)}) collective-permute-start(bf16[256,128]{1,0:T(8,128)(2,1)S(1)} %fusion.2), channel_id=1, source_target_pairs={{0,4},{4,8},{8,12},{12,0},{1,5},{5,9},{9,13},{13,1},{2,6},{6,10},{... | collective-permute-start | bytes 196616 | tf_op jit(solution)/shard_map/ppermute | solution.py:59
  102.2 8.5 %collective-permute-start.30 = (bf16[512,1024]{1,0:T(8,128)(2,1)S(1)}, bf16[512,1024]{1,0:T(8,128)(2,1)S(1)}, u32[]{:S(2)}, u32[]{:S(2)}) collective-permute-start(bf16[512,1024]{1,0:T(8,128)(2,1)S(1)} %get-tuple-element.26), channel_id=1, source_target_pairs={{0,1},{1,0},{2,3},{3,2},{4,5},{5,4},{6,7},{7,6},{8,9},{9,8},{10,11... | collective-permute-start | bytes 3145736 | tf_op jit(solution)/shard_map/ppermute | solution.py:55
  110.2 3.2 %collective-permute-start.35 = (bf16[1024,512]{1,0:T(8,128)(2,1)}, bf16[1024,512]{1,0:T(8,128)(2,1)}, u32[]{:S(2)}, u32[]{:S(2)}) collective-permute-start(bf16[1024,512]{1,0:T(8,128)(2,1)} %get-tuple-element.33), channel_id=1, source_target_pairs={{0,1},{1,0},{2,3},{3,2},{4,5},{5,4},{6,7},{7,6},{8,9},{9,8},{10,11... | collective-permute-start | bytes 3145736 | tf_op jit(solution)/shard_map/ppermute | solution.py:55
  (20 other events, 129.2 us)
